TPU v7x, 32 devices: a whole 2x2x4 slice. The times are simulated.
32 devices in a mesh: dp: 8 (over z, x), tensor: 4 (over y, core).
Axes of the slice: x: 2, y: 2, z: 4, core: 2. Of those that a mesh axis runs over, the one named last changes fastest.
Arguments:
- tokens: bfloat16 [32768, 768], P(('dp', 'tensor')), may hold values from -6 to 6
- segment_ids: int32 [8, 4096], P('dp'), may hold values from 0 to 15, never falling along the last dimension, each value on 1 to 2048 neighbouring positions
- valid_mask: int32 [32768], P(('dp', 'tensor')), may hold values from 0 to 1, as said below
- teacher: bfloat16 [32768, 768], P(('dp', 'tensor')), may hold values from -6 to 6
- ask_query_weight: bfloat16 [768, 768], P('dp', 'tensor'), may hold values from -0.21875 to 0.21875
- ask_key_weight: bfloat16 [768, 768], P('dp', 'tensor'), may hold values from -0.21875 to 0.21875
- ask_value_weight: bfloat16 [768, 768], P('dp', 'tensor'), may hold values from -0.21875 to 0.21875
- ask_query_bias: float32 [768], P('tensor'), may hold values from -3 to 3
- ask_value_bias: float32 [768], P('tensor'), may hold values from -1 to 1
- ask_out_weight: bfloat16 [768, 768], P('tensor', 'dp'), may hold values from -0.875 to 0.875
- ask_out_bias: float32 [768], replicated, may hold values from -3 to 3
- ask_attn_gain: float32 [768], replicated, may hold values from 0.25 to 1.75
- ask_attn_shift: float32 [768], replicated, may hold values from -1.8 to 1.8
- ask_up_weight: bfloat16 [768, 3072], P('dp', 'tensor'), may hold values from -0.21875 to 0.21875
- ask_up_bias: float32 [3072], P('tensor'), may hold values from -3 to 3
- ask_down_weight: bfloat16 [3072, 768], P('tensor', 'dp'), may hold values from -0.109375 to 0.109375
- ask_down_bias: float32 [768], replicated, may hold values from -1.8 to 1.8
- ask_ffn_gain: float32 [768], replicated, may hold values from 0.25 to 1.75
- ask_ffn_shift: float32 [768], replicated, may hold values from -1.8 to 1.8
- doc_query_weight: bfloat16 [768, 768], P('dp', 'tensor'), may hold values from -0.21875 to 0.21875
- doc_key_weight: bfloat16 [768, 768], P('dp', 'tensor'), may hold values from -0.21875 to 0.21875
- doc_value_weight: bfloat16 [768, 768], P('dp', 'tensor'), may hold values from -0.21875 to 0.21875
- doc_query_bias: float32 [768], P('tensor'), may hold values from -3 to 3
- doc_value_bias: float32 [768], P('tensor'), may hold values from -1 to 1
- doc_out_weight: bfloat16 [768, 768], P('tensor', 'dp'), may hold values from -0.875 to 0.875
- doc_out_bias: float32 [768], replicated, may hold values from -3 to 3
- doc_attn_gain: float32 [768], replicated, may hold values from 0.25 to 1.75
- doc_attn_shift: float32 [768], replicated, may hold values from -1.8 to 1.8
- doc_up_weight: bfloat16 [768, 3072], P('dp', 'tensor'), may hold values from -0.21875 to 0.21875
- doc_up_bias: float32 [3072], P('tensor'), may hold values from -3 to 3
- doc_down_weight: bfloat16 [3072, 768], P('tensor', 'dp'), may hold values from -0.109375 to 0.109375
- doc_down_bias: float32 [768], replicated, may hold values from -1.8 to 1.8
- doc_ffn_gain: float32 [768], replicated, may hold values from 0.25 to 1.75
- doc_ffn_shift: float32 [768], replicated, may hold values from -1.8 to 1.8
Outputs:
- output: bfloat16 [32768, 768], P(('dp', 'tensor'))
- input_grad: float32 [32768, 768], P(('dp', 'tensor'))
- grad_ask_query_weight: float32 [768, 768], P('dp', 'tensor')
- grad_ask_key_weight: float32 [768, 768], P('dp', 'tensor')
- grad_ask_value_weight: float32 [768, 768], P('dp', 'tensor')
- grad_ask_query_bias: float32 [768], P('tensor')
- grad_ask_value_bias: float32 [768], P('tensor')
- grad_ask_out_weight: float32 [768, 768], P('tensor', 'dp')
- grad_ask_out_bias: float32 [768], replicated
- grad_ask_attn_gain: float32 [768], replicated
- grad_ask_attn_shift: float32 [768], replicated
- grad_ask_up_weight: float32 [768, 3072], P('dp', 'tensor')
- grad_ask_up_bias: float32 [3072], P('tensor')
- grad_ask_down_weight: float32 [3072, 768], P('tensor', 'dp')
- grad_ask_down_bias: float32 [768], replicated
- grad_ask_ffn_gain: float32 [768], replicated
- grad_ask_ffn_shift: float32 [768], replicated
- grad_doc_query_weight: float32 [768, 768], P('dp', 'tensor')
- grad_doc_key_weight: float32 [768, 768], P('dp', 'tensor')
- grad_doc_value_weight: float32 [768, 768], P('dp', 'tensor')
- grad_doc_query_bias: float32 [768], P('tensor')
- grad_doc_value_bias: float32 [768], P('tensor')
- grad_doc_out_weight: float32 [768, 768], P('tensor', 'dp')
- grad_doc_out_bias: float32 [768], replicated
- grad_doc_attn_gain: float32 [768], replicated
- grad_doc_attn_shift: float32 [768], replicated
- grad_doc_up_weight: float32 [768, 3072], P('dp', 'tensor')
- grad_doc_up_bias: float32 [3072], P('tensor')
- grad_doc_down_weight: float32 [3072, 768], P('tensor', 'dp')
- grad_doc_down_bias: float32 [768], replicated
- grad_doc_ffn_gain: float32 [768], replicated
- grad_doc_ffn_shift: float32 [768], replicated
Inputs may be any that keep to these rules, and one draw needn't show every extreme that they name: `segment_ids`: segment numbers never fall along a sequence; a document has 1 to 2048 tokens, and some document has exactly 2048. `valid_mask`: the first token is always valid.
All inputs are finite; a program needn't handle non-finite values.
Results may differ from a plain program's by a relative error of at most 0.025.
Values may be sent and summed in bfloat16 or wider, within the bound.
No kernel may reach another device: no remote copies, remote signals or barrier semaphores. Data moves between devices by JAX's collectives and lax.ppermute only.
A program may use at most 320 MiB of HBM per device.

v0:
```python
from functools import partial

import jax
import jax.numpy as jnp
from jax import lax
from jax.sharding import PartitionSpec as P

HEAD_DIM = 64


eps_norm = 1e-12


def layer_norm(values, scale_vec, shift_vec):
    centered = values - jnp.mean(values, axis=-1, keepdims=True)
    variance = jnp.mean(centered * centered, axis=-1, keepdims=True)
    return centered * lax.rsqrt(variance + eps_norm) * scale_vec + shift_vec


def product(first_mat, second_mat):
    return jnp.dot(first_mat, second_mat, preferred_element_type=jnp.float32)


def product_tn(first_mat, second_mat):
    return lax.dot_general(
        first_mat, second_mat, (((0,), (0,)), ((), ())), preferred_element_type=jnp.float32
    )


def product_nt(first_mat, second_mat):
    return lax.dot_general(
        first_mat, second_mat, (((1,), (1,)), ((), ())), preferred_element_type=jnp.float32
    )


def gather_weights(params):
    return (
        lax.all_gather(params[0], "dp", axis=0, tiled=True),
        lax.all_gather(params[1], "dp", axis=0, tiled=True),
        lax.all_gather(params[2], "dp", axis=0, tiled=True),
        lax.all_gather(params[5], "dp", axis=1, tiled=True),
        lax.all_gather(params[9], "dp", axis=0, tiled=True),
        lax.all_gather(params[11], "dp", axis=1, tiled=True),
    )


def regather_weights(params):
    return (
        lax.all_gather(params[0], "dp", axis=0, tiled=True),
        lax.all_gather(params[1], "dp", axis=0, tiled=True),
        lax.all_gather(params[2], "dp", axis=0, tiled=True),
        lax.all_gather(params[5], "dp", axis=1, tiled=True),
        lax.all_gather(params[9], "dp", axis=0, tiled=True),
        lax.all_gather(params[11], "dp", axis=1, tiled=True),
    )


def gather_rows(values):
    return lax.all_gather(values, "tensor", axis=0, tiled=True)


def regather_rows(values):
    return lax.all_gather(values, "tensor", axis=0, tiled=True)


def gather_grads(values):
    return lax.all_gather(values, "tensor", axis=0, tiled=True)


def sum_rows(first_mat, second_mat, rows_dev):

    def partial_term(row_begin, row_count):
        return product(first_mat, second_mat)

    return lax.psum_scatter(
        partial_term(jnp.int32(0), rows_dev * lax.axis_size("tensor")).astype(jnp.bfloat16),
        "tensor",
        scatter_dimension=0,
        tiled=True,
    ).astype(jnp.float32)


def sum_back(first_mat, second_mat, rows_dev):

    def partial_term(row_begin, row_count):
        return product_nt(first_mat, second_mat)

    return lax.psum_scatter(
        partial_term(jnp.int32(0), rows_dev * lax.axis_size("tensor")).astype(jnp.bfloat16),
        "tensor",
        scatter_dimension=0,
        tiled=True,
    ).astype(jnp.float32)


def block_setup(block_index, query_heads, key_heads, value_heads, segments, block_rows, per_seq):
    seq_index = block_index // per_seq
    query_part = lax.dynamic_slice_in_dim(query_heads, block_index * block_rows, block_rows, 0)
    seq_segments = lax.dynamic_index_in_dim(segments, seq_index, 0, keepdims=False)
    row_segments = lax.dynamic_slice_in_dim(
        seq_segments, block_index % per_seq * block_rows, block_rows, 0
    )
    same_doc = row_segments[:, None] == seq_segments[None, :]
    raw_scores = jnp.einsum(
        "qhd,khd->hqk", query_part, key_heads, preferred_element_type=jnp.float32
    )
    scores = jnp.where(same_doc[None], raw_scores * HEAD_DIM ** (-0.5), -1000000000.0)
    return (seq_index, query_part, key_heads, value_heads, scores)


def attention_forward(queries, key_rows, value_rows, segments):
    seq_count, seq_len = segments.shape
    head_count = queries.shape[1] // HEAD_DIM
    block_rows = min(512, seq_len)
    per_seq = seq_len // block_rows
    query_heads = queries.reshape(-1, head_count, HEAD_DIM)
    key_heads = key_rows.reshape(-1, head_count, HEAD_DIM)
    value_heads = value_rows.reshape(-1, head_count, HEAD_DIM)

    def one_block(block_index):
        setup = block_setup(
            block_index, query_heads, key_heads, value_heads, segments, block_rows, per_seq
        )
        scores = setup[4]
        row_peak = jnp.max(scores, axis=-1, keepdims=True)
        exponent = jnp.exp(scores - row_peak)
        row_total = jnp.sum(exponent, axis=-1, keepdims=True)
        attn_probs = (exponent / row_total).astype(jnp.bfloat16)
        context = jnp.einsum(
            "hqk,khd->qhd", attn_probs, setup[3], preferred_element_type=jnp.float32
        )
        return (context.astype(jnp.bfloat16).reshape(block_rows, -1), row_peak, row_total)

    blocks = jnp.arange(seq_count * per_seq, dtype=jnp.int32)
    contexts, peaks, totals = lax.map(one_block, blocks)
    return (contexts.reshape(queries.shape), peaks, totals)


def attention_backward(queries, key_rows, value_rows, segments, peaks, totals, grad_context):
    seq_count, seq_len = segments.shape
    head_count = queries.shape[1] // HEAD_DIM
    block_rows = min(512, seq_len)
    per_seq = seq_len // block_rows
    query_heads = queries.reshape(-1, head_count, HEAD_DIM)
    key_heads = key_rows.reshape(-1, head_count, HEAD_DIM)
    value_heads = value_rows.reshape(-1, head_count, HEAD_DIM)
    grad_heads = grad_context.reshape(-1, head_count, HEAD_DIM)

    def one_block(carry, inputs):
        grad_keys, grad_values = carry
        block_index, row_peak, row_total = inputs
        seq_index, query_part, key_part, value_part, scores = block_setup(
            block_index, query_heads, key_heads, value_heads, segments, block_rows, per_seq
        )
        attn_probs = jnp.exp(scores - row_peak) / row_total
        probs_low = attn_probs.astype(jnp.bfloat16)
        grad_part = lax.dynamic_slice_in_dim(grad_heads, block_index * block_rows, block_rows, 0)
        grad_probs = jnp.einsum(
            "qhd,khd->hqk", grad_part, value_part, preferred_element_type=jnp.float32
        )
        row_dot = jnp.sum(attn_probs * grad_probs, axis=-1, keepdims=True)
        grad_raw = (HEAD_DIM ** (-0.5) * (attn_probs * (grad_probs - row_dot))).astype(jnp.bfloat16)
        grad_query = jnp.einsum(
            "hqk,khd->qhd", grad_raw, key_part, preferred_element_type=jnp.float32
        )
        key_add = jnp.einsum(
            "hqk,qhd->khd", grad_raw, query_part, preferred_element_type=jnp.float32
        )
        value_add = jnp.einsum(
            "hqk,qhd->khd", probs_low, grad_part, preferred_element_type=jnp.float32
        )
        grad_keys = grad_keys + key_add
        grad_values = grad_values + value_add
        return ((grad_keys, grad_values), grad_query)

    empty = jnp.zeros(query_heads.shape, jnp.float32)
    blocks = jnp.arange(seq_count * per_seq, dtype=jnp.int32)
    (grad_keys, grad_values), grad_queries = lax.scan(
        one_block, (empty, empty), (blocks, peaks, totals)
    )
    return (
        grad_queries.reshape(queries.shape).astype(jnp.bfloat16),
        grad_keys.reshape(queries.shape).astype(jnp.bfloat16),
        grad_values.reshape(queries.shape).astype(jnp.bfloat16),
    )


def layer_forward(hidden_in, segments, params):
    rows_dev = hidden_in.shape[0]
    matrices = gather_weights(params)
    sent_rows = hidden_in.astype(jnp.bfloat16)
    gathered = gather_rows(sent_rows)
    queries = (product(gathered, matrices[0]) + params[3]).astype(jnp.bfloat16)
    key_rows = product(gathered, matrices[1]).astype(jnp.bfloat16)
    value_rows = (product(gathered, matrices[2]) + params[4]).astype(jnp.bfloat16)
    context, peaks, totals = attention_forward(queries, key_rows, value_rows, segments)
    attn_sum = sum_rows(context, matrices[3], rows_dev)
    first_sum = hidden_in + attn_sum + params[6]
    normed = layer_norm(first_sum, params[7], params[8])
    normed_sent = normed.astype(jnp.bfloat16)
    ffn_rows = gather_rows(normed_sent)
    inner = product(ffn_rows, matrices[4]) + params[10]
    activated = jax.nn.gelu(inner, approximate=False).astype(jnp.bfloat16)
    ffn_sum = sum_rows(activated, matrices[5], rows_dev)
    second_sum = normed + ffn_sum + params[12]
    result = layer_norm(second_sum, params[13], params[14])
    rows_saved = (sent_rows, normed_sent)
    weights_saved = ()
    saved = (
        queries,
        key_rows,
        value_rows,
        context,
        peaks,
        totals,
        first_sum,
        second_sum,
        inner,
        activated,
        rows_saved,
        weights_saved,
    )
    return (result, saved)


def spread_out(vector, full_width):
    place = lax.axis_index("tensor") * vector.shape[0]
    return lax.dynamic_update_slice(jnp.zeros((full_width,), jnp.float32), vector, (place,))


def take_local(vector, width):
    return lax.dynamic_slice_in_dim(vector, lax.axis_index("tensor") * width, width, 0)


def layer_backward(grad_out, segments, params, saved):
    (
        queries,
        key_rows,
        value_rows,
        context,
        peaks,
        totals,
        first_sum,
        second_sum,
        inner,
        activated,
        rows_saved,
        weights_saved,
    ) = saved
    rows_dev, width = grad_out.shape
    matrices = regather_weights(params)
    gathered = regather_rows(rows_saved[0])
    ffn_rows = regather_rows(rows_saved[1])
    ignored, norm_back = jax.vjp(layer_norm, second_sum, params[13], params[14])
    grad_second, grad_ffn_gain, grad_ffn_shift = norm_back(grad_out)
    grad_down_bias = jnp.sum(grad_second, axis=0)
    grad_ffn_rows = gather_grads(grad_second.astype(jnp.bfloat16))
    grad_act = product_nt(grad_ffn_rows, matrices[5])
    grad_down = product_tn(activated, grad_ffn_rows)
    ignored, gelu_back = jax.vjp(partial(jax.nn.gelu, approximate=False), inner)
    grad_inner = gelu_back(grad_act)[0].astype(jnp.bfloat16)
    grad_up_bias = jnp.sum(grad_inner.astype(jnp.float32), axis=0)
    grad_up = product_tn(ffn_rows, grad_inner)
    grad_normed = grad_second + sum_back(grad_inner, matrices[4], rows_dev)
    ignored, norm_back = jax.vjp(layer_norm, first_sum, params[7], params[8])
    grad_first, grad_attn_gain, grad_attn_shift = norm_back(grad_normed)
    grad_out_bias = jnp.sum(grad_first, axis=0)
    grad_attn_rows = gather_grads(grad_first.astype(jnp.bfloat16))
    grad_outmat = product_tn(context, grad_attn_rows)
    grad_context = product_nt(grad_attn_rows, matrices[3]).astype(jnp.bfloat16)
    grad_q, grad_k, grad_v = attention_backward(
        queries, key_rows, value_rows, segments, peaks, totals, grad_context
    )
    grad_query_bias = jnp.sum(grad_q.astype(jnp.float32), axis=0)
    grad_value_bias = jnp.sum(grad_v.astype(jnp.float32), axis=0)
    grad_querymat = product_tn(gathered, grad_q)
    grad_keymat = product_tn(gathered, grad_k)
    grad_valuemat = product_tn(gathered, grad_v)
    grad_all = jnp.concatenate([grad_q, grad_k, grad_v], axis=1)
    proj_all = jnp.concatenate([matrices[0], matrices[1], matrices[2]], axis=1)
    grad_in = grad_first + sum_back(grad_all, proj_all, rows_dev)
    summed = (
        lax.psum_scatter(grad_querymat, "dp", scatter_dimension=0, tiled=True),
        lax.psum_scatter(grad_keymat, "dp", scatter_dimension=0, tiled=True),
        lax.psum_scatter(grad_valuemat, "dp", scatter_dimension=0, tiled=True),
        lax.psum_scatter(grad_outmat, "dp", scatter_dimension=1, tiled=True),
        lax.psum_scatter(grad_up, "dp", scatter_dimension=0, tiled=True),
        lax.psum_scatter(grad_down, "dp", scatter_dimension=1, tiled=True),
    )
    head_width = grad_query_bias.shape[0]
    unit_width = params[10].shape[0]
    unit_full = unit_width * lax.axis_size("tensor")
    up_bias_term = spread_out(grad_up_bias, unit_full)
    small = lax.psum(
        (
            spread_out(grad_query_bias, width),
            spread_out(grad_value_bias, width),
            up_bias_term,
            grad_out_bias,
            grad_down_bias,
            grad_attn_gain,
            grad_attn_shift,
            grad_ffn_gain,
            grad_ffn_shift,
        ),
        ("dp", "tensor"),
    )
    grads = (
        summed[0],
        summed[1],
        summed[2],
        take_local(small[0], head_width),
        take_local(small[1], head_width),
        summed[3],
        small[3],
        small[5],
        small[6],
        summed[4],
        take_local(small[2], unit_width),
        summed[5],
        small[4],
        small[7],
        small[8],
    )
    return (grad_in, grads)


def on_device(
    tokens,
    segment_ids,
    valid_mask,
    teacher,
    ask_query_weight,
    ask_key_weight,
    ask_value_weight,
    ask_query_bias,
    ask_value_bias,
    ask_out_weight,
    ask_out_bias,
    ask_attn_gain,
    ask_attn_shift,
    ask_up_weight,
    ask_up_bias,
    ask_down_weight,
    ask_down_bias,
    ask_ffn_gain,
    ask_ffn_shift,
    doc_query_weight,
    doc_key_weight,
    doc_value_weight,
    doc_query_bias,
    doc_value_bias,
    doc_out_weight,
    doc_out_bias,
    doc_attn_gain,
    doc_attn_shift,
    doc_up_weight,
    doc_up_bias,
    doc_down_weight,
    doc_down_bias,
    doc_ffn_gain,
    doc_ffn_shift,
):
    ask_params = (
        ask_query_weight,
        ask_key_weight,
        ask_value_weight,
        ask_query_bias,
        ask_value_bias,
        ask_out_weight,
        ask_out_bias,
        ask_attn_gain,
        ask_attn_shift,
        ask_up_weight,
        ask_up_bias,
        ask_down_weight,
        ask_down_bias,
        ask_ffn_gain,
        ask_ffn_shift,
    )
    doc_params = (
        doc_query_weight,
        doc_key_weight,
        doc_value_weight,
        doc_query_bias,
        doc_value_bias,
        doc_out_weight,
        doc_out_bias,
        doc_attn_gain,
        doc_attn_shift,
        doc_up_weight,
        doc_up_bias,
        doc_down_weight,
        doc_down_bias,
        doc_ffn_gain,
        doc_ffn_shift,
    )
    hidden_in = tokens.astype(jnp.float32)
    middle, ask_saved = layer_forward(hidden_in, segment_ids, ask_params)
    final, doc_saved = layer_forward(middle, segment_ids, doc_params)
    mask_rows = valid_mask.astype(jnp.float32)
    valid_total = lax.psum(jnp.sum(mask_rows), ("dp", "tensor"))
    all_rows = tokens.shape[0] * lax.axis_size("dp") * lax.axis_size("tensor")
    grad_final = (
        mask_rows[:, None] * (final - teacher.astype(jnp.float32)) * (all_rows / valid_total)
    )
    grad_middle, doc_grads = layer_backward(grad_final, segment_ids, doc_params, doc_saved)
    grad_input, ask_grads = layer_backward(grad_middle, segment_ids, ask_params, ask_saved)
    return (final.astype(jnp.bfloat16), grad_input) + ask_grads + doc_grads


def solution(mesh):
    return jax.shard_map(
        on_device,
        mesh=mesh,
        in_specs=(
            P(("dp", "tensor"), None),
            P("dp", None),
            P(("dp", "tensor")),
            P(("dp", "tensor"), None),
            P("dp", "tensor"),
            P("dp", "tensor"),
            P("dp", "tensor"),
            P("tensor"),
            P("tensor"),
            P("tensor", "dp"),
            P(),
            P(),
            P(),
            P("dp", "tensor"),
            P("tensor"),
            P("tensor", "dp"),
            P(),
            P(),
            P(),
            P("dp", "tensor"),
            P("dp", "tensor"),
            P("dp", "tensor"),
            P("tensor"),
            P("tensor"),
            P("tensor", "dp"),
            P(),
            P(),
            P(),
            P("dp", "tensor"),
            P("tensor"),
            P("tensor", "dp"),
            P(),
            P(),
            P(),
        ),
        out_specs=(
            P(("dp", "tensor"), None),
            P(("dp", "tensor"), None),
            P("dp", "tensor"),
            P("dp", "tensor"),
            P("dp", "tensor"),
            P("tensor"),
            P("tensor"),
            P("tensor", "dp"),
            P(),
            P(),
            P(),
            P("dp", "tensor"),
            P("tensor"),
            P("tensor", "dp"),
            P(),
            P(),
            P(),
            P("dp", "tensor"),
            P("dp", "tensor"),
            P("dp", "tensor"),
            P("tensor"),
            P("tensor"),
            P("tensor", "dp"),
            P(),
            P(),
            P(),
            P("dp", "tensor"),
            P("tensor"),
            P("tensor", "dp"),
            P(),
            P(),
            P(),
        ),
        check_vma=False,
    )
```

profile of v0, /device:TPU:0, one launch (start us, length us, event | category | flops | bytes accessed | tf_op | source)
XLA Modules:
  0.0 4520.6 jit_solution(4212715173199403432)
XLA Ops:
  9.7 35.1 all_gather.80
  151.0 323.7 %while.66 = (s32[]{:T(128)}, bf16[8,512,192]{1,2,0:T(8,128)(2,1)S(1)}, f32[8,3,512,1]{2,1,3,0:T(4,128)S(1)}, f32[8,3,512,1]{2,1,3,0:T(4,128)S(1)}, s32[8]{0:T(12...) while((s32[]{:T(128)}, ...), condition=%wide.region_3.4_spmd, body=%wide.region_0.3_spmd.sunk | while | flops 1688302592 | bytes 87904624 | solution.py:135
  481.8 58.9 %reduce-scatter.31.cloned.1.call-done = bf16[1024,768]{1,0:T(8,128)(2,1)} async-done(((bf16[4096,768]{1,0:T(8,128)(2,1)}), bf16[1024,768]{1,0:T(8,128)(2,1)}) %reduce-scatter.31.cloned.1.call-update) | async-done | bytes 1572880 | tf_op jit(solution)/shard_map/reduce_scatter | solution.py:75
  547.0 45.7 %all-gather.15.cloned.1.call-done = bf16[4096,768]{1,0:T(8,128)(2,1)} async-done(((bf16[1024,768]{1,0:T(8,128)(2,1)}), bf16[4096,768]{1,0:T(8,128)(2,1)}) %all-gather.15.cloned.1.call-update) | async-done | bytes 6291472 | tf_op jit(solution)/shard_map/all_gather | solution.py:59
  592.7 34.8 multiply_convert_fusion.3
  645.4 57.2 %reduce-scatter.33.cloned.1.call-done = bf16[1024,768]{1,0:T(8,128)(2,1)} async-done(((bf16[4096,768]{1,0:T(8,128)(2,1)}), bf16[1024,768]{1,0:T(8,128)(2,1)}) %reduce-scatter.33.cloned.1.call-update) | async-done | bytes 1572880 | tf_op jit(solution)/shard_map/reduce_scatter | solution.py:75
  709.8 33.1 all_gather.88
  848.7 323.6 %while.67 = (s32[]{:T(128)}, bf16[8,512,192]{1,2,0:T(8,128)(2,1)S(1)}, f32[8,3,512,1]{2,1,3,0:T(4,128)S(1)}, f32[8,3,512,1]{2,1,3,0:T(4,128)S(1)}, s32[8]{0:T(12...) while((s32[]{:T(128)}, ...), condition=%wide.region_13.14_spmd, body=%wide.region_10.13_spmd.sunk | while | flops 1688302592 | bytes 87904624 | solution.py:135
  1179.5 57.6 %reduce-scatter.35.cloned.1.call-done = bf16[1024,768]{1,0:T(8,128)(2,1)} async-done(((bf16[4096,768]{1,0:T(8,128)(2,1)}), bf16[1024,768]{1,0:T(8,128)(2,1)}) %reduce-scatter.35.cloned.1.call-update) | async-done | bytes 1572880 | tf_op jit(solution)/shard_map/reduce_scatter | solution.py:75
  1243.7 37.0 all-gather.25.cloned.1.call-done
  1280.7 46.6 %all-gather.23.cloned.1.call-done = bf16[4096,768]{1,0:T(8,128)(2,1)} async-done(((bf16[1024,768]{1,0:T(8,128)(2,1)}), bf16[4096,768]{1,0:T(8,128)(2,1)}) %all-gather.23.cloned.1.call-update) | async-done | bytes 6291472 | tf_op jit(solution)/shard_map/all_gather | solution.py:59
  1327.4 34.9 multiply_convert_fusion.2
  1381.4 39.1 psum.133
  1451.9 46.5 %all-gather.29.cloned.1.call-done = bf16[4096,768]{1,0:T(8,128)(2,1)} async-done(((bf16[1024,768]{1,0:T(8,128)(2,1)}), bf16[4096,768]{1,0:T(8,128)(2,1)}) %all-gather.29.cloned.1.call-update) | async-done | bytes 6291472 | tf_op jit(solution)/shard_map/all_gather | solution.py:67
  1527.4 58.8 %reduce-scatter.39.cloned.1.call-done = bf16[1024,768]{1,0:T(8,128)(2,1)} async-done(((bf16[4096,768]{1,0:T(8,128)(2,1)}), bf16[1024,768]{1,0:T(8,128)(2,1)}) %reduce-scatter.39.cloned.1.call-update) | async-done | bytes 1572880 | tf_op jit(solution)/shard_map/reduce_scatter | solution.py:88
  1595.6 46.5 %all-gather.31.cloned.1.call-done = bf16[4096,768]{1,0:T(8,128)(2,1)} async-done(((bf16[1024,768]{1,0:T(8,128)(2,1)}), bf16[4096,768]{1,0:T(8,128)(2,1)}) %all-gather.31.cloned.1.call-update) | async-done | bytes 6291472 | tf_op jit(solution)/shard_map/all_gather | solution.py:67
  1649.5 873.0 %while.68 = (s32[]{:T(128)}, f32[4096,3,64]{0,2,1:T(8,128)}, f32[4096,3,64]{0,2,1:T(8,128)S(1)}, bf16[8,512,3,64]{1,3,2,0:T(8,128)(2,1)}, s32[8]{0:T(128)S(1)}, ...) while((s32[]{:T(128)}, f32[4096,3,64]{0,2,1:T(8,128)}, ...), condition=%wide.region_29.30_spmd.clone, body=%wide.region_27.29_spmd.clone.sunk | while | flops 4126157824 | bytes 305850816 | solution.py:178
  1724.1 34.1 fusion.301
  1832.4 35.0 fusion.301
  1941.7 34.9 fusion.301
  2050.8 35.0 fusion.301
  2159.9 35.0 fusion.301
  2269.1 35.0 fusion.301
  2378.3 35.0 fusion.301
  2487.4 35.0 fusion.301
  2536.1 58.9 %reduce-scatter.41.cloned.1.call-done = bf16[1024,768]{1,0:T(8,128)(2,1)} async-done(((bf16[4096,768]{1,0:T(8,128)(2,1)}), bf16[1024,768]{1,0:T(8,128)(2,1)}) %reduce-scatter.41.cloned.1.call-update) | async-done | bytes 1572880 | tf_op jit(solution)/shard_map/reduce_scatter | solution.py:88
  2604.6 46.3 %all-gather.33.cloned.1.call-done = bf16[4096,768]{1,0:T(8,128)(2,1)} async-done(((bf16[1024,768]{1,0:T(8,128)(2,1)}), bf16[4096,768]{1,0:T(8,128)(2,1)}) %all-gather.33.cloned.1.call-update) | async-done | bytes 6291472 | tf_op jit(solution)/shard_map/all_gather | solution.py:67
  2679.2 58.6 %reduce-scatter.43.cloned.1.call-done = bf16[1024,768]{1,0:T(8,128)(2,1)} async-done(((bf16[4096,768]{1,0:T(8,128)(2,1)}), bf16[1024,768]{1,0:T(8,128)(2,1)}) %reduce-scatter.43.cloned.1.call-update) | async-done | bytes 1572880 | tf_op jit(solution)/shard_map/reduce_scatter | solution.py:88
  2802.6 874.2 %while.69 = (s32[]{:T(128)}, f32[4096,3,64]{0,2,1:T(8,128)}, f32[4096,3,64]{0,2,1:T(8,128)S(1)}, bf16[8,512,3,64]{1,3,2,0:T(8,128)(2,1)}, s32[8]{0:T(128)S(1)}, ...) while((s32[]{:T(128)}, f32[4096,3,64]{0,2,1:T(8,128)}, ...), condition=%wide.region_38.39_spmd.clone, body=%wide.region_36.38_spmd.clone.sunk | while | flops 4126157824 | bytes 305850816 | solution.py:178
  2877.3 34.1 fusion.315
  2985.7 35.0 fusion.315
  3095.0 35.1 fusion.315
  3204.3 35.0 fusion.315
  3313.6 35.1 fusion.315
  3423.0 35.0 fusion.315
  3532.3 35.0 fusion.315
  3641.6 35.1 fusion.315
  3784.0 52.1 %all-reduce.3.cloned.1.call-done = (f32[768]{0:T(1024)}, f32[768]{0:T(1024)}, f32[768]{0:T(1024)}, f32[768]{0:T(1024)}, f32[768]{0:T(1024)}, /*index=5*/f32[3072...) async-done(((f32[768]{0:T(1024)}, f32[768]{0:T(1024)}, ...) | async-done | bytes 73744 | tf_op jit(solution)/shard_map/psum | solution.py:294
  3849.3 40.6 reduce-scatter.57.cloned.1.call-done
  3889.9 73.1 %reduce-scatter.59.cloned.1.call-done = f32[768,96]{0,1:T(8,128)} async-done(((f32[768,768]{0,1:T(8,128)}), f32[768,96]{0,1:T(8,128)}) %reduce-scatter.59.cloned.1.call-update) | async-done | bytes 294928 | tf_op jit(solution)/shard_map/reduce_scatter | solution.py:288
  3963.0 66.4 %reduce-scatter.51.cloned.1.call-done = f32[96,192]{1,0:T(8,128)} async-done(((f32[768,192]{1,0:T(8,128)}), f32[96,192]{1,0:T(8,128)}) %reduce-scatter.51.cloned.1.call-update) | async-done | bytes 73744 | tf_op jit(solution)/shard_map/reduce_scatter | solution.py:283
  4029.4 66.2 %reduce-scatter.53.cloned.1.call-done = f32[96,192]{1,0:T(8,128)} async-done(((f32[768,192]{1,0:T(8,128)}), f32[96,192]{1,0:T(8,128)}) %reduce-scatter.53.cloned.1.call-update) | async-done | bytes 73744 | tf_op jit(solution)/shard_map/reduce_scatter | solution.py:284
  4095.6 66.1 %reduce-scatter.55.cloned.1.call-done = f32[96,192]{1,0:T(8,128)} async-done(((f32[768,192]{1,0:T(8,128)}), f32[96,192]{1,0:T(8,128)}) %reduce-scatter.55.cloned.1.call-update) | async-done | bytes 73744 | tf_op jit(solution)/shard_map/reduce_scatter | solution.py:285
  4161.7 72.9 %reduce-scatter.47.cloned.1.call-done = f32[96,768]{1,0:T(8,128)} async-done(((f32[768,768]{1,0:T(8,128)}), f32[96,768]{1,0:T(8,128)}) %reduce-scatter.47.cloned.1.call-update) | async-done | bytes 294928 | tf_op jit(solution)/shard_map/reduce_scatter | solution.py:287
  4234.6 72.9 %reduce-scatter.49.cloned.1.call-done = f32[768,96]{0,1:T(8,128)} async-done(((f32[768,768]{0,1:T(8,128)}), f32[768,96]{0,1:T(8,128)}) %reduce-scatter.49.cloned.1.call-update) | async-done | bytes 294928 | tf_op jit(solution)/shard_map/reduce_scatter | solution.py:288
  4307.5 66.2 %reduce-scatter.61.cloned.1.call-done = f32[96,192]{1,0:T(8,128)} async-done(((f32[768,192]{1,0:T(8,128)}), f32[96,192]{1,0:T(8,128)}) %reduce-scatter.61.cloned.1.call-update) | async-done | bytes 73744
  4373.7 66.1 %reduce-scatter.63.cloned.1.call-done = f32[96,192]{1,0:T(8,128)} async-done(((f32[768,192]{1,0:T(8,128)}), f32[96,192]{1,0:T(8,128)}) %reduce-scatter.63.cloned.1.call-update) | async-done | bytes 73744
  4439.9 66.2 %reduce-scatter.65.cloned.1.call-done = f32[96,192]{1,0:T(8,128)} async-done(((f32[768,192]{1,0:T(8,128)}), f32[96,192]{1,0:T(8,128)}) %reduce-scatter.65.cloned.1.call-update) | async-done | bytes 73744
  (765 shorter events, 2353.8 us)
Async XLA Ops:
  8.0 130.6 %all-gather.13.cloned.1.call-start = ((), (), s32[]{:S(2)}) async-start(), calls=%async_computation.20 | async-start | bytes 7864320 | tf_op jit(solution)/shard_map/all_gather | solution.py:59
  8.8 531.9 %reduce-scatter.31.cloned.1.call-start = ((), (), s32[]{:S(2)}) async-start(), calls=%async_computation.21 | async-start | bytes 7864320 | tf_op jit(solution)/shard_map/reduce_scatter | solution.py:75
  480.7 66.3 %all-gather.17.cloned.1.call-start = ((), (), s32[]{:S(2)}) async-start(), calls=%async_computation.23 | async-start | bytes 1327104 | tf_op jit(solution)/shard_map/all_gather | solution.py:42
  481.3 111.3 %all-gather.15.cloned.1.call-start = ((), (), s32[]{:S(2)}) async-start(), calls=%async_computation.22 | async-start | bytes 7864320 | tf_op jit(solution)/shard_map/all_gather | solution.py:59
  542.8 159.8 %copy-start.63 = (f32[1024]{0:T(1024)}, f32[1024]{0:T(1024)S(1)}, u32[]{:S(2)}) copy-start(f32[1024]{0:T(1024)S(1)} %broadcast_multiply_fusion.3) | copy-start | bytes 12292
  544.3 158.4 %copy-start.68 = (f32[1024]{0:T(1024)}, f32[1024]{0:T(1024)S(1)}, u32[]{:S(2)}) copy-start(f32[1024]{0:T(1024)S(1)} %fusion.147) | copy-start | bytes 12292
  546.4 89.8 %all-gather.19.cloned.1.call-start = ((), (), s32[]{:S(2)}) async-start(), calls=%async_computation.24 | async-start | bytes 1327104 | tf_op jit(solution)/shard_map/all_gather | solution.py:43
  546.9 155.7 %reduce-scatter.33.cloned.1.call-start = ((), (), s32[]{:S(2)}) async-start(), calls=%async_computation.25 | async-start | bytes 7864320 | tf_op jit(solution)/shard_map/reduce_scatter | solution.py:75
  645.4 191.0 %all-gather.21.cloned.1.call-start = ((), (), s32[]{:S(2)}) async-start(), calls=%async_computation.26 | async-start | bytes 7864320 | tf_op jit(solution)/shard_map/all_gather | solution.py:59
  707.9 97.4 %copy-start.83 = (bf16[96,192]{1,0:T(8,128)(2,1)S(1)}, bf16[96,192]{1,0:T(8,128)(2,1)}, u32[]{:S(2)}) copy-start(bf16[96,192]{1,0:T(8,128)(2,1)} %param.63) | copy-start | bytes 110596
  709.6 527.5 %reduce-scatter.35.cloned.1.call-start = ((), (), s32[]{:S(2)}) async-start(), calls=%async_computation.27 | async-start | bytes 7864320 | tf_op jit(solution)/shard_map/reduce_scatter | solution.py:75
  1178.3 102.4 %all-gather.25.cloned.1.call-start = ((), (), s32[]{:S(2)}) async-start(), calls=%async_computation.29 | async-start | bytes 1327104 | tf_op jit(solution)/shard_map/all_gather | solution.py:42
  1179.1 148.3 %all-gather.23.cloned.1.call-start = ((), (), s32[]{:S(2)}) async-start(), calls=%async_computation.28 | async-start | bytes 7864320 | tf_op jit(solution)/shard_map/all_gather | solution.py:59
  1243.1 127.8 %all-gather.27.cloned.1.call-start = ((), (), s32[]{:S(2)}) async-start(), calls=%async_computation.30 | async-start | bytes 1327104 | tf_op jit(solution)/shard_map/all_gather | solution.py:43
  1243.7 194.5 %reduce-scatter.37.cloned.1.call-start = ((), (), s32[]{:S(2)}) async-start(), calls=%async_computation.31 | async-start | bytes 7864320 | tf_op jit(solution)/shard_map/reduce_scatter | solution.py:75
  1380.1 118.3 %all-gather.29.cloned.1.call-start = ((), (), s32[]{:S(2)}) async-start(), calls=%async_computation.32 | async-start | bytes 7864320 | tf_op jit(solution)/shard_map/all_gather | solution.py:67
  1451.9 134.3 %reduce-scatter.39.cloned.1.call-start = ((), (), s32[]{:S(2)}) async-start(), calls=%async_computation.33 | async-start | bytes 7864320 | tf_op jit(solution)/shard_map/reduce_scatter | solution.py:88
  1527.3 114.7 %all-gather.31.cloned.1.call-start = ((), (), s32[]{:S(2)}) async-start(), calls=%async_computation.34 | async-start | bytes 7864320 | tf_op jit(solution)/shard_map/all_gather | solution.py:67
  1595.5 999.5 %reduce-scatter.41.cloned.1.call-start = ((), (), s32[]{:S(2)}) async-start(), calls=%async_computation.35 | async-start | bytes 7864320 | tf_op jit(solution)/shard_map/reduce_scatter | solution.py:88
  2536.0 114.9 %all-gather.33.cloned.1.call-start = ((), (), s32[]{:S(2)}) async-start(), calls=%async_computation.36 | async-start | bytes 7864320 | tf_op jit(solution)/shard_map/all_gather | solution.py:67
  2604.5 133.2 %reduce-scatter.43.cloned.1.call-start = ((), (), s32[]{:S(2)}) async-start(), calls=%async_computation.37 | async-start | bytes 7864320 | tf_op jit(solution)/shard_map/reduce_scatter | solution.py:88
  2678.9 116.1 %all-gather.35.cloned.1.call-start = ((), (), s32[]{:S(2)}) async-start(), calls=%async_computation.38 | async-start | bytes 7864320 | tf_op jit(solution)/shard_map/all_gather | solution.py:67
  2748.5 1033.9 %reduce-scatter.69.cloned.1.call-start = ((), (), s32[]{:S(2)}) async-start(), calls=%async_computation.51 | async-start | bytes 884736
  2758.9 1077.2 %all-reduce.3.cloned.1.call-start = ((), (), s32[]{:S(2)}) async-start(), calls=%async_computation.52 | async-start | bytes 180224 | tf_op jit(solution)/shard_map/psum | solution.py:294
  3681.1 163.0 %reduce-scatter.67.cloned.1.call-start = ((), (), s32[]{:S(2)}) async-start(), calls=%async_computation.50 | async-start | bytes 884736
  3691.9 154.0 %reduce-scatter.45.cloned.1.call-start = ((), (), s32[]{:S(2)}) async-start(), calls=%async_computation.39 | async-start | bytes 7864320 | tf_op jit(solution)/shard_map/reduce_scatter | solution.py:88
  3701.2 188.7 %reduce-scatter.57.cloned.1.call-start = ((), (), s32[]{:S(2)}) async-start(), calls=%async_computation.45 | async-start | bytes 2654208 | tf_op jit(solution)/shard_map/reduce_scatter | solution.py:287
  3711.4 251.6 %reduce-scatter.59.cloned.1.call-start = ((), (), s32[]{:S(2)}) async-start(), calls=%async_computation.46 | async-start | bytes 2654208 | tf_op jit(solution)/shard_map/reduce_scatter | solution.py:288
  3721.9 307.5 %reduce-scatter.51.cloned.1.call-start = ((), (), s32[]{:S(2)}) async-start(), calls=%async_computation.42 | async-start | bytes 884736 | tf_op jit(solution)/shard_map/reduce_scatter | solution.py:283
  3727.6 368.1 %reduce-scatter.53.cloned.1.call-start = ((), (), s32[]{:S(2)}) async-start(), calls=%async_computation.43 | async-start | bytes 884736 | tf_op jit(solution)/shard_map/reduce_scatter | solution.py:284
  3733.8 427.9 %reduce-scatter.55.cloned.1.call-start = ((), (), s32[]{:S(2)}) async-start(), calls=%async_computation.44 | async-start | bytes 884736 | tf_op jit(solution)/shard_map/reduce_scatter | solution.py:285
  3739.4 495.2 %reduce-scatter.47.cloned.1.call-start = ((), (), s32[]{:S(2)}) async-start(), calls=%async_computation.40 | async-start | bytes 2654208 | tf_op jit(solution)/shard_map/reduce_scatter | solution.py:287
  3749.7 557.8 %reduce-scatter.49.cloned.1.call-start = ((), (), s32[]{:S(2)}) async-start(), calls=%async_computation.41 | async-start | bytes 2654208 | tf_op jit(solution)/shard_map/reduce_scatter | solution.py:288
  3760.2 613.6 %reduce-scatter.61.cloned.1.call-start = ((), (), s32[]{:S(2)}) async-start(), calls=%async_computation.47 | async-start | bytes 884736
  3768.7 671.2 %reduce-scatter.63.cloned.1.call-start = ((), (), s32[]{:S(2)}) async-start(), calls=%async_computation.48 | async-start | bytes 884736
  3774.4 731.7 %reduce-scatter.65.cloned.1.call-start = ((), (), s32[]{:S(2)}) async-start(), calls=%async_computation.49 | async-start | bytes 884736
  3845.7 660.3 %copy-start.118 = (f32[768]{0:T(1024)S(1)}, f32[768]{0:T(1024)}, u32[]{:S(2)}) copy-start(f32[768]{0:T(1024)} %get-tuple-element.1400) | copy-start | bytes 9220
  3845.7 660.9 %copy-start.117 = (f32[768]{0:T(1024)S(1)}, f32[768]{0:T(1024)}, u32[]{:S(2)}) copy-start(f32[768]{0:T(1024)} %get-tuple-element.1401) | copy-start | bytes 9220
  3845.7 661.5 %copy-start.116 = (f32[768]{0:T(1024)S(1)}, f32[768]{0:T(1024)}, u32[]{:S(2)}) copy-start(f32[768]{0:T(1024)} %get-tuple-element.1402) | copy-start | bytes 9220
  3845.7 662.1 %copy-start.115 = (f32[768]{0:T(1024)S(1)}, f32[768]{0:T(1024)}, u32[]{:S(2)}) copy-start(f32[768]{0:T(1024)} %get-tuple-element.1406) | copy-start | bytes 9220
  3845.7 662.7 %copy-start.114 = (f32[768]{0:T(1024)S(1)}, f32[768]{0:T(1024)}, u32[]{:S(2)}) copy-start(f32[768]{0:T(1024)} %get-tuple-element.1407) | copy-start | bytes 9220
  3845.8 663.3 %copy-start.113 = (f32[768]{0:T(1024)S(1)}, f32[768]{0:T(1024)}, u32[]{:S(2)}) copy-start(f32[768]{0:T(1024)} %get-tuple-element.1408) | copy-start | bytes 9220
  3845.8 663.9 %copy-start.112 = (f32[768]{0:T(1024)S(1)}, f32[768]{0:T(1024)}, u32[]{:S(2)}) copy-start(f32[768]{0:T(1024)} %get-tuple-element.1415) | copy-start | bytes 9220
  3845.8 664.5 %copy-start.111 = (f32[768]{0:T(1024)S(1)}, f32[768]{0:T(1024)}, u32[]{:S(2)}) copy-start(f32[768]{0:T(1024)} %get-tuple-element.1416) | copy-start | bytes 9220
  3845.8 665.1 %copy-start.110 = (f32[768]{0:T(1024)S(1)}, f32[768]{0:T(1024)}, u32[]{:S(2)}) copy-start(f32[768]{0:T(1024)} %get-tuple-element.1417) | copy-start | bytes 9220
  3845.8 665.7 %copy-start.109 = (f32[768]{0:T(1024)S(1)}, f32[768]{0:T(1024)}, u32[]{:S(2)}) copy-start(f32[768]{0:T(1024)} %get-tuple-element.1421) | copy-start | bytes 9220
  3845.8 666.2 %copy-start.108 = (f32[768]{0:T(1024)S(1)}, f32[768]{0:T(1024)}, u32[]{:S(2)}) copy-start(f32[768]{0:T(1024)} %get-tuple-element.1422) | copy-start | bytes 9220
  3845.8 666.8 %copy-start.107 = (f32[768]{0:T(1024)S(1)}, f32[768]{0:T(1024)}, u32[]{:S(2)}) copy-start(f32[768]{0:T(1024)} %get-tuple-element.1423) | copy-start | bytes 9220
  (128 other events, 2863.7 us)
Sparse Core Ops, SparseCore 0:
  10.4 49.0 all-gather.12
  480.8 59.7 reduce-scatter.30
  709.7 46.3 all-gather.20
  1380.2 57.9 reduce-scatter.36
  1452.0 46.3 all-gather.28
  1595.6 46.3 all-gather.30
  2536.1 58.8 reduce-scatter.40
  2748.6 46.3 all-gather.34
  3681.2 154.8 all-reduce.2
Sparse Core Ops, SparseCore 1:
  483.4 42.2 all-gather.16
  546.4 46.2 all-gather.14
  594.7 41.3 all-gather.18
  645.5 57.1 reduce-scatter.32
  1178.4 58.7 reduce-scatter.34
  1239.3 41.4 all-gather.24
  1282.8 44.6 all-gather.22
  1329.4 41.4 all-gather.26
  1527.4 58.7 reduce-scatter.38
  2604.6 46.2 all-gather.32
  2679.0 58.7 reduce-scatter.42
  2759.0 63.2 reduce-scatter.68
  3692.0 63.3 reduce-scatter.66
  3757.9 57.7 reduce-scatter.44
  3819.8 70.1 reduce-scatter.56
  3894.0 68.9 reduce-scatter.58
  3966.9 62.5 reduce-scatter.50
  4033.3 62.3 reduce-scatter.52
  4099.4 62.3 reduce-scatter.54
  4165.8 68.8 reduce-scatter.46
  4238.5 68.9 reduce-scatter.48
  4311.3 62.4 reduce-scatter.60
  4377.5 62.3 reduce-scatter.62
  4443.8 62.3 reduce-scatter.64
where the time goes:
time: 4530 us; the launch traced here: 4520 us
  matrix products  2340 us (52%)
  waiting for transfers between devices  1400 us (31%)
  blocking collectives  295 us (7%)
  other arithmetic  294 us (6%)
  local copies, waits for them, and re-layouts  89.3 us (2%)
  loops' own time  86.2 us (2%)
    dot_general x16, matrix products, one_block(): jnp.einsum('hqk,qhd->khd', grad_raw, query_part, preferred_element_type=j...  558 us
    dot_general x16, matrix products, one_block(): jnp.einsum('hqk,khd->qhd', grad_raw, key_part, preferred_element_type=jnp...  527 us
    dot_general x32, matrix products, block_setup(): jnp.einsum('qhd,khd->hqk', query_part, key_heads, preferred_element_type=...  416 us
    unnamed x38, waiting for transfers between devices  202 us
    dot_general x16, matrix products, one_block(): jnp.einsum('hqk,khd->qhd', attn_probs, setup[3], preferred_element_type=j...  192 us
    reduce_scatter x4, waiting for transfers between devices, sum_rows(): lax.psum_scatter(partial_term(jnp.int32(0), rows_dev * lax.axis_size('ten...  191 us
    reduce_sum x16, other arithmetic, one_block(): row_total = jnp.sum(exponent, axis=-1, keepdims=True)  189 us
    dot_general x16, matrix products, one_block(): jnp.einsum('hqk,qhd->khd', probs_low, grad_part, preferred_element_type=j...  177 us
  transfers between devices with their start and end apart: 33, of which 27 were waited for; matrix products, arithmetic and copies ran while one was open for 24% of the time, Pallas kernels for 0%

commit v1 on v0

v1 whole, which is shorter than its diff:
```python
import jax
import jax.numpy as jnp
from jax import lax
from jax.experimental import pallas as pl
from jax.experimental.pallas import tpu as pltpu
from jax.sharding import PartitionSpec as P

HEAD_DIM = 64
LANES = 128
TILE = 256
BLOCKED = 1e9
SEGMENTS = 16
eps_norm = 1e-12

bf16 = jnp.bfloat16
f32 = jnp.float32
NT = (((1,), (1,)), ((), ()))
TN = (((0,), (0,)), ((), ()))
WHOLE = pl.BlockSpec(memory_space=pltpu.VMEM)


def dot_nn(first_mat, second_mat):
    return jnp.dot(first_mat, second_mat, preferred_element_type=f32)


def dot_nt(first_mat, second_mat):
    return lax.dot_general(first_mat, second_mat, NT, preferred_element_type=f32)


def dot_tn(first_mat, second_mat):
    return lax.dot_general(first_mat, second_mat, TN, preferred_element_type=f32)


def kernel_params():
    return pltpu.CompilerParams(vmem_limit_bytes=60 * 1024 * 1024)


def flip(values, bit):
    size = lax.axis_size("tensor")
    return lax.ppermute(values, "tensor", [(i, i ^ bit) for i in range(size)])


def gather_chunks(own):
    half = own.shape[0] // 2
    near = flip(own, 1)
    far = [flip(own[:half], 2), flip(own[half:], 2)]
    last = [flip(part, 1) for part in far]
    return own, near, jnp.concatenate(far, axis=0), jnp.concatenate(last, axis=0)


def exchange_pieces(pieces):
    return [pieces[0]] + [flip(pieces[r], r) for r in range(1, 4)]


def scatter_chunks(chunks):
    crossing = chunks[2].astype(f32) + flip(chunks[3], 1).astype(f32)
    near = flip(chunks[1], 1).astype(f32)
    far = flip(crossing.astype(bf16), 2).astype(f32)
    return chunks[0].astype(f32) + near + far


def butterfly(values, axes):
    for axis in axes:
        size = lax.axis_size(axis)
        step = 1
        while step < size:
            other = lax.ppermute(values, axis, [(i, i ^ step) for i in range(size)])
            values = values + other
            step *= 2
    return values


def project(pieces, matrix, query_bias, value_bias, query_marks, key_marks):
    rows, width = pieces[0].shape
    heads = matrix.shape[1] // 3 // HEAD_DIM
    group = heads * HEAD_DIM
    wide = heads * LANES
    sub = rows // 2

    def body(p0, p1, p2, p3, mat, bias_q, bias_v, mark_q, mark_k, out_q, out_k, out_v):
        chunk = pl.program_id(0)
        lane = lax.broadcasted_iota(jnp.int32, (sub, HEAD_DIM), 1)
        ones = jnp.where(lane < 2, 1.0, 0.0).astype(bf16)

        def run(piece):
            for part in range(2):
                at = slice(part * sub, (part + 1) * sub)
                full = dot_nn(piece[at, :], mat[...])
                for h in range(heads):
                    lo = h * HEAD_DIM
                    to = slice(h * LANES, (h + 1) * LANES)
                    q = full[:, lo : lo + HEAD_DIM] + bias_q[:, lo : lo + HEAD_DIM]
                    q = (q.astype(bf16).astype(f32) * HEAD_DIM ** (-0.5)).astype(bf16)
                    k = full[:, group + lo : group + lo + HEAD_DIM].astype(bf16)
                    v = full[:, 2 * group + lo : 2 * group + lo + HEAD_DIM]
                    v = (v + bias_v[:, lo : lo + HEAD_DIM]).astype(bf16)
                    out_q[at, to] = jnp.concatenate([q, mark_q[at, :]], axis=1)
                    out_k[at, to] = jnp.concatenate([k, mark_k[at, :]], axis=1)
                    out_v[at, to] = jnp.concatenate([v, ones], axis=1)

        for r, piece in enumerate((p0, p1, p2, p3)):

            @pl.when(chunk == r)
            def _(piece=piece):
                run(piece)

    out = jax.ShapeDtypeStruct((4 * rows, wide), bf16)
    spec = pl.BlockSpec((rows, wide), lambda i: (i, 0))
    mark_spec = pl.BlockSpec((rows, HEAD_DIM), lambda i: (i, 0))
    return pl.pallas_call(
        body,
        grid=(4,),
        in_specs=[WHOLE] * 7 + [mark_spec] * 2,
        out_specs=[spec] * 3,
        out_shape=[out] * 3,
        compiler_params=kernel_params(),
        name="project",
    )(*pieces, matrix, query_bias[None], value_bias[None], query_marks, key_marks)


def attention_forward(low, high, place, queries, keys, values):
    rows, wide = queries.shape
    heads = wide // LANES
    count = rows // TILE
    per_chunk = count // 4
    half = rows // 8
    half_blocks = half // TILE
    group = heads * HEAD_DIM

    def body(
        low_ref, high_ref, place_ref, q_ref, k_ref, v_ref, ctx_ref, ql_ref, score, peak, total
    ):
        block = pl.program_id(0)
        own = place_ref[0]
        first = low_ref[block]
        last = high_ref[block]
        peak[...] = jnp.full_like(peak, -3e38)
        total[...] = jnp.zeros_like(total)
        q_heads = [q_ref[:, h * LANES : (h + 1) * LANES] for h in range(heads)]

        def where_is(j):
            spot = ((j // per_chunk) ^ own) * per_chunk + j % per_chunk
            return pl.multiple_of(spot * TILE, TILE)

        def score_step(j, carry):
            at = where_is(j)
            for h in range(heads):
                s = dot_nt(q_heads[h], k_ref[pl.ds(at, TILE), h * LANES : (h + 1) * LANES])
                score[h, j - first] = s
                top = s[:, 0:LANES]
                for c in range(1, TILE // LANES):
                    top = jnp.maximum(top, s[:, c * LANES : (c + 1) * LANES])
                peak[h] = jnp.maximum(peak[h], top)
            return carry

        lax.fori_loop(first, last, score_step, 0)
        tops = []
        for h in range(heads):
            top = jnp.max(peak[h], axis=1, keepdims=True)
            tops.append(top)
            peak[h] = jnp.broadcast_to(top, (TILE, LANES))

        def sum_step(j, carry):
            at = where_is(j)
            for h in range(heads):
                top = peak[h]
                parts = [
                    jnp.exp(score[h, j - first, :, c * LANES : (c + 1) * LANES] - top)
                    for c in range(TILE // LANES)
                ]
                p = jnp.concatenate(parts, axis=1).astype(bf16)
                total[h] += dot_nn(p, v_ref[pl.ds(at, TILE), h * LANES : (h + 1) * LANES])
            return carry

        lax.fori_loop(first, last, sum_step, 0)
        lane = lax.broadcasted_iota(jnp.int32, (TILE, LANES), 1)
        outs = []
        for h in range(heads):
            acc = total[h]
            norm = acc[:, HEAD_DIM : HEAD_DIM + 1]
            outs.append((acc[:, 0:HEAD_DIM] * (1.0 / norm)).astype(bf16))
            shift = -(tops[h] + jnp.log(norm))
            one = shift.astype(bf16).astype(f32)
            two = (shift - one).astype(bf16).astype(f32)
            three = shift - one - two
            q = q_heads[h].astype(f32)
            q = jnp.where(lane == HEAD_DIM + SEGMENTS, one, q)
            q = jnp.where(lane == HEAD_DIM + SEGMENTS + 1, two, q)
            q = jnp.where(lane == HEAD_DIM + SEGMENTS + 2, three, q)
            ql_ref[:, h * LANES : (h + 1) * LANES] = q.astype(bf16)
        ctx = jnp.concatenate(outs, axis=1)
        inside = block % per_chunk
        at = pl.multiple_of((inside % half_blocks) * TILE, TILE)

        @pl.when(inside < half_blocks)
        def _():
            ctx_ref[0, pl.ds(at, TILE), 0:group] = ctx

        @pl.when(inside >= half_blocks)
        def _():
            ctx_ref[0, pl.ds(at, TILE), group : 2 * group] = ctx

    row_spec = pl.BlockSpec((TILE, wide), lambda i, *_: (i, 0))
    return pl.pallas_call(
        body,
        grid_spec=pltpu.PrefetchScalarGridSpec(
            num_scalar_prefetch=3,
            grid=(count,),
            in_specs=[row_spec, WHOLE, WHOLE],
            out_specs=[
                pl.BlockSpec((1, half, 2 * group), lambda i, *_: (i // per_chunk, 0, 0)),
                row_spec,
            ],
            scratch_shapes=[
                pltpu.VMEM((heads, count, TILE, TILE), f32),
                pltpu.VMEM((heads, TILE, LANES), f32),
                pltpu.VMEM((heads, TILE, LANES), f32),
            ],
        ),
        out_shape=[
            jax.ShapeDtypeStruct((4, half, 2 * group), bf16),
            jax.ShapeDtypeStruct((rows, wide), bf16),
        ],
        compiler_params=kernel_params(),
        name="attention_forward",
    )(low, high, place, queries, keys, values)


def attention_backward(low, high, place, queries, keys, values, contexts, grads):
    rows, wide = queries.shape
    heads = wide // LANES
    count = rows // TILE
    per_chunk = count // 4
    half = rows // 8
    half_blocks = half // TILE
    group = heads * HEAD_DIM

    def body(low_ref, high_ref, place_ref, q_ref, k_ref, v_ref, c_ref, g0, g1, g2, g3, *rest):
        dq_ref, dk_ref, dv_ref, do_all, dq_all, acc_k, acc_v = rest
        block = pl.program_id(0)
        own = place_ref[0]
        first = low_ref[block]
        last = high_ref[block]

        @pl.when(block == 0)
        def _():
            dq_all[...] = jnp.zeros_like(dq_all)
            lane = lax.broadcasted_iota(jnp.int32, (TILE, HEAD_DIM), 1)
            for chunk, g_ref in enumerate((g0, g1, g2, g3)):

                def prepare(b, carry, chunk=chunk, g_ref=g_ref):
                    at = pl.multiple_of(b * TILE, TILE)
                    for side in range(2):
                        cols = slice(side * group, (side + 1) * group)
                        row = pl.multiple_of((2 * chunk + side) * half + at, TILE)
                        c = c_ref[chunk, pl.ds(at, TILE), cols].astype(f32)
                        g = g_ref[pl.ds(at, TILE), cols].astype(f32)
                        for h in range(heads):
                            lo = h * HEAD_DIM
                            gh = g[:, lo : lo + HEAD_DIM]
                            ch = c[:, lo : lo + HEAD_DIM]
                            delta = -jnp.sum(gh * ch, axis=1, keepdims=True)
                            one = delta.astype(bf16).astype(f32)
                            two = delta - one
                            tail = jnp.where(lane == 0, one, jnp.where(lane == 1, two, 0.0))
                            both = jnp.concatenate([gh, tail], axis=1).astype(bf16)
                            do_all[pl.ds(row, TILE), h * LANES : (h + 1) * LANES] = both
                    return carry

                lax.fori_loop(0, half_blocks, prepare, 0)

        acc_k[...] = jnp.zeros_like(acc_k)
        acc_v[...] = jnp.zeros_like(acc_v)

        def step(j, carry):
            spot = ((j // per_chunk) ^ own) * per_chunk + j % per_chunk
            at = pl.multiple_of(spot * TILE, TILE)
            for h in range(heads):
                to = slice(h * LANES, (h + 1) * LANES)
                q = q_ref[pl.ds(at, TILE), to]
                k = k_ref[:, to]
                do = do_all[pl.ds(at, TILE), to]
                p = jnp.exp(dot_nt(k, q))
                ds = (p * dot_nt(v_ref[:, to], do)).astype(bf16)
                acc_v[h] += dot_nn(p.astype(bf16), do)
                acc_k[h] += dot_nn(ds, q)
                dq_all[pl.ds(at, TILE), to] += dot_tn(ds, k)
            return carry

        lax.fori_loop(first, last, step, 0)
        dk = [acc_k[h, :, 0:HEAD_DIM] for h in range(heads)]
        dv = [acc_v[h, :, 0:HEAD_DIM] for h in range(heads)]
        dk_ref[...] = jnp.concatenate(dk, axis=1).astype(bf16)
        dv_ref[...] = jnp.concatenate(dv, axis=1).astype(bf16)

        @pl.when(block == count - 1)
        def _():
            def finish(b, carry):
                at = pl.multiple_of(b * TILE, TILE)
                dq = [
                    dq_all[pl.ds(at, TILE), h * LANES : h * LANES + HEAD_DIM] for h in range(heads)
                ]
                dq = jnp.concatenate(dq, axis=1) * HEAD_DIM ** (-0.5)
                dq_ref[pl.ds(at, TILE), :] = dq.astype(bf16)
                return carry

            lax.fori_loop(0, count, finish, 0)

    row_spec = pl.BlockSpec((TILE, wide), lambda i, *_: (i, 0))
    out_spec = pl.BlockSpec((TILE, group), lambda i, *_: (i, 0))
    out = jax.ShapeDtypeStruct((rows, group), bf16)
    return pl.pallas_call(
        body,
        grid_spec=pltpu.PrefetchScalarGridSpec(
            num_scalar_prefetch=3,
            grid=(count,),
            in_specs=[WHOLE, row_spec, row_spec] + [WHOLE] * 5,
            out_specs=[WHOLE, out_spec, out_spec],
            scratch_shapes=[
                pltpu.VMEM((rows, wide), bf16),
                pltpu.VMEM((rows, wide), f32),
                pltpu.VMEM((heads, TILE, LANES), f32),
                pltpu.VMEM((heads, TILE, LANES), f32),
            ],
        ),
        out_shape=[out] * 3,
        compiler_params=kernel_params(),
        name="attention_backward",
    )(low, high, place, queries, keys, values, contexts, *grads)


SQRT_HALF = 0.7071067811865476
PHI_SCALE = 0.3989422804014327


def norm_parts(values):
    centered = values - jnp.mean(values, axis=-1, keepdims=True)
    variance = jnp.mean(centered * centered, axis=-1, keepdims=True)
    scale = lax.rsqrt(variance + eps_norm)
    return centered * scale, scale


def tokens_forward(place, hidden, pieces, weights, up_bias, vectors):
    rows, width = hidden.shape
    half = rows // 2
    group = pieces[0].shape[1] // 2
    part = TILE
    steps = half // part
    size = 2 * part

    def body(place_ref, x_ref, c0, c1, c2, c3, w_ref, ub_ref, vec_ref, *outs):
        o_ref, ob_ref, nb_ref, act_ref, slope_ref, y1_ref, y2_ref, r1_ref, r2_ref = outs
        own = place_ref[0]
        first = x_ref[...].reshape(size, width).astype(f32) + vec_ref[0:1, :]
        for r, c_ref in enumerate((c0, c1, c2, c3)):
            ctx = jnp.concatenate([c_ref[:, 0:group], c_ref[:, group : 2 * group]], axis=0)
            first = first + dot_nt(ctx, w_ref[own ^ r, :, 2 * width : 2 * width + group])
        y1, r1 = norm_parts(first)
        y1_ref[...] = y1.reshape(2, part, width)
        r1_ref[...] = jnp.broadcast_to(r1, (size, LANES)).reshape(2, part, LANES)
        normed = y1 * vec_ref[1:2, :] + vec_ref[2:3, :]
        sent = normed.astype(bf16)
        nb_ref[...] = sent.reshape(2, part, width)
        second = normed + vec_ref[3:4, :]
        for t in range(4):
            cols = slice(t * width, (t + 1) * width)
            inner = dot_nn(sent, w_ref[t, :, 0:width]) + ub_ref[t : t + 1, :]
            cdf = 0.5 + 0.5 * lax.erf(inner * SQRT_HALF)
            act = (inner * cdf).astype(bf16)
            slope = cdf + inner * (PHI_SCALE * jnp.exp(-0.5 * inner * inner))
            act_ref[:, :, cols] = act.reshape(2, part, width)
            slope_ref[:, :, cols] = slope.astype(bf16).reshape(2, part, width)
            second = second + dot_nt(act, w_ref[t, :, width : 2 * width])
        y2, r2 = norm_parts(second)
        y2_ref[...] = y2.reshape(2, part, width)
        r2_ref[...] = jnp.broadcast_to(r2, (size, LANES)).reshape(2, part, LANES)
        result = y2 * vec_ref[4:5, :] + vec_ref[5:6, :]
        o_ref[...] = result.reshape(2, part, width)
        ob_ref[...] = result.astype(bf16).reshape(2, part, width)

    def spec(cols):
        return pl.BlockSpec((2, part, cols), lambda i, *_: (0, i, 0))

    def out(cols, kind):
        return jax.ShapeDtypeStruct((2, half, cols), kind)

    piece_spec = pl.BlockSpec((part, 2 * group), lambda i, *_: (i, 0))
    units = 4 * width
    results = pl.pallas_call(
        body,
        grid_spec=pltpu.PrefetchScalarGridSpec(
            num_scalar_prefetch=1,
            grid=(steps,),
            in_specs=[spec(width)] + [piece_spec] * 4 + [WHOLE] * 3,
            out_specs=[
                spec(width),
                spec(width),
                spec(width),
                spec(units),
                spec(units),
                spec(width),
                spec(width),
                spec(LANES),
                spec(LANES),
            ],
        ),
        out_shape=[
            out(width, f32),
            out(width, bf16),
            out(width, bf16),
            out(units, bf16),
            out(units, bf16),
            out(width, f32),
            out(width, f32),
            out(LANES, f32),
            out(LANES, f32),
        ],
        compiler_params=kernel_params(),
        name="tokens_forward",
    )(place, hidden.reshape(2, half, width), *pieces, weights, up_bias, vectors)
    return [item.reshape(rows, item.shape[2]) for item in results]


def tokens_backward(place, grad, saved, weights, vectors, group):
    slope, y1, y2, r1, r2 = saved
    rows, width = grad.shape
    half = rows // 2
    part = TILE
    steps = half // part
    size = 2 * part
    units = 4 * width

    def norm_back(g, y, r, gain):
        e = g * gain
        mean_e = jnp.mean(e, axis=-1, keepdims=True)
        mean_ey = jnp.mean(e * y, axis=-1, keepdims=True)
        return r * (e - mean_e - y * mean_ey)

    def body(place_ref, g_ref, sl_ref, y1_ref, y2_ref, r1_ref, r2_ref, w_ref, vec_ref, *outs):
        bg_ref, gi_ref, gf_ref, ag_ref, p0, p1, p2, p3, sum_ref = outs
        own = place_ref[0]

        @pl.when(pl.program_id(0) == 0)
        def _():
            sum_ref[...] = jnp.zeros_like(sum_ref)

        def total(values):
            return jnp.sum(values, axis=0, keepdims=True)

        g = g_ref[...].reshape(size, width)
        y2 = y2_ref[...].reshape(size, width)
        r2 = r2_ref[...].reshape(size, LANES)[:, 0:1]
        second = norm_back(g, y2, r2, vec_ref[4:5, :])
        sum_ref[0:1, :] += total(g * y2)
        sum_ref[1:2, :] += total(g)
        sum_ref[2:3, :] += total(second)
        branch = second.astype(bf16)
        bg_ref[...] = branch.reshape(2, part, width)
        normed = second
        for t in range(4):
            cols = slice(t * width, (t + 1) * width)
            slope_t = sl_ref[:, :, cols].reshape(size, width).astype(f32)
            inner = (dot_nn(branch, w_ref[t, :, width : 2 * width]) * slope_t).astype(bf16)
            gi_ref[:, :, cols] = inner.reshape(2, part, width)
            sum_ref[6 + t : 7 + t, :] += total(inner.astype(f32))
            normed = normed + dot_nt(inner, w_ref[t, :, 0:width])
        y1 = y1_ref[...].reshape(size, width)
        r1 = r1_ref[...].reshape(size, LANES)[:, 0:1]
        first = norm_back(normed, y1, r1, vec_ref[1:2, :])
        sum_ref[3:4, :] += total(normed * y1)
        sum_ref[4:5, :] += total(normed)
        sum_ref[5:6, :] += total(first)
        gf_ref[...] = first.reshape(2, part, width)
        sent = first.astype(bf16)
        ag_ref[...] = sent.reshape(2, part, width)
        for r, p_ref in enumerate((p0, p1, p2, p3)):
            ctx = dot_nn(sent, w_ref[own ^ r, :, 2 * width : 2 * width + group]).astype(bf16)
            p_ref[...] = jnp.concatenate([ctx[0:part], ctx[part:size]], axis=1)

    def spec(cols):
        return pl.BlockSpec((2, part, cols), lambda i, *_: (0, i, 0))

    def out(cols, kind):
        return jax.ShapeDtypeStruct((2, half, cols), kind)

    piece_spec = pl.BlockSpec((part, 2 * group), lambda i, *_: (i, 0))
    piece = jax.ShapeDtypeStruct((half, 2 * group), bf16)
    sums = jax.ShapeDtypeStruct((16, width), f32)

    def view(values):
        return values.reshape(2, half, values.shape[1])

    results = pl.pallas_call(
        body,
        grid_spec=pltpu.PrefetchScalarGridSpec(
            num_scalar_prefetch=1,
            grid=(steps,),
            in_specs=[
                spec(width),
                spec(units),
                spec(width),
                spec(width),
                spec(LANES),
                spec(LANES),
                WHOLE,
                WHOLE,
            ],
            out_specs=[spec(width), spec(units), spec(width), spec(width)]
            + [piece_spec] * 4
            + [pl.BlockSpec((16, width), lambda i, *_: (0, 0))],
        ),
        out_shape=[out(width, bf16), out(units, bf16), out(width, f32), out(width, bf16)]
        + [piece] * 4
        + [sums],
        compiler_params=kernel_params(),
        name="tokens_backward",
    )(place, view(grad), view(slope), view(y1), view(y2), view(r1), view(r2), weights, vectors)
    big = [item.reshape(rows, item.shape[2]) for item in results[:4]]
    return big, list(results[4:8]), results[8]


def weight_grads(place, sent, inner, branch, act, attn, pieces):
    rows, width = sent.shape
    half = rows // 2
    group = pieces[0].shape[1] // 2

    def body(place_ref, s_ref, i_ref, b_ref, a_ref, g_ref, c0, c1, c2, c3, o_ref):
        t = pl.program_id(0)
        own = place_ref[0]
        o_ref[0, :, 0:width] = dot_tn(s_ref[...], i_ref[...]).astype(bf16)
        o_ref[0, :, width : 2 * width] = dot_tn(b_ref[...], a_ref[...]).astype(bf16)
        for r, c_ref in enumerate((c0, c1, c2, c3)):

            @pl.when(t == own ^ r)
            def _(c_ref=c_ref):
                ctx = jnp.concatenate([c_ref[:, 0:group], c_ref[:, group : 2 * group]], axis=0)
                o_ref[0, :, 2 * width : 2 * width + group] = dot_tn(g_ref[...], ctx).astype(bf16)

    unit_spec = pl.BlockSpec((rows, width), lambda i, *_: (0, i))
    cols = 2 * width + group
    return pl.pallas_call(
        body,
        grid_spec=pltpu.PrefetchScalarGridSpec(
            num_scalar_prefetch=1,
            grid=(4,),
            in_specs=[WHOLE, unit_spec, WHOLE, unit_spec, WHOLE] + [WHOLE] * 4,
            out_specs=pl.BlockSpec((1, width, cols), lambda i, *_: (i, 0, 0)),
        ),
        out_shape=jax.ShapeDtypeStruct((4, width, cols), bf16),
        compiler_params=kernel_params(),
        name="weight_grads",
    )(place, sent, inner, branch, act, attn, *pieces)


def input_grads(grad_q, grad_k, grad_v, matrix):
    rows, group = grad_q.shape
    width = matrix.shape[0]
    chunk = rows // 4

    def body(q_ref, k_ref, v_ref, mat, o0, o1, o2, o3):
        full = dot_nt(q_ref[...], mat[:, 0:group])
        full = full + dot_nt(k_ref[...], mat[:, group : 2 * group])
        full = (full + dot_nt(v_ref[...], mat[:, 2 * group : 3 * group])).astype(bf16)
        for r, o_ref in enumerate((o0, o1, o2, o3)):

            @pl.when(pl.program_id(0) == r)
            def _(o_ref=o_ref):
                o_ref[...] = full

    spec = pl.BlockSpec((chunk, group), lambda i: (i, 0))
    out = jax.ShapeDtypeStruct((chunk, width), bf16)
    return pl.pallas_call(
        body,
        grid=(4,),
        in_specs=[spec] * 3 + [WHOLE],
        out_specs=[WHOLE] * 4,
        out_shape=[out] * 4,
        compiler_params=kernel_params(),
        name="input_grads",
    )(grad_q, grad_k, grad_v, matrix)


def projection_grads(pieces, grad_q, grad_k, grad_v):
    chunk, width = pieces[0].shape
    group = grad_q.shape[1]

    def body(p0, p1, p2, p3, q_ref, k_ref, v_ref, o_ref, b_ref):
        for n, g_ref in enumerate((q_ref, k_ref, v_ref)):
            cols = slice(n * group, (n + 1) * group)
            acc = jnp.zeros((width, group), f32)
            for r, p_ref in enumerate((p0, p1, p2, p3)):
                acc = acc + dot_tn(p_ref[...], g_ref[r * chunk : (r + 1) * chunk, :])
            o_ref[:, cols] = acc.astype(bf16)
            b_ref[n : n + 1, :] = jnp.sum(g_ref[...].astype(f32), axis=0, keepdims=True)

    return pl.pallas_call(
        body,
        in_specs=[WHOLE] * 7,
        out_specs=[WHOLE] * 2,
        out_shape=[
            jax.ShapeDtypeStruct((width, 3 * group), bf16),
            jax.ShapeDtypeStruct((8, group), f32),
        ],
        compiler_params=kernel_params(),
        name="projection_grads",
    )(*pieces, grad_q, grad_k, grad_v)


def pack_local(params):
    return jnp.concatenate([params[9], params[11].T, params[5].T], axis=1)


def gather_all(local):
    parts = lax.all_gather(local, ("tensor", "dp"), axis=0, tiled=False)
    return parts.reshape(4, -1, local.shape[1])


def layer_forward(hidden, sent, context, params, matrix, weights, up_bias):
    low, high, place, query_marks, key_marks = context
    vectors = jnp.stack([params[6], params[7], params[8], params[12], params[13], params[14]])
    vectors = jnp.concatenate([vectors, jnp.zeros_like(vectors[:2])], axis=0)
    chunks = gather_chunks(sent)
    queries, keys, values = project(
        chunks, matrix, params[3], params[4], query_marks, key_marks
    )
    contexts, queries = attention_forward(low, high, place, queries, keys, values)
    pieces = exchange_pieces([contexts[r] for r in range(4)])
    out, out_low, normed, act, slope, y1, y2, r1, r2 = tokens_forward(
        place, hidden, pieces, weights, up_bias, vectors
    )
    saved = (chunks, queries, keys, values, contexts, pieces, normed, act, slope, y1, y2, r1, r2)
    return out, out_low, saved + (vectors,)


def layer_backward(grad, context, params, matrix, weights, saved):
    low, high, place = context[:3]
    chunks, queries, keys, values, contexts, pieces, normed, act, slope = saved[:9]
    y1, y2, r1, r2, vectors = saved[9:]
    width = grad.shape[1]
    group = pieces[0].shape[1] // 2
    (branch, inner, first, attn), sends, sums = tokens_backward(
        place, grad, (slope, y1, y2, r1, r2), weights, vectors, group
    )
    grads = exchange_pieces(sends)
    packed = weight_grads(place, normed, inner, branch, act, attn, pieces)
    wide = lax.psum_scatter(
        packed.reshape(4 * width, -1), ("tensor", "dp"), scatter_dimension=0, tiled=True
    ).astype(f32)
    grad_q, grad_k, grad_v = attention_backward(
        low, high, place, queries, keys, values, contexts, grads
    )
    partial = input_grads(grad_q, grad_k, grad_v, matrix)
    grad_in = first + scatter_chunks(partial)
    proj, proj_bias = projection_grads(chunks, grad_q, grad_k, grad_v)
    narrow = lax.psum_scatter(proj, "dp", scatter_dimension=0, tiled=True).astype(f32)
    sums = butterfly(sums, ("tensor", "dp"))
    proj_bias = butterfly(proj_bias, ("dp",))
    up_rows = lax.dynamic_slice_in_dim(sums, 6 + place[0], 1, 0)[0]
    out = (
        narrow[:, 0:group],
        narrow[:, group : 2 * group],
        narrow[:, 2 * group : 3 * group],
        proj_bias[0],
        proj_bias[2],
        wide[:, 2 * width : 2 * width + group].T,
        sums[5],
        sums[3],
        sums[4],
        wide[:, 0:width],
        up_rows,
        wide[:, width : 2 * width].T,
        sums[2],
        sums[0],
        sums[1],
    )
    return grad_in, out


def block_bounds(segments, place):
    total = segments.shape[0]
    blocks = segments.reshape(-1, TILE)
    begin = jnp.sum((segments[None] < blocks[:, :1]).astype(jnp.int32), axis=1) // TILE
    end = jnp.sum((segments[None] <= blocks[:, -1:]).astype(jnp.int32), axis=1)
    end = (end + TILE - 1) // TILE
    both = jnp.stack([begin, end]).reshape(2, 4, -1)
    both = reorder(both, place, 1).reshape(2, total // TILE)
    return both[0], both[1]


def reorder(values, place, axis):
    parts = [lax.dynamic_slice_in_dim(values, place ^ r, 1, axis) for r in range(4)]
    return jnp.concatenate(parts, axis=axis)


def on_device(tokens, segment_ids, valid_mask, teacher, *params):
    ask_params, doc_params = params[:15], params[15:]
    rows, width = tokens.shape
    place = lax.axis_index("tensor")
    segments = segment_ids[0]
    low, high = block_bounds(segments, place)
    local = reorder(segments.reshape(4, rows), place, 0).reshape(-1)
    same = local[:, None] == jnp.arange(SEGMENTS, dtype=jnp.int32)[None]
    spare = HEAD_DIM - SEGMENTS
    query_marks = jnp.pad(jnp.where(same, 0.0, -BLOCKED).astype(bf16), ((0, 0), (0, spare)))
    key_marks = jnp.concatenate(
        [same.astype(bf16), jnp.ones((4 * rows, 3), bf16), jnp.zeros((4 * rows, spare - 3), bf16)],
        axis=1,
    )
    context = (low, high, place[None], query_marks, key_marks)

    ask_matrix = lax.all_gather(
        jnp.concatenate(ask_params[0:3], axis=1), "dp", axis=0, tiled=True
    )
    doc_local = jnp.concatenate(doc_params[0:3], axis=1)
    group3 = doc_local.shape[1]
    doc_local = jnp.pad(doc_local, ((0, 0), (0, LANES)))
    ask_weights = gather_all(pack_local(ask_params))
    doc_matrix = lax.all_gather(doc_local, "dp", axis=0, tiled=True)[:, :group3]
    doc_weights = gather_all(pack_local(doc_params))
    up_local = jnp.stack([ask_params[10], doc_params[10]])
    up_all = jnp.stack([up_local] + [flip(up_local, r) for r in range(1, 4)])
    up_all = reorder(up_all, place, 0)

    mask_rows = valid_mask.astype(f32)
    valid_total = butterfly(
        jnp.full((8, LANES), jnp.sum(mask_rows), f32), ("tensor", "dp")
    )[0, 0]
    all_rows = rows * lax.axis_size("dp") * lax.axis_size("tensor")

    middle, middle_low, ask_saved = layer_forward(
        tokens, tokens, context, ask_params, ask_matrix, ask_weights, up_all[:, 0]
    )
    final, final_low, doc_saved = layer_forward(
        middle, middle_low, context, doc_params, doc_matrix, doc_weights, up_all[:, 1]
    )
    grad_final = mask_rows[:, None] * (final - teacher.astype(f32)) * (all_rows / valid_total)
    grad_middle, doc_grads = layer_backward(
        grad_final, context, doc_params, doc_matrix, doc_weights, doc_saved
    )
    grad_input, ask_grads = layer_backward(
        grad_middle, context, ask_params, ask_matrix, ask_weights, ask_saved
    )
    return (final_low, grad_input) + ask_grads + doc_grads


def layer_specs():
    return (
        P("dp", "tensor"),
        P("dp", "tensor"),
        P("dp", "tensor"),
        P("tensor"),
        P("tensor"),
        P("tensor", "dp"),
        P(),
        P(),
        P(),
        P("dp", "tensor"),
        P("tensor"),
        P("tensor", "dp"),
        P(),
        P(),
        P(),
    )


def solution(mesh):
    rows = P(("dp", "tensor"), None)
    return jax.shard_map(
        on_device,
        mesh=mesh,
        in_specs=(rows, P("dp", None), P(("dp", "tensor")), rows) + layer_specs() * 2,
        out_specs=(rows, rows) + layer_specs() * 2,
        check_vma=False,
    )
```

time: 4530 us -> 1250 us (0.28)
  matrix products: 2340 us -> 0 us
  waiting for transfers between devices: 1400 us -> 430 us
  Pallas kernels: 0 us -> 620 us
  other arithmetic: 294 us -> 36.4 us
  blocking collectives: 295 us -> 37.6 us
  loops' own time: 86.2 us -> 0 us
  starting transfers between devices: 2.44 us -> 53.6 us
    dot_general x142 -> x0, matrix products: 2330 us -> none  [the longest x16 558 us: one_block(): jnp.einsum('hqk,qhd->khd', grad_raw, query_part, preferred_element_type=j...]
    pallas_call x0 -> x16, Pallas kernels: none -> 620 us  [the longest x2 268 us: attention_backward(): pl.pallas_call(body, grid_spec=pltpu.PrefetchScalarGridSpec(num_scalar_pr...]
    reduce_scatter x15 -> x4, waiting for transfers between devices: 825 us -> 217 us  [the longest x2 217 us: layer_backward(): lax.psum_scatter(packed.reshape(4 * width, -1), ('tensor', 'dp'), scatter...]
    all_gather x12 -> x3, waiting for transfers between devices: 316 us -> 0.02 us  [the longest x2 0.02 us: gather_all(): parts = lax.all_gather(local, ('tensor', 'dp'), axis=0, tiled=False)]
    reduce_sum x38 -> x2, other arithmetic: 236 us -> 1.34 us  [the longest x1 0.74 us: block_bounds(): end = jnp.sum((segments[None] <= blocks[:, -1:]).astype(jnp.int32), axis=1)]
    all_gather x8 -> x1, blocking collectives: 256 us -> 37.6 us  [on_device(): lax.all_gather(jnp.concatenate(ask_params[0:3], axis=1), 'dp', axis=0, ti...]
    ppermute x0 -> x52, waiting for transfers between devices: none -> 212 us  [the longest x31 133 us: flip(): return lax.ppermute(values, 'tensor', [(i, i ^ bit) for i in range(size)])]
    unnamed x38 -> x7, waiting for transfers between devices: 202 us -> 0.11 us
  transfers between devices with their start and end apart: 33 -> 59, of which waited for: 27 -> 29; matrix products, arithmetic and copies ran while one was open for 24% -> 6% of each run, Pallas kernels for 0% -> 34%
where the time goes in v1:
time: 1250 us; the launch traced here: 1240 us
  Pallas kernels  620 us (50%)
  waiting for transfers between devices  430 us (34%)
  starting transfers between devices  53.6 us (4%)
  local copies, waits for them, and re-layouts  48.1 us (4%)
  blocking collectives  37.6 us (3%)
  other arithmetic  36.4 us (3%)
  between operations  15.9 us (1%)
    pallas_call x2, Pallas kernels, attention_backward(): pl.pallas_call(body, grid_spec=pltpu.PrefetchScalarGridSpec(num_scalar_pr...  268 us
    reduce_scatter x2, waiting for transfers between devices, layer_backward(): lax.psum_scatter(packed.reshape(4 * width, -1), ('tensor', 'dp'), scatter...  217 us
    pallas_call x2, Pallas kernels, attention_forward(): pl.pallas_call(body, grid_spec=pltpu.PrefetchScalarGridSpec(num_scalar_pr...  145 us
    ppermute x31, waiting for transfers between devices, flip(): return lax.ppermute(values, 'tensor', [(i, i ^ bit) for i in range(size)])  133 us
    ppermute x21, waiting for transfers between devices, butterfly(): other = lax.ppermute(values, axis, [(i, i ^ step) for i in range(size)])  79.5 us
    pallas_call x2, Pallas kernels, tokens_forward(): pl.pallas_call(body, grid_spec=pltpu.PrefetchScalarGridSpec(num_scalar_pr...  53.9 us
    pallas_call x2, Pallas kernels, tokens_backward(): pl.pallas_call(body, grid_spec=pltpu.PrefetchScalarGridSpec(num_scalar_pr...  48.9 us
    pallas_call x2, Pallas kernels, weight_grads(): pl.pallas_call(body, grid_spec=pltpu.PrefetchScalarGridSpec(num_scalar_pr...  37.6 us
  transfers between devices with their start and end apart: 59, of which 29 were waited for; matrix products, arithmetic and copies ran while one was open for 6% of the time, Pallas kernels for 34%

profile of v1, /device:TPU:0, one launch (start us, length us, event | category | flops | bytes accessed | tf_op | source)
XLA Modules:
  0.0 1241.5 jit_solution(8574442643484405532)
XLA Ops:
  15.1 2.6 collective-permute-start.9
  30.4 37.6 %all_gather.18.mat = bf16[768,576]{1,0:T(8,128)(2,1)} all-gather(bf16[96,576]{1,0:T(8,128)(2,1)S(1)} %pad_maximum_fusion.2), channel_id=1, replica_groups=mesh['dp'=8,'tensor'=4] {'dp'}, dimensions={0}, use_global_device_ids=true | all-gather | bytes 995328 | tf_op jit(solution)/shard_map/all_gather | solution.py:711
  81.5 10.7 project.2
  92.2 72.7 %attention_forward.2 = (bf16[4,512,384]{2,1,0:T(8,128)(2,1)}, bf16[4096,384]{1,0:T(8,128)(2,1)}) custom-call(s32[16]{0:T(128)} %squeeze.91.low_ref, s32[16]{0:T(128)} %squeeze.92.high_ref, s32[1]{0:T(128)} %bitcast.place_ref, bf16[4096,384]{1,0:T(8,128)(2,1)} %get-tuple-element.96.q_ref, bf16[4096,384]{1,0:T(8,128)(2,1)} %get-tuple-element.97.k_ref, ...), custom_call_target="tpu_custom_call" | custom-call | tf_op jit(solution)/shard_map/attention_forward/pallas_call | solution.py:204
  169.9 11.3 collective-permute-done.6.c2
  181.2 7.8 collective-permute-done.7.c3
  189.7 27.2 %tokens_forward.2 = (f32[2,512,768]{2,1,0:T(8,128)}, bf16[2,512,768]{2,1,0:T(8,128)(2,1)}, bf16[2,512,768]{2,1,0:T(8,128)(2,1)}, bf16[2,512,3072]{2,1,0:T(8,128)...) custom-call(s32[1]{0:T(128)} %bitcast.place_ref, ...), custom_call_target="tpu_custom_call" | custom-call | tf_op jit(solution)/shard_map/tokens_forward/pallas_call | solution.py:389
  220.7 30.2 %collective-permute-done.12 = bf16[512,768]{1,0:T(8,128)(2,1)S(1)} collective-permute-done((bf16[512,768]{1,0:T(8,128)(2,1)S(1)}, bf16[512,768]{1,0:T(8,128)(2,1)S(1)}, u32[]{:S(2)}, u32[]{:S(2)}) %collective-permute-start.12) | collective-permute-done | bytes 786464 | tf_op jit(solution)/shard_map/ppermute | solution.py:40
  250.9 16.8 %collective-permute-done.13 = bf16[512,768]{1,0:T(8,128)(2,1)} collective-permute-done((bf16[512,768]{1,0:T(8,128)(2,1)S(1)}, bf16[512,768]{1,0:T(8,128)(2,1)}, u32[]{:S(2)}, u32[]{:S(2)}) %collective-permute-start.13) | collective-permute-done | bytes 786464 | tf_op jit(solution)/shard_map/ppermute | solution.py:40
  277.1 10.8 project.3
  287.9 72.7 %attention_forward.3 = (bf16[4,512,384]{2,1,0:T(8,128)(2,1)}, bf16[4096,384]{1,0:T(8,128)(2,1)}) custom-call(s32[16]{0:T(128)} %squeeze.91.low_ref, s32[16]{0:T(128)} %squeeze.92.high_ref, s32[1]{0:T(128)} %bitcast.place_ref, bf16[4096,384]{1,0:T(8,128)(2,1)} %get-tuple-element.102.q_ref, bf16[4096,384]{1,0:T(8,128)(2,1)} %get-tuple-element.103.k_ref, ...), custom_call_target="tpu_custom_call" | custom-call | tf_op jit(solution)/shard_map/attention_forward/pallas_call | solution.py:204
  360.6 2.3 slice_bitcast_fusion.2
  365.9 17.1 %collective-permute-done.20 = f32[8,128]{1,0:T(8,128)S(1)} collective-permute-done((f32[8,128]{1,0:T(8,128)S(1)}, f32[8,128]{1,0:T(8,128)S(1)}, u32[]{:S(2)}, u32[]{:S(2)}) %collective-permute-start.20) | collective-permute-done | bytes 4128 | tf_op jit(solution)/shard_map/ppermute | solution.py:67
  387.3 2.6 collective-permute-start.22
  391.5 4.0 collective-permute-start.23
  399.3 26.7 %tokens_forward.3 = (f32[2,512,768]{2,1,0:T(8,128)}, bf16[2,512,768]{2,1,0:T(8,128)(2,1)}, bf16[2,512,768]{2,1,0:T(8,128)(2,1)}, bf16[2,512,3072]{2,1,0:T(8,128)...) custom-call(s32[1]{0:T(128)} %bitcast.place_ref, ...), custom_call_target="tpu_custom_call" | custom-call | tf_op jit(solution)/shard_map/tokens_forward/pallas_call | solution.py:389
  426.1 4.0 fusion.1
  430.1 24.5 %tokens_backward.2 = (bf16[2,512,768]{2,1,0:T(8,128)(2,1)}, bf16[2,512,3072]{2,1,0:T(8,128)(2,1)}, f32[2,512,768]{2,1,0:T(8,128)}, bf16[2,512,768]{2,1,0:T(8,128...) custom-call(s32[1]{0:T(128)} %bitcast.place_ref, ...), custom_call_target="tpu_custom_call" | custom-call | tf_op jit(solution)/shard_map/tokens_backward/pallas_call | solution.py:493
  456.6 10.3 collective-permute-done.25.g2
  466.9 7.3 collective-permute-done.26.g3
  475.0 133.7 %attention_backward.2 = (bf16[4096,192]{1,0:T(8,128)(2,1)}, bf16[4096,192]{1,0:T(8,128)(2,1)}, bf16[4096,192]{1,0:T(8,128)(2,1)}) custom-call(s32[16]{0:T(128)} %squeeze.91.low_ref, s32[16]{0:T(128)} %squeeze.92.high_ref, s32[1]{0:T(128)} %bitcast.place_ref, bf16[4096,384]{1,0:T(8,128)(2,1)} %get-tuple-element.114.q_ref, ...), custom_call_target="tpu_custom_call" | custom-call | tf_op jit(solution)/shard_map/attention_backward/pallas_call | solution.py:312
  608.7 11.4 input_grads.2
  620.6 3.1 collective-permute-done.28
  623.7 3.0 add_convert_fusion.1
  627.3 11.2 projection_grads.3
  638.6 25.2 %collective-permute-done.29 = bf16[1024,768]{1,0:T(8,128)(2,1)} collective-permute-done((bf16[1024,768]{1,0:T(8,128)(2,1)}, bf16[1024,768]{1,0:T(8,128)(2,1)}, u32[]{:S(2)}, u32[]{:S(2)}) %collective-permute-start.29) | collective-permute-done | bytes 1572896 | tf_op jit(solution)/shard_map/ppermute | solution.py:40
  663.7 4.7 bitcast_add_fusion.1
  668.5 24.4 %tokens_backward.3 = (bf16[2,512,768]{2,1,0:T(8,128)(2,1)}, bf16[2,512,3072]{2,1,0:T(8,128)(2,1)}, f32[2,512,768]{2,1,0:T(8,128)}, bf16[2,512,768]{2,1,0:T(8,128...) custom-call(s32[1]{0:T(128)} %bitcast.place_ref, ...), custom_call_target="tpu_custom_call" | custom-call | tf_op jit(solution)/shard_map/tokens_backward/pallas_call | solution.py:493
  694.9 10.3 collective-permute-done.31.g2
  705.3 7.3 collective-permute-done.32.g3
  713.4 134.1 %attention_backward.3 = (bf16[4096,192]{1,0:T(8,128)(2,1)}, bf16[4096,192]{1,0:T(8,128)(2,1)}, bf16[4096,192]{1,0:T(8,128)(2,1)}) custom-call(s32[16]{0:T(128)} %squeeze.91.low_ref, s32[16]{0:T(128)} %squeeze.92.high_ref, s32[1]{0:T(128)} %bitcast.place_ref, bf16[4096,384]{1,0:T(8,128)(2,1)} %get-tuple-element.132.q_ref, ...), custom_call_target="tpu_custom_call" | custom-call | tf_op jit(solution)/shard_map/attention_backward/pallas_call | solution.py:312
  847.4 11.0 projection_grads.2
  858.5 18.7 %weight_grads.3 = bf16[4,768,1728]{2,1,0:T(8,128)(2,1)} custom-call(s32[1]{0:T(128)} %bitcast.place_ref, bf16[1024,768]{1,0:T(8,128)(2,1)} %bitcast.105, bf16[1024,3072]{1,0:T(8,128)(2,1)} %bitcast.102, bf16[1024,768]{1,0:T(8,128)(2,1)} %bitcast.106, bf16[1024,3072]{1,0:T(8,128)(2,1)} %bitcast.101, bf16[1024,768]{1,0:T(8,128)(2,1)} %bitcast.107, ...), custom_call_target="tpu_custom_call" | custom-call | tf_op jit(solution)/shard_map/weight_grads/pallas_call | solution.py:541
  877.3 18.9 %weight_grads.2 = bf16[4,768,1728]{2,1,0:T(8,128)(2,1)} custom-call(s32[1]{0:T(128)} %bitcast.place_ref, bf16[1024,768]{1,0:T(8,128)(2,1)} %bitcast.104, bf16[1024,3072]{1,0:T(8,128)(2,1)} %bitcast.103, bf16[1024,768]{1,0:T(8,128)(2,1)} %bitcast.108, bf16[1024,3072]{1,0:T(8,128)(2,1)} %bitcast.100, bf16[1024,768]{1,0:T(8,128)(2,1)} %bitcast.109, ...), custom_call_target="tpu_custom_call" | custom-call | tf_op jit(solution)/shard_map/weight_grads/pallas_call | solution.py:541
  896.3 11.3 input_grads.3
  908.0 3.1 collective-permute-done.34
  911.2 3.2 add_convert_fusion
  917.7 34.5 %collective-permute-done.48 = f32[16,768]{1,0:T(8,128)S(1)} collective-permute-done((f32[16,768]{1,0:T(8,128)S(1)}, f32[16,768]{1,0:T(8,128)S(1)}, u32[]{:S(2)}, u32[]{:S(2)}) %collective-permute-start.48) | collective-permute-done | bytes 49184 | tf_op jit(solution)/shard_map/ppermute | solution.py:67
  953.7 2.6 collective-permute-done.49
  956.4 5.5 collective-permute-start.50
  963.9 8.8 collective-permute-start.51
  977.1 3.6 collective-permute-done.45
  989.5 2.6 collective-permute-start.43
  993.8 3.8 collective-permute-done.43
  999.0 3.7 collective-permute-done.38
  1004.9 4.7 bitcast_add_fusion
  1009.6 72.6 %reduce-scatter.11.cloned.1.call-done = bf16[96,1728]{1,0:T(8,128)(2,1)} async-done(((bf16[3072,1728]{1,0:T(8,128)(2,1)}), bf16[96,1728]{1,0:T(8,128)(2,1)}) %reduce-scatter.11.cloned.1.call-update) | async-done | bytes 331792 | tf_op jit(solution)/shard_map/reduce_scatter | solution.py:646
  1086.3 144.8 %reduce-scatter.7.cloned.1.call-done = bf16[96,1728]{1,0:T(8,128)(2,1)} async-done(((bf16[3072,1728]{1,0:T(8,128)(2,1)}), bf16[96,1728]{1,0:T(8,128)(2,1)}) %reduce-scatter.7.cloned.1.call-update) | async-done | bytes 331792 | tf_op jit(solution)/shard_map/reduce_scatter | solution.py:646
  (289 shorter events, 104.5 us)
Async XLA Ops:
  7.2 181.7 %all-gather.8.cloned.1.call-start = ((), (), s32[]{:S(2)}) async-start(), calls=%async_computation.9 | async-start | bytes 11354112 | tf_op jit(solution)/shard_map/all_gather | solution.py:614
  10.1 259.4 %all-gather.6.cloned.1.call-start = ((), (), s32[]{:S(2)}) async-start(), calls=%async_computation.4 | async-start | bytes 1327104 | tf_op jit(solution)/shard_map/all_gather | solution.py:718
  11.7 386.6 %all-gather.10.cloned.1.call-start = ((), (), s32[]{:S(2)}) async-start(), calls=%async_computation.10 | async-start | bytes 11354112 | tf_op jit(solution)/shard_map/all_gather | solution.py:614
  14.5 977.6 %reduce-scatter.9.cloned.1.call-start = ((), (), s32[]{:S(2)}) async-start(), calls=%async_computation.7 | async-start | bytes 1105920 | tf_op jit(solution)/shard_map/reduce_scatter | solution.py:655
  14.6 54.0 %collective-permute-start.8 = (f32[2,768]{1,0:T(2,128)S(1)}, f32[2,768]{1,0:T(2,128)S(1)}, u32[]{:S(2)}, u32[]{:S(2)}) collective-permute-start(f32[2,768]{1,0:T(2,128)S(1)} %get-tuple-element.275), channel_id=1, source_target_pairs={{0,1},{1,0},{2,3},{3,2},{4,5},{5,4},{6,7},{7,6},{8,9},{9,8},{10,11... | collective-permute-start | bytes 18440 | tf_op jit(solution)/shard_map/ppermute | solution.py:40
  15.1 60.8 %collective-permute-start.9 = (f32[2,768]{1,0:T(2,128)S(1)}, f32[2,768]{1,0:T(2,128)S(1)}, u32[]{:S(2)}, u32[]{:S(2)}) collective-permute-start(f32[2,768]{1,0:T(2,128)S(1)} %get-tuple-element.275), channel_id=1, source_target_pairs={{0,2},{1,3},{2,0},{3,1},{4,6},{5,7},{6,4},{7,5},{8,10},{9,11},{10,... | collective-permute-start | bytes 18440 | tf_op jit(solution)/shard_map/ppermute | solution.py:40
  17.7 62.7 %collective-permute-start = (bf16[1024,768]{1,0:T(8,128)(2,1)S(1)}, bf16[1024,768]{1,0:T(8,128)(2,1)}, u32[]{:S(2)}, u32[]{:S(2)}) collective-permute-start(bf16[1024,768]{1,0:T(8,128)(2,1)S(1)} %copy-done), channel_id=1, source_target_pairs={{0,1},{1,0},{2,3},{3,2},{4,5},{5,4},{6,7},{7,6},{8,9},{9,8},{10,11... | collective-permute-start | bytes 4718600 | tf_op jit(solution)/shard_map/ppermute | solution.py:40
  19.1 48.8 %collective-permute-start.1 = (bf16[512,768]{1,0:T(8,128)(2,1)}, bf16[512,768]{1,0:T(8,128)(2,1)S(1)}, u32[]{:S(2)}, u32[]{:S(2)}) collective-permute-start(bf16[512,768]{1,0:T(8,128)(2,1)} %get-tuple-element.251), channel_id=1, source_target_pairs={{0,2},{1,3},{2,0},{3,1},{4,6},{5,7},{6,4},{7,5},{8,10},{9,11},{10,... | collective-permute-start | bytes 2359304 | tf_op jit(solution)/shard_map/ppermute | solution.py:40
  19.4 48.6 %collective-permute-start.2 = (bf16[512,768]{1,0:T(8,128)(2,1)}, bf16[512,768]{1,0:T(8,128)(2,1)}, u32[]{:S(2)}, u32[]{:S(2)}) collective-permute-start(bf16[512,768]{1,0:T(8,128)(2,1)} %get-tuple-element.250), channel_id=1, source_target_pairs={{0,2},{1,3},{2,0},{3,1},{4,6},{5,7},{6,4},{7,5},{8,10},{9,11},{10,... | collective-permute-start | bytes 2359304 | tf_op jit(solution)/shard_map/ppermute | solution.py:40
  67.9 9.4 collective-permute-start.3
  68.0 11.2 collective-permute-start.4
  68.6 7.4 collective-permute-start.10
  167.8 13.4 %collective-permute-start.6 = (bf16[512,384]{1,0:T(8,128)(2,1)S(1)}, bf16[512,384]{1,0:T(8,128)(2,1)S(1)}, u32[]{:S(2)}, u32[]{:S(2)}) collective-permute-start(bf16[512,384]{1,0:T(8,128)(2,1)S(1)} %get-tuple-element.247), channel_id=1, source_target_pairs={{0,2},{1,3},{2,0},{3,1},{4,6},{5,7},{6,4},{7,5},{8,10},{9,11},{10,... | collective-permute-start | bytes 1179656 | tf_op jit(solution)/shard_map/ppermute | solution.py:40
  169.2 19.7 %collective-permute-start.7 = (bf16[512,384]{1,0:T(8,128)(2,1)S(1)}, bf16[512,384]{1,0:T(8,128)(2,1)S(1)}, u32[]{:S(2)}, u32[]{:S(2)}) collective-permute-start(bf16[512,384]{1,0:T(8,128)(2,1)S(1)} %get-tuple-element.246), channel_id=1, source_target_pairs={{0,3},{1,2},{2,1},{3,0},{4,7},{5,6},{6,5},{7,4},{8,11},{9,10},{10,... | collective-permute-start | bytes 1179656 | tf_op jit(solution)/shard_map/ppermute | solution.py:40
  218.6 32.3 %collective-permute-start.12 = (bf16[512,768]{1,0:T(8,128)(2,1)S(1)}, bf16[512,768]{1,0:T(8,128)(2,1)S(1)}, u32[]{:S(2)}, u32[]{:S(2)}) collective-permute-start(bf16[512,768]{1,0:T(8,128)(2,1)S(1)} %get-tuple-element.245), channel_id=1, source_target_pairs={{0,2},{1,3},{2,0},{3,1},{4,6},{5,7},{6,4},{7,5},{8,10},{9,11},{10,... | collective-permute-start | bytes 2359304 | tf_op jit(solution)/shard_map/ppermute | solution.py:40
  219.3 48.4 %collective-permute-start.13 = (bf16[512,768]{1,0:T(8,128)(2,1)S(1)}, bf16[512,768]{1,0:T(8,128)(2,1)}, u32[]{:S(2)}, u32[]{:S(2)}) collective-permute-start(bf16[512,768]{1,0:T(8,128)(2,1)S(1)} %get-tuple-element.244), channel_id=1, source_target_pairs={{0,2},{1,3},{2,0},{3,1},{4,6},{5,7},{6,4},{7,5},{8,10},{9,11},{10,... | collective-permute-start | bytes 2359304 | tf_op jit(solution)/shard_map/ppermute | solution.py:40
  220.7 55.3 %collective-permute-start.11 = (bf16[1024,768]{1,0:T(8,128)(2,1)S(1)}, bf16[1024,768]{1,0:T(8,128)(2,1)}, u32[]{:S(2)}, u32[]{:S(2)}) collective-permute-start(bf16[1024,768]{1,0:T(8,128)(2,1)S(1)} %bitcast.97), channel_id=1, source_target_pairs={{0,1},{1,0},{2,3},{3,2},{4,5},{5,4},{6,7},{7,6},{8,9},{9,8},{10,11... | collective-permute-start | bytes 4718600 | tf_op jit(solution)/shard_map/ppermute | solution.py:40
  250.8 22.1 %collective-permute-start.14 = (bf16[512,768]{1,0:T(8,128)(2,1)S(1)}, bf16[512,768]{1,0:T(8,128)(2,1)}, u32[]{:S(2)}, u32[]{:S(2)}) collective-permute-start(bf16[512,768]{1,0:T(8,128)(2,1)S(1)} %collective-permute-done.12), channel_id=1, source_target_pairs={{0,1},{1,0},{2,3},{3,2},{4,5},{5,4},{6,7},{7,6},{8,9},{9,8},{10,11... | collective-permute-start | bytes 2359304 | tf_op jit(solution)/shard_map/ppermute | solution.py:40
  267.7 7.1 collective-permute-start.15
  268.9 95.9 %collective-permute-start.19 = (f32[8,128]{1,0:T(8,128)S(1)}, f32[8,128]{1,0:T(8,128)S(1)}, u32[]{:S(2)}, u32[]{:S(2)}) collective-permute-start(f32[8,128]{1,0:T(8,128)S(1)} %broadcast_in_dim.43), channel_id=1, source_target_pairs={{0,1},{1,0},{2,3},{3,2},{4,5},{5,4},{6,7},{7,6},{8,9},{9,8},{10,11... | collective-permute-start | bytes 12296 | tf_op jit(solution)/shard_map/ppermute | solution.py:67
  363.0 35.4 %collective-permute-start.16 = (bf16[512,384]{1,0:T(8,128)(2,1)S(1)}, bf16[512,384]{1,0:T(8,128)(2,1)S(1)}, u32[]{:S(2)}, u32[]{:S(2)}) collective-permute-start(bf16[512,384]{1,0:T(8,128)(2,1)S(1)} %get-tuple-element.242), channel_id=1, source_target_pairs={{0,1},{1,0},{2,3},{3,2},{4,5},{5,4},{6,7},{7,6},{8,9},{9,8},{10,11... | collective-permute-start | bytes 1179656 | tf_op jit(solution)/shard_map/ppermute | solution.py:40
  363.0 35.4 %collective-permute-start.17 = (bf16[512,384]{1,0:T(8,128)(2,1)S(1)}, bf16[512,384]{1,0:T(8,128)(2,1)S(1)}, u32[]{:S(2)}, u32[]{:S(2)}) collective-permute-start(bf16[512,384]{1,0:T(8,128)(2,1)S(1)} %get-tuple-element.241), channel_id=1, source_target_pairs={{0,2},{1,3},{2,0},{3,1},{4,6},{5,7},{6,4},{7,5},{8,10},{9,11},{10,... | collective-permute-start | bytes 1179656 | tf_op jit(solution)/shard_map/ppermute | solution.py:40
  363.4 35.0 %collective-permute-start.18 = (bf16[512,384]{1,0:T(8,128)(2,1)S(1)}, bf16[512,384]{1,0:T(8,128)(2,1)S(1)}, u32[]{:S(2)}, u32[]{:S(2)}) collective-permute-start(bf16[512,384]{1,0:T(8,128)(2,1)S(1)} %get-tuple-element.240), channel_id=1, source_target_pairs={{0,3},{1,2},{2,1},{3,0},{4,7},{5,6},{6,5},{7,4},{8,11},{9,10},{10,... | collective-permute-start | bytes 1179656 | tf_op jit(solution)/shard_map/ppermute | solution.py:40
  365.5 17.5 %collective-permute-start.20 = (f32[8,128]{1,0:T(8,128)S(1)}, f32[8,128]{1,0:T(8,128)S(1)}, u32[]{:S(2)}, u32[]{:S(2)}) collective-permute-start(f32[8,128]{1,0:T(8,128)S(1)} %broadcast_add_fusion), channel_id=1, source_target_pairs={{0,2},{1,3},{2,0},{3,1},{4,6},{5,7},{6,4},{7,5},{8,10},{9,11},{10,... | collective-permute-start | bytes 12296 | tf_op jit(solution)/shard_map/ppermute | solution.py:67
  387.3 4.2 collective-permute-start.22
  391.5 5.6 collective-permute-start.23
  454.6 12.3 collective-permute-start.25
  455.3 19.0 %collective-permute-start.26 = (bf16[512,384]{1,0:T(8,128)(2,1)}, bf16[512,384]{1,0:T(8,128)(2,1)S(1)}, u32[]{:S(2)}, u32[]{:S(2)}) collective-permute-start(bf16[512,384]{1,0:T(8,128)(2,1)} %get-tuple-element.118), channel_id=1, source_target_pairs={{0,3},{1,2},{2,1},{3,0},{4,7},{5,6},{6,5},{7,4},{8,11},{9,10},{10,... | collective-permute-start | bytes 1179656 | tf_op jit(solution)/shard_map/ppermute | solution.py:40
  620.5 18.1 %collective-permute-start.27 = (bf16[1024,768]{1,0:T(8,128)(2,1)}, bf16[1024,768]{1,0:T(8,128)(2,1)}, u32[]{:S(2)}, u32[]{:S(2)}) collective-permute-start(bf16[1024,768]{1,0:T(8,128)(2,1)} %get-tuple-element.123), channel_id=1, source_target_pairs={{0,1},{1,0},{2,3},{3,2},{4,5},{5,4},{6,7},{7,6},{8,9},{9,8},{10,11... | collective-permute-start | bytes 4718600 | tf_op jit(solution)/shard_map/ppermute | solution.py:40
  626.7 37.0 %collective-permute-start.29 = (bf16[1024,768]{1,0:T(8,128)(2,1)}, bf16[1024,768]{1,0:T(8,128)(2,1)}, u32[]{:S(2)}, u32[]{:S(2)}) collective-permute-start(bf16[1024,768]{1,0:T(8,128)(2,1)} %add_convert_fusion.1), channel_id=1, source_target_pairs={{0,2},{1,3},{2,0},{3,1},{4,6},{5,7},{6,4},{7,5},{8,10},{9,11},{10,... | collective-permute-start | bytes 4718600 | tf_op jit(solution)/shard_map/ppermute | solution.py:40
  638.5 364.7 %reduce-scatter.5.cloned.1.call-start = ((), (), s32[]{:S(2)}) async-start(), calls=%async_computation.5 | async-start | bytes 1105920 | tf_op jit(solution)/shard_map/reduce_scatter | solution.py:655
  693.0 12.3 collective-permute-start.31
  693.6 19.0 %collective-permute-start.32 = (bf16[512,384]{1,0:T(8,128)(2,1)}, bf16[512,384]{1,0:T(8,128)(2,1)S(1)}, u32[]{:S(2)}, u32[]{:S(2)}) collective-permute-start(bf16[512,384]{1,0:T(8,128)(2,1)} %get-tuple-element.136), channel_id=1, source_target_pairs={{0,3},{1,2},{2,1},{3,0},{4,7},{5,6},{6,5},{7,4},{8,11},{9,10},{10,... | collective-permute-start | bytes 1179656 | tf_op jit(solution)/shard_map/ppermute | solution.py:40
  858.5 223.7 %reduce-scatter.11.cloned.1.call-start = ((), (), s32[]{:S(2)}) async-start(), calls=%async_computation.8 | async-start | bytes 11354112 | tf_op jit(solution)/shard_map/reduce_scatter | solution.py:646
  877.3 353.9 %reduce-scatter.7.cloned.1.call-start = ((), (), s32[]{:S(2)}) async-start(), calls=%async_computation.6 | async-start | bytes 11354112 | tf_op jit(solution)/shard_map/reduce_scatter | solution.py:646
  907.8 97.0 %collective-permute-start.33 = (bf16[1024,768]{1,0:T(8,128)(2,1)}, bf16[1024,768]{1,0:T(8,128)(2,1)}, u32[]{:S(2)}, u32[]{:S(2)}) collective-permute-start(bf16[1024,768]{1,0:T(8,128)(2,1)} %get-tuple-element.141), channel_id=1, source_target_pairs={{0,1},{1,0},{2,3},{3,2},{4,5},{5,4},{6,7},{7,6},{8,9},{9,8},{10,11... | collective-permute-start | bytes 4718600 | tf_op jit(solution)/shard_map/ppermute | solution.py:40
  914.3 90.5 %collective-permute-start.35 = (bf16[1024,768]{1,0:T(8,128)(2,1)}, bf16[1024,768]{1,0:T(8,128)(2,1)}, u32[]{:S(2)}, u32[]{:S(2)}) collective-permute-start(bf16[1024,768]{1,0:T(8,128)(2,1)} %add_convert_fusion), channel_id=1, source_target_pairs={{0,2},{1,3},{2,0},{3,1},{4,6},{5,7},{6,4},{7,5},{8,10},{9,11},{10,... | collective-permute-start | bytes 4718600 | tf_op jit(solution)/shard_map/ppermute | solution.py:40
  916.1 36.1 %collective-permute-start.48 = (f32[16,768]{1,0:T(8,128)S(1)}, f32[16,768]{1,0:T(8,128)S(1)}, u32[]{:S(2)}, u32[]{:S(2)}) collective-permute-start(f32[16,768]{1,0:T(8,128)S(1)} %add.192), channel_id=1, source_target_pairs={{0,2},{1,3},{2,0},{3,1},{4,6},{5,7},{6,4},{7,5},{8,10},{9,11},{10,... | collective-permute-start | bytes 147464 | tf_op jit(solution)/shard_map/ppermute | solution.py:67
  956.4 7.6 collective-permute-start.50
  961.9 10.9 collective-permute-start.39
  963.9 13.2 %collective-permute-start.51 = (f32[16,768]{1,0:T(8,128)S(1)}, f32[16,768]{1,0:T(8,128)S(1)}, u32[]{:S(2)}, u32[]{:S(2)}) collective-permute-start(f32[16,768]{1,0:T(8,128)S(1)} %add.195), channel_id=1, source_target_pairs={{0,16},{4,20},{8,24},{12,28},{16,0},{20,4},{24,8},{28,12},{1,17},{... | collective-permute-start | bytes 147464 | tf_op jit(solution)/shard_map/ppermute | solution.py:67
  972.8 8.0 collective-permute-start.40
  980.7 4.5 collective-permute-start.46
  980.8 4.5 collective-permute-start.41
  985.4 6.7 collective-permute-start.36
  989.5 8.1 collective-permute-start.43
  992.1 5.5 collective-permute-start.37
  997.6 5.1 collective-permute-start.38
  (49 other events, 784.4 us)
Sparse Core Ops, SparseCore 0:
  11.0 103.2 all-gather.7
  117.1 39.7 all-gather.5
  159.9 100.4 all-gather.9
  638.6 69.0 reduce-scatter.8
  858.6 72.6 reduce-scatter.4
  937.1 145.0 reduce-scatter.10
  1088.2 142.9 reduce-scatter.6

commit v2 on v1

--- a/solution.py
+++ b/solution.py
@@ -31,6 +31,10 @@
     return lax.dot_general(first_mat, second_mat, TN, preferred_element_type=f32)
 
 
+def cost(flops):
+    return pl.CostEstimate(flops=int(flops), bytes_accessed=0, transcendentals=0)
+
+
 def kernel_params():
     return pltpu.CompilerParams(vmem_limit_bytes=60 * 1024 * 1024)
 
@@ -59,14 +63,31 @@
     return chunks[0].astype(f32) + near + far
 
 
-def butterfly(values, axes):
-    for axis in axes:
-        size = lax.axis_size(axis)
-        step = 1
-        while step < size:
-            other = lax.ppermute(values, axis, [(i, i ^ step) for i in range(size)])
-            values = values + other
-            step *= 2
+def tie(*items):
+    return lax.optimization_barrier(items)
+
+
+def send_around(values, axis, step, count):
+    size = lax.axis_size(axis)
+    return [
+        lax.ppermute(values, axis, [(i, i ^ (step * r)) for i in range(size)])
+        for r in range(1, count)
+    ]
+
+
+def add_up(values, others):
+    for other in others:
+        values = values + other
+    return values
+
+
+def sum_over(values, axis):
+    size = lax.axis_size(axis)
+    step = 1
+    while step < size:
+        count = min(8, size // step)
+        values = add_up(values, send_around(values, axis, step, count))
+        step *= count
     return values
 
 
@@ -114,6 +135,7 @@
         out_specs=[spec] * 3,
         out_shape=[out] * 3,
         compiler_params=kernel_params(),
+        cost_estimate=cost(6 * rows * 4 * pieces[0].shape[1] * matrix.shape[1]),
         name="project",
     )(*pieces, matrix, query_bias[None], value_bias[None], query_marks, key_marks)
 
@@ -222,6 +244,7 @@
             jax.ShapeDtypeStruct((rows, wide), bf16),
         ],
         compiler_params=kernel_params(),
+        cost_estimate=cost(12 * rows * rows * wide),
         name="attention_forward",
     )(low, high, place, queries, keys, values)
 
@@ -325,6 +348,7 @@
         ),
         out_shape=[out] * 3,
         compiler_params=kernel_params(),
+        cost_estimate=cost(24 * rows * rows * wide),
         name="attention_backward",
     )(low, high, place, queries, keys, values, contexts, *grads)
 
@@ -416,6 +440,7 @@
             out(LANES, f32),
         ],
         compiler_params=kernel_params(),
+        cost_estimate=cost(8 * rows * width * width * 3),
         name="tokens_forward",
     )(place, hidden.reshape(2, half, width), *pieces, weights, up_bias, vectors)
     return [item.reshape(rows, item.shape[2]) for item in results]
@@ -513,6 +538,7 @@
         + [piece] * 4
         + [sums],
         compiler_params=kernel_params(),
+        cost_estimate=cost(8 * rows * width * width * 3),
         name="tokens_backward",
     )(place, view(grad), view(slope), view(y1), view(y2), view(r1), view(r2), weights, vectors)
     big = [item.reshape(rows, item.shape[2]) for item in results[:4]]
@@ -548,6 +574,7 @@
         ),
         out_shape=jax.ShapeDtypeStruct((4, width, cols), bf16),
         compiler_params=kernel_params(),
+        cost_estimate=cost(8 * rows * width * width * 3),
         name="weight_grads",
     )(place, sent, inner, branch, act, attn, *pieces)
 
@@ -576,6 +603,7 @@
         out_specs=[WHOLE] * 4,
         out_shape=[out] * 4,
         compiler_params=kernel_params(),
+        cost_estimate=cost(6 * rows * width * 3 * group),
         name="input_grads",
     )(grad_q, grad_k, grad_v, matrix)
 
@@ -602,6 +630,7 @@
             jax.ShapeDtypeStruct((8, group), f32),
         ],
         compiler_params=kernel_params(),
+        cost_estimate=cost(24 * chunk * width * 3 * group),
         name="projection_grads",
     )(*pieces, grad_q, grad_k, grad_v)
 
@@ -615,65 +644,95 @@
     return parts.reshape(4, -1, local.shape[1])
 
 
-def layer_forward(hidden, sent, context, params, matrix, weights, up_bias):
+def layer_forward(hidden, chunks, context, params, matrix, weights, up_bias, ahead=None):
     low, high, place, query_marks, key_marks = context
     vectors = jnp.stack([params[6], params[7], params[8], params[12], params[13], params[14]])
     vectors = jnp.concatenate([vectors, jnp.zeros_like(vectors[:2])], axis=0)
-    chunks = gather_chunks(sent)
     queries, keys, values = project(
         chunks, matrix, params[3], params[4], query_marks, key_marks
     )
     contexts, queries = attention_forward(low, high, place, queries, keys, values)
+    contexts, ahead = tie(contexts, ahead)
     pieces = exchange_pieces([contexts[r] for r in range(4)])
     out, out_low, normed, act, slope, y1, y2, r1, r2 = tokens_forward(
         place, hidden, pieces, weights, up_bias, vectors
     )
     saved = (chunks, queries, keys, values, contexts, pieces, normed, act, slope, y1, y2, r1, r2)
-    return out, out_low, saved + (vectors,)
-
-
-def layer_backward(grad, context, params, matrix, weights, saved):
+    return out, out_low, saved + (vectors,), ahead
+
+
+def with_bias(proj, bias, parts):
+    rows, cols = proj.shape
+    high = bias.astype(bf16)
+    low = (bias - high.astype(f32)).astype(bf16)
+    tail = jnp.concatenate([high[None], low[None], jnp.zeros((14, cols), bf16)], axis=0)
+    tail = jnp.broadcast_to(tail[None], (parts,) + tail.shape)
+    return jnp.concatenate([proj.reshape(parts, rows // parts, cols), tail], axis=1)
+
+
+def layer_backward(grad, context, matrix, weights, saved, earlier=None):
     low, high, place = context[:3]
     chunks, queries, keys, values, contexts, pieces, normed, act, slope = saved[:9]
     y1, y2, r1, r2, vectors = saved[9:]
     width = grad.shape[1]
-    group = pieces[0].shape[1] // 2
+    parts = lax.axis_size("dp")
     (branch, inner, first, attn), sends, sums = tokens_backward(
-        place, grad, (slope, y1, y2, r1, r2), weights, vectors, group
-    )
+        place, grad, (slope, y1, y2, r1, r2), weights, vectors, pieces[0].shape[1] // 2
+    )
+    around = narrow = None
+    if earlier is not None:
+        sums = jnp.concatenate([earlier[0], sums], axis=0)
+        around = send_around(sums, "tensor", 1, 4)
+        narrow = lax.all_to_all(earlier[1], "dp", 0, 0, tiled=True)
     grads = exchange_pieces(sends)
     packed = weight_grads(place, normed, inner, branch, act, attn, pieces)
+    grads, packed, around, narrow = tie(grads, packed, around, narrow)
+    if earlier is not None:
+        sums = sum_over(add_up(sums, around), "dp")
     wide = lax.psum_scatter(
         packed.reshape(4 * width, -1), ("tensor", "dp"), scatter_dimension=0, tiled=True
     ).astype(f32)
     grad_q, grad_k, grad_v = attention_backward(
         low, high, place, queries, keys, values, contexts, grads
     )
+    if earlier is not None:
+        grad_q, grad_k, grad_v, sums = tie(grad_q, grad_k, grad_v, sums)
     partial = input_grads(grad_q, grad_k, grad_v, matrix)
     grad_in = first + scatter_chunks(partial)
     proj, proj_bias = projection_grads(chunks, grad_q, grad_k, grad_v)
-    narrow = lax.psum_scatter(proj, "dp", scatter_dimension=0, tiled=True).astype(f32)
-    sums = butterfly(sums, ("tensor", "dp"))
-    proj_bias = butterfly(proj_bias, ("dp",))
-    up_rows = lax.dynamic_slice_in_dim(sums, 6 + place[0], 1, 0)[0]
-    out = (
-        narrow[:, 0:group],
-        narrow[:, group : 2 * group],
-        narrow[:, 2 * group : 3 * group],
-        proj_bias[0],
-        proj_bias[2],
+    both = with_bias(proj, proj_bias[0:3].reshape(-1), parts)
+    if earlier is None:
+        grad_in, wide, both = tie(grad_in, wide, both)
+        return grad_in, wide, (sums, both)
+    both, wide = tie(both, wide)
+    both = lax.all_to_all(both, "dp", 0, 0, tiled=True)
+    return grad_in, wide, (sums, both, narrow)
+
+
+def layer_outputs(wide, narrow, sums, place):
+    narrow = jnp.sum(narrow.astype(f32), axis=0)
+    width = sums.shape[1]
+    group = wide.shape[1] - 2 * width
+    own = narrow.shape[0] - 16
+    bias = narrow[own] + narrow[own + 1]
+    up_row = lax.dynamic_slice_in_dim(sums, 6 + place[0], 1, 0)[0]
+    return (
+        narrow[:own, 0:group],
+        narrow[:own, group : 2 * group],
+        narrow[:own, 2 * group : 3 * group],
+        bias[0:group],
+        bias[2 * group : 3 * group],
         wide[:, 2 * width : 2 * width + group].T,
         sums[5],
         sums[3],
         sums[4],
         wide[:, 0:width],
-        up_rows,
+        up_row,
         wide[:, width : 2 * width].T,
         sums[2],
         sums[0],
         sums[1],
     )
-    return grad_in, out
 
 
 def block_bounds(segments, place):
@@ -716,30 +775,42 @@
     doc_local = jnp.pad(doc_local, ((0, 0), (0, LANES)))
     ask_weights = gather_all(pack_local(ask_params))
     doc_matrix = lax.all_gather(doc_local, "dp", axis=0, tiled=True)[:, :group3]
-    doc_weights = gather_all(pack_local(doc_params))
     up_local = jnp.stack([ask_params[10], doc_params[10]])
     up_all = jnp.stack([up_local] + [flip(up_local, r) for r in range(1, 4)])
     up_all = reorder(up_all, place, 0)
 
     mask_rows = valid_mask.astype(f32)
-    valid_total = butterfly(
-        jnp.full((8, LANES), jnp.sum(mask_rows), f32), ("tensor", "dp")
-    )[0, 0]
+    valid_total = jnp.full((8, LANES), jnp.sum(mask_rows), f32)
+    valid_total = sum_over(sum_over(valid_total, "tensor"), "dp")
+    ask_matrix, up_all, valid_total = tie(ask_matrix, up_all, valid_total)
+    valid_total = valid_total[0, 0]
     all_rows = rows * lax.axis_size("dp") * lax.axis_size("tensor")
 
-    middle, middle_low, ask_saved = layer_forward(
-        tokens, tokens, context, ask_params, ask_matrix, ask_weights, up_all[:, 0]
-    )
-    final, final_low, doc_saved = layer_forward(
-        middle, middle_low, context, doc_params, doc_matrix, doc_weights, up_all[:, 1]
+    middle, middle_low, ask_saved, doc_matrix = layer_forward(
+        tokens,
+        gather_chunks(tokens),
+        context,
+        ask_params,
+        ask_matrix,
+        ask_weights,
+        up_all[:, 0],
+        doc_matrix,
+    )
+    doc_chunks, doc_pack = tie(gather_chunks(middle_low), pack_local(doc_params))
+    doc_weights = gather_all(doc_pack)
+    final, final_low, doc_saved, _ = layer_forward(
+        middle, doc_chunks, context, doc_params, doc_matrix, doc_weights, up_all[:, 1]
     )
     grad_final = mask_rows[:, None] * (final - teacher.astype(f32)) * (all_rows / valid_total)
-    grad_middle, doc_grads = layer_backward(
-        grad_final, context, doc_params, doc_matrix, doc_weights, doc_saved
-    )
-    grad_input, ask_grads = layer_backward(
-        grad_middle, context, ask_params, ask_matrix, ask_weights, ask_saved
-    )
+    grad_middle, doc_wide, pending = layer_backward(
+        grad_final, context, doc_matrix, doc_weights, doc_saved
+    )
+    grad_input, ask_wide, (sums, ask_narrow, doc_narrow) = layer_backward(
+        grad_middle, context, ask_matrix, ask_weights, ask_saved, pending
+    )
+    half = sums.shape[0] // 2
+    doc_grads = layer_outputs(doc_wide, doc_narrow, sums[:half], context[2])
+    ask_grads = layer_outputs(ask_wide, ask_narrow, sums[half:], context[2])
     return (final_low, grad_input) + ask_grads + doc_grads
 
 

time: 1250 us -> 952 us (0.76)
  waiting for transfers between devices: 430 us -> 117 us
  starting transfers between devices: 53.6 us -> 68.8 us
  local copies, waits for them, and re-layouts: 48.1 us -> 33.3 us
    reduce_scatter x2, waiting for transfers between devices: 217 us -> 0.01 us  [layer_backward(): lax.psum_scatter(packed.reshape(4 * width, -1), ('tensor', 'dp'), scatter...]
    ppermute x21 -> x20, waiting for transfers between devices: 79.5 us -> 7.06 us  [send_around(): lax.ppermute(values, axis, [(i, i ^ step * r) for i in range(size)])]
    ppermute x31, waiting for transfers between devices: 133 us -> 110 us  [flip(): return lax.ppermute(values, 'tensor', [(i, i ^ bit) for i in range(size)])]
    all_to_all x0 -> x2, starting transfers between devices: none -> 21.4 us  [the longest x1 11.9 us: layer_backward(): narrow = lax.all_to_all(earlier[1], 'dp', 0, 0, tiled=True)]
    ppermute x21 -> x20, starting transfers between devices: 35.3 us -> 27.6 us  [send_around(): lax.ppermute(values, axis, [(i, i ^ step * r) for i in range(size)])]
  transfers between devices with their start and end apart: 59 -> 58, of which waited for: 29 -> 17; matrix products, arithmetic and copies ran while one was open for 6% -> 7% of each run, Pallas kernels for 34% -> 58%
where the time goes in v2:
time: 952 us; the launch traced here: 939 us
  Pallas kernels  620 us (65%)
  waiting for transfers between devices  117 us (12%)
  starting transfers between devices  68.8 us (7%)
  other arithmetic  46.3 us (5%)
  blocking collectives  37.6 us (4%)
  local copies, waits for them, and re-layouts  33.3 us (3%)
  between operations  16 us (2%)
    pallas_call x2, Pallas kernels, attention_backward(): pl.pallas_call(body, grid_spec=pltpu.PrefetchScalarGridSpec(num_scalar_pr...  269 us
    pallas_call x2, Pallas kernels, attention_forward(): pl.pallas_call(body, grid_spec=pltpu.PrefetchScalarGridSpec(num_scalar_pr...  145 us
    ppermute x31, waiting for transfers between devices, flip(): return lax.ppermute(values, 'tensor', [(i, i ^ bit) for i in range(size)])  110 us
    pallas_call x2, Pallas kernels, tokens_forward(): pl.pallas_call(body, grid_spec=pltpu.PrefetchScalarGridSpec(num_scalar_pr...  53 us
    pallas_call x2, Pallas kernels, tokens_backward(): pl.pallas_call(body, grid_spec=pltpu.PrefetchScalarGridSpec(num_scalar_pr...  48.6 us
    all_gather x1, blocking collectives, on_device(): lax.all_gather(jnp.concatenate(ask_params[0:3], axis=1), 'dp', axis=0, ti...  37.6 us
    pallas_call x2, Pallas kernels, weight_grads(): pl.pallas_call(body, grid_spec=pltpu.PrefetchScalarGridSpec(num_scalar_pr...  37.4 us
    ppermute x20, starting transfers between devices, send_around(): lax.ppermute(values, axis, [(i, i ^ step * r) for i in range(size)])  27.6 us
  transfers between devices with their start and end apart: 58, of which 17 were waited for; matrix products, arithmetic and copies ran while one was open for 7% of the time, Pallas kernels for 58%

profile of v2, /device:TPU:0, one launch (start us, length us, event | category | flops | bytes accessed | tf_op | source)
XLA Modules:
  0.0 939.1 jit_solution(5700801579658701147)
XLA Ops:
  13.8 2.5 collective-permute-start.10
  18.2 2.0 collective-permute-start.1
  22.5 37.6 %all_gather.18.mat = bf16[768,576]{1,0:T(8,128)(2,1)} all-gather(bf16[96,576]{1,0:T(8,128)(2,1)S(1)} %pad_maximum_fusion.6), channel_id=1, replica_groups=mesh['dp'=8,'tensor'=4] {'dp'}, dimensions={0}, use_global_device_ids=true | all-gather | bytes 995328 | tf_op jit(solution)/shard_map/all_gather | solution.py:770
  74.2 2.0 collective-permute-start.13
  79.1 2.2 collective-permute-start.15
  82.4 2.4 collective-permute-start.16
  84.8 2.3 collective-permute-start.17
  87.8 3.3 collective-permute-done.17
  94.3 10.7 %project.2 = (bf16[4096,384]{1,0:T(8,128)(2,1)}, bf16[4096,384]{1,0:T(8,128)(2,1)}, bf16[4096,384]{1,0:T(8,128)(2,1)}) custom-call(bf16[1024,768]{1,0:T(8,128)(2,1)} %p0.3, bf16[1024,768]{1,0:T(8,128)(2,1)} %collective-permute-done.p1, bf16[1024,768]{1,0:T(8,128)(2,1)} %copy-done.12, bf16[1024,768]{1,0:T(8,128)(2,1)} %copy-done.11, ...), custom_call_target="tpu_custom_call" | custom-call | flops 10871635968 | tf_op jit(solution)/shard_map/project/pallas_call | solution.py:131
  105.0 72.7 %attention_forward.2 = (bf16[4,512,384]{2,1,0:T(8,128)(2,1)}, bf16[4096,384]{1,0:T(8,128)(2,1)}) custom-call(s32[16]{0:T(128)} %squeeze.83.low_ref, s32[16]{0:T(128)} %squeeze.84.high_ref, s32[1]{0:T(128)} %bitcast.place_ref, bf16[4096,384]{1,0:T(8,128)(2,1)} %get-tuple-element.130.q_ref, bf16[4096,384]{1,0:T(8,128)(2,1)} %get-tuple-element.131.k_ref, ...), custom_call_target="tpu_custom_call" | custom-call | flops 77309411328 | tf_op jit(solution)/shard_map/attention_forward/pallas_call | solution.py:226
  177.7 2.3 slice.266.mat
  184.3 8.7 collective-permute-done.19.c2
  193.0 7.5 collective-permute-done.20.c3
  201.2 26.4 %tokens_forward.2 = (f32[2,512,768]{2,1,0:T(8,128)}, bf16[2,512,768]{2,1,0:T(8,128)(2,1)}, bf16[2,512,768]{2,1,0:T(8,128)(2,1)}, bf16[2,512,3072]{2,1,0:T(8,128)...) custom-call(s32[1]{0:T(128)} %bitcast.place_ref, ...), custom_call_target="tpu_custom_call" | custom-call | flops 14495514624 | tf_op jit(solution)/shard_map/tokens_forward/pallas_call | solution.py:413
  231.4 18.4 %collective-permute-done.22 = bf16[512,768]{1,0:T(8,128)(2,1)S(1)} collective-permute-done((bf16[512,768]{1,0:T(8,128)(2,1)S(1)}, bf16[512,768]{1,0:T(8,128)(2,1)S(1)}, u32[]{:S(2)}, u32[]{:S(2)}) %collective-permute-start.22) | collective-permute-done | bytes 786464 | tf_op jit(solution)/shard_map/ppermute | solution.py:44
  249.8 16.2 %collective-permute-done.23 = bf16[512,768]{1,0:T(8,128)(2,1)S(1)} collective-permute-done((bf16[512,768]{1,0:T(8,128)(2,1)S(1)}, bf16[512,768]{1,0:T(8,128)(2,1)S(1)}, u32[]{:S(2)}, u32[]{:S(2)}) %collective-permute-start.23) | collective-permute-done | bytes 786464 | tf_op jit(solution)/shard_map/ppermute | solution.py:44
  268.3 2.6 pad_maximum_fusion.1.p3
  271.1 11.1 %project.3 = (bf16[4096,384]{1,0:T(8,128)(2,1)}, bf16[4096,384]{1,0:T(8,128)(2,1)}, bf16[4096,384]{1,0:T(8,128)(2,1)}) custom-call(bf16[1024,768]{1,0:T(8,128)(2,1)} %bitcast.95, bf16[1024,768]{1,0:T(8,128)(2,1)} %collective-permute-done.21.p1, bf16[1024,768]{1,0:T(8,128)(2,1)} %pad_maximum_fusion.p2, bf16[1024,768]{1,0:T(8,128)(2,1)} %pad_maximum_fusion.1.p3, ...), custom_call_target="tpu_custom_call" | custom-call | flops 10871635968 | tf_op jit(solution)/shard_map/project/pallas_call | solution.py:131
  282.2 72.7 %attention_forward.3 = (bf16[4,512,384]{2,1,0:T(8,128)(2,1)}, bf16[4096,384]{1,0:T(8,128)(2,1)}) custom-call(s32[16]{0:T(128)} %squeeze.83.low_ref, s32[16]{0:T(128)} %squeeze.84.high_ref, s32[1]{0:T(128)} %bitcast.place_ref, bf16[4096,384]{1,0:T(8,128)(2,1)} %get-tuple-element.143.q_ref, bf16[4096,384]{1,0:T(8,128)(2,1)} %get-tuple-element.144.k_ref, ...), custom_call_target="tpu_custom_call" | custom-call | flops 77309411328 | tf_op jit(solution)/shard_map/attention_forward/pallas_call | solution.py:226
  354.9 2.4 slice_bitcast_fusion.2
  361.8 7.6 collective-permute-done.27.c2
  369.5 7.1 collective-permute-done.28.c3
  377.3 26.6 %tokens_forward.3 = (f32[2,512,768]{2,1,0:T(8,128)}, bf16[2,512,768]{2,1,0:T(8,128)(2,1)}, bf16[2,512,768]{2,1,0:T(8,128)(2,1)}, bf16[2,512,3072]{2,1,0:T(8,128)...) custom-call(s32[1]{0:T(128)} %bitcast.place_ref, ...), custom_call_target="tpu_custom_call" | custom-call | flops 14495514624 | tf_op jit(solution)/shard_map/tokens_forward/pallas_call | solution.py:413
  404.0 4.0 fusion.1
  408.0 24.3 %tokens_backward.2 = (bf16[2,512,768]{2,1,0:T(8,128)(2,1)}, bf16[2,512,3072]{2,1,0:T(8,128)(2,1)}, f32[2,512,768]{2,1,0:T(8,128)}, bf16[2,512,768]{2,1,0:T(8,128...) custom-call(s32[1]{0:T(128)} %bitcast.place_ref, ...), custom_call_target="tpu_custom_call" | custom-call | flops 14495514624 | tf_op jit(solution)/shard_map/tokens_backward/pallas_call | solution.py:518
  434.4 18.7 %weight_grads.2 = bf16[4,768,1728]{2,1,0:T(8,128)(2,1)} custom-call(s32[1]{0:T(128)} %bitcast.place_ref, bf16[1024,768]{1,0:T(8,128)(2,1)} %bitcast.132, bf16[1024,3072]{1,0:T(8,128)(2,1)} %bitcast.127, bf16[1024,768]{1,0:T(8,128)(2,1)} %bitcast.133, bf16[1024,3072]{1,0:T(8,128)(2,1)} %bitcast.126, bf16[1024,768]{1,0:T(8,128)(2,1)} %bitcast.134, ...), custom_call_target="tpu_custom_call" | custom-call | flops 14495514624 | tf_op jit(solution)/shard_map/weight_grads/pallas_call | solution.py:567
  454.1 134.2 %attention_backward.2 = (bf16[4096,192]{1,0:T(8,128)(2,1)}, bf16[4096,192]{1,0:T(8,128)(2,1)}, bf16[4096,192]{1,0:T(8,128)(2,1)}) custom-call(s32[16]{0:T(128)} %squeeze.83.low_ref, s32[16]{0:T(128)} %squeeze.84.high_ref, s32[1]{0:T(128)} %bitcast.place_ref, bf16[4096,384]{1,0:T(8,128)(2,1)} %get-tuple-element.157.q_ref, ...), custom_call_target="tpu_custom_call" | custom-call | flops 154618822656 | tf_op jit(solution)/shard_map/attention_backward/pallas_call | solution.py:335
  588.3 11.4 %input_grads.2 = (bf16[1024,768]{1,0:T(8,128)(2,1)}, bf16[1024,768]{1,0:T(8,128)(2,1)}, bf16[1024,768]{1,0:T(8,128)(2,1)}, bf16[1024,768]{1,0:T(8,128)(2,1)}) custom-call(bf16[4096,192]{1,0:T(8,128)(2,1)} %get-tuple-element.171.q_ref, bf16[4096,192]{1,0:T(8,128)(2,1)} %get-tuple-element.172.k_ref, bf16[4096,192]{1,0:T(8,128)(2,1)} %get-tuple-element.173.v_ref, ...), custom_call_target="tpu_custom_call" | custom-call | flops 10871635968 | tf_op jit(solution)/shard_map/input_grads/pallas_call | solution.py:599
  600.5 3.1 collective-permute-done.33
  603.6 3.1 add_convert_fusion.1
  608.2 11.1 %projection_grads.2 = (bf16[768,576]{1,0:T(8,128)(2,1)}, f32[8,192]{1,0:T(8,128)}) custom-call(bf16[1024,768]{1,0:T(8,128)(2,1)} %bitcast.96, bf16[1024,768]{1,0:T(8,128)(2,1)} %collective-permute-done.21.p1, bf16[1024,768]{1,0:T(8,128)(2,1)} %pad_maximum_fusion.p2, bf16[1024,768]{1,0:T(8,128)(2,1)} %pad_maximum_fusion.1.p3, ...), custom_call_target="tpu_custom_call" | custom-call | flops 10871635968 | tf_op jit(solution)/shard_map/projection_grads/pallas_call | solution.py:624
  620.2 2.4 pad_maximum_fusion.2
  622.6 21.0 %collective-permute-done.34 = bf16[1024,768]{1,0:T(8,128)(2,1)} collective-permute-done((bf16[1024,768]{1,0:T(8,128)(2,1)}, bf16[1024,768]{1,0:T(8,128)(2,1)}, u32[]{:S(2)}, u32[]{:S(2)}) %collective-permute-start.34) | collective-permute-done | bytes 1572896 | tf_op jit(solution)/shard_map/ppermute | solution.py:44
  643.7 4.5 bitcast_add_fusion.1
  648.1 1.9 convert_element_type.150
  650.0 11.9 %all-to-all-start = ((bf16[8,112,576]{2,1,0:T(8,128)(2,1)}), bf16[8,112,576]{2,1,0:T(8,128)(2,1)S(1)}, u32[]{:S(2)}, u32[]{:S(2)}) async-start(bf16[8,112,576]{2,1,0:T(8,128)(2,1)} %pad_maximum_fusion.2), calls=%async_computation.1 | async-start | bytes 2293760 | tf_op jit(solution)/shard_map/all_to_all | solution.py:686
  661.9 24.3 %tokens_backward.3 = (bf16[2,512,768]{2,1,0:T(8,128)(2,1)}, bf16[2,512,3072]{2,1,0:T(8,128)(2,1)}, f32[2,512,768]{2,1,0:T(8,128)}, bf16[2,512,768]{2,1,0:T(8,128...) custom-call(s32[1]{0:T(128)} %bitcast.place_ref, ...), custom_call_target="tpu_custom_call" | custom-call | flops 14495514624 | tf_op jit(solution)/shard_map/tokens_backward/pallas_call | solution.py:518
  690.8 18.7 %weight_grads.3 = bf16[4,768,1728]{2,1,0:T(8,128)(2,1)} custom-call(s32[1]{0:T(128)} %bitcast.place_ref, bf16[1024,768]{1,0:T(8,128)(2,1)} %bitcast.129, bf16[1024,3072]{1,0:T(8,128)(2,1)} %bitcast.125, bf16[1024,768]{1,0:T(8,128)(2,1)} %bitcast.130, bf16[1024,3072]{1,0:T(8,128)(2,1)} %bitcast.124, bf16[1024,768]{1,0:T(8,128)(2,1)} %bitcast.131, ...), custom_call_target="tpu_custom_call" | custom-call | flops 14495514624 | tf_op jit(solution)/shard_map/weight_grads/pallas_call | solution.py:567
  711.5 2.0 collective-permute-start.41
  715.0 2.9 collective-permute-start.44
  719.4 3.3 collective-permute-start.46
  722.8 134.3 %attention_backward.3 = (bf16[4096,192]{1,0:T(8,128)(2,1)}, bf16[4096,192]{1,0:T(8,128)(2,1)}, bf16[4096,192]{1,0:T(8,128)(2,1)}) custom-call(s32[16]{0:T(128)} %squeeze.83.low_ref, s32[16]{0:T(128)} %squeeze.84.high_ref, s32[1]{0:T(128)} %bitcast.place_ref, bf16[4096,384]{1,0:T(8,128)(2,1)} %get-tuple-element.188.q_ref, ...), custom_call_target="tpu_custom_call" | custom-call | flops 154618822656 | tf_op jit(solution)/shard_map/attention_backward/pallas_call | solution.py:335
  858.5 11.6 %input_grads.3 = (bf16[1024,768]{1,0:T(8,128)(2,1)}, bf16[1024,768]{1,0:T(8,128)(2,1)}, bf16[1024,768]{1,0:T(8,128)(2,1)}, bf16[1024,768]{1,0:T(8,128)(2,1)}) custom-call(bf16[4096,192]{1,0:T(8,128)(2,1)} %get-tuple-element.211.q_ref, bf16[4096,192]{1,0:T(8,128)(2,1)} %get-tuple-element.212.k_ref, bf16[4096,192]{1,0:T(8,128)(2,1)} %get-tuple-element.213.v_ref, ...), custom_call_target="tpu_custom_call" | custom-call | flops 10871635968 | tf_op jit(solution)/shard_map/input_grads/pallas_call | solution.py:599
  872.6 11.1 %projection_grads.3 = (bf16[768,576]{1,0:T(8,128)(2,1)}, f32[8,192]{1,0:T(8,128)}) custom-call(bf16[1024,768]{1,0:T(8,128)(2,1)} %p0.3, bf16[1024,768]{1,0:T(8,128)(2,1)} %collective-permute-done.p1, bf16[1024,768]{1,0:T(8,128)(2,1)} %copy-done.12, bf16[1024,768]{1,0:T(8,128)(2,1)} %copy-done.11, bf16[4096,192]{1,0:T(8,128)(2,1)} %get-tuple-element.211.q_ref, ...), custom_call_target="tpu_custom_call" | custom-call | flops 10871635968 | tf_op jit(solution)/shard_map/projection_grads/pallas_call | solution.py:624
  885.0 1.9 add_convert_fusion
  890.6 9.5 %all-to-all-start.1 = ((bf16[8,112,576]{2,1,0:T(8,128)(2,1)}), bf16[8,112,576]{2,1,0:T(8,128)(2,1)S(1)}, u32[]{:S(2)}, u32[]{:S(2)}) async-start(bf16[8,112,576]{2,1,0:T(8,128)(2,1)} %pad_maximum_fusion.3), calls=%async_computation.3 | async-start | bytes 2293760 | tf_op jit(solution)/shard_map/all_to_all | solution.py:708
  905.2 18.2 %collective-permute-done.50 = bf16[1024,768]{1,0:T(8,128)(2,1)} collective-permute-done((bf16[1024,768]{1,0:T(8,128)(2,1)S(1)}, bf16[1024,768]{1,0:T(8,128)(2,1)}, u32[]{:S(2)}, u32[]{:S(2)}) %collective-permute-start.50) | collective-permute-done | bytes 1572896 | tf_op jit(solution)/shard_map/ppermute | solution.py:44
  923.4 5.6 bitcast_add_fusion
  (314 shorter events, 81.0 us)
Async XLA Ops:
  7.2 170.5 %all-gather.6.cloned.1.call-start = ((), (), s32[]{:S(2)}) async-start(), calls=%async_computation.4 | async-start | bytes 1327104 | tf_op jit(solution)/shard_map/all_gather | solution.py:777
  9.0 191.5 %all-gather.8.cloned.1.call-start = ((), (), s32[]{:S(2)}) async-start(), calls=%async_computation.7 | async-start | bytes 11354112 | tf_op jit(solution)/shard_map/all_gather | solution.py:643
  11.8 364.8 %all-gather.10.cloned.1.call-start = ((), (), s32[]{:S(2)}) async-start(), calls=%async_computation.8 | async-start | bytes 11354112 | tf_op jit(solution)/shard_map/all_gather | solution.py:643
  13.8 51.5 %collective-permute-start.10 = (f32[8,128]{1,0:T(8,128)S(1)}, f32[8,128]{1,0:T(8,128)S(1)}, u32[]{:S(2)}, u32[]{:S(2)}) collective-permute-start(f32[8,128]{1,0:T(8,128)S(1)} %broadcast_in_dim.51), channel_id=1, source_target_pairs={{0,3},{1,2},{2,1},{3,0},{4,7},{5,6},{6,5},{7,4},{8,11},{9,10},{10,... | collective-permute-start | bytes 12296 | tf_op jit(solution)/shard_map/ppermute | solution.py:73
  16.3 49.1 %collective-permute-start.8 = (f32[8,128]{1,0:T(8,128)S(1)}, f32[8,128]{1,0:T(8,128)S(1)}, u32[]{:S(2)}, u32[]{:S(2)}) collective-permute-start(f32[8,128]{1,0:T(8,128)S(1)} %broadcast_in_dim.51), channel_id=1, source_target_pairs={{0,1},{1,0},{2,3},{3,2},{4,5},{5,4},{6,7},{7,6},{8,9},{9,8},{10,11... | collective-permute-start | bytes 12296 | tf_op jit(solution)/shard_map/ppermute | solution.py:73
  16.9 49.0 %collective-permute-start.9 = (f32[8,128]{1,0:T(8,128)S(1)}, f32[8,128]{1,0:T(8,128)S(1)}, u32[]{:S(2)}, u32[]{:S(2)}) collective-permute-start(f32[8,128]{1,0:T(8,128)S(1)} %broadcast_in_dim.51), channel_id=1, source_target_pairs={{0,2},{1,3},{2,0},{3,1},{4,6},{5,7},{6,4},{7,5},{8,10},{9,11},{10,... | collective-permute-start | bytes 12296 | tf_op jit(solution)/shard_map/ppermute | solution.py:73
  18.2 58.0 %collective-permute-start.1 = (bf16[512,768]{1,0:T(8,128)(2,1)}, bf16[512,768]{1,0:T(8,128)(2,1)S(1)}, u32[]{:S(2)}, u32[]{:S(2)}) collective-permute-start(bf16[512,768]{1,0:T(8,128)(2,1)} %get-tuple-element.315), channel_id=1, source_target_pairs={{0,2},{1,3},{2,0},{3,1},{4,6},{5,7},{6,4},{7,5},{8,10},{9,11},{10,... | collective-permute-start | bytes 2359304 | tf_op jit(solution)/shard_map/ppermute | solution.py:44
  20.2 61.0 %collective-permute-start.2 = (bf16[512,768]{1,0:T(8,128)(2,1)}, bf16[512,768]{1,0:T(8,128)(2,1)S(1)}, u32[]{:S(2)}, u32[]{:S(2)}) collective-permute-start(bf16[512,768]{1,0:T(8,128)(2,1)} %get-tuple-element.314), channel_id=1, source_target_pairs={{0,2},{1,3},{2,0},{3,1},{4,6},{5,7},{6,4},{7,5},{8,10},{9,11},{10,... | collective-permute-start | bytes 2359304 | tf_op jit(solution)/shard_map/ppermute | solution.py:44
  65.3 27.9 %collective-permute-start = (bf16[1024,768]{1,0:T(8,128)(2,1)S(1)}, bf16[1024,768]{1,0:T(8,128)(2,1)}, u32[]{:S(2)}, u32[]{:S(2)}) collective-permute-start(bf16[1024,768]{1,0:T(8,128)(2,1)S(1)} %copy-done.5), channel_id=1, source_target_pairs={{0,1},{1,0},{2,3},{3,2},{4,5},{5,4},{6,7},{7,6},{8,9},{9,8},{10,11... | collective-permute-start | bytes 4718600 | tf_op jit(solution)/shard_map/ppermute | solution.py:44
  68.9 5.3 collective-permute-start.7
  74.2 4.8 collective-permute-start.13
  76.3 16.8 %collective-permute-start.3 = (bf16[512,768]{1,0:T(8,128)(2,1)S(1)}, bf16[512,768]{1,0:T(8,128)(2,1)S(1)}, u32[]{:S(2)}, u32[]{:S(2)}) collective-permute-start(bf16[512,768]{1,0:T(8,128)(2,1)S(1)} %collective-permute-done.1), channel_id=1, source_target_pairs={{0,1},{1,0},{2,3},{3,2},{4,5},{5,4},{6,7},{7,6},{8,9},{9,8},{10,11... | collective-permute-start | bytes 2359304 | tf_op jit(solution)/shard_map/ppermute | solution.py:44
  79.1 5.7 collective-permute-start.15
  81.2 11.8 %collective-permute-start.4 = (bf16[512,768]{1,0:T(8,128)(2,1)S(1)}, bf16[512,768]{1,0:T(8,128)(2,1)S(1)}, u32[]{:S(2)}, u32[]{:S(2)}) collective-permute-start(bf16[512,768]{1,0:T(8,128)(2,1)S(1)} %collective-permute-done.2), channel_id=1, source_target_pairs={{0,1},{1,0},{2,3},{3,2},{4,5},{5,4},{6,7},{7,6},{8,9},{9,8},{10,11... | collective-permute-start | bytes 2359304 | tf_op jit(solution)/shard_map/ppermute | solution.py:44
  82.4 5.4 collective-permute-start.16
  84.8 6.3 collective-permute-start.17
  181.0 12.0 %collective-permute-start.19 = (bf16[512,384]{1,0:T(8,128)(2,1)S(1)}, bf16[512,384]{1,0:T(8,128)(2,1)S(1)}, u32[]{:S(2)}, u32[]{:S(2)}) collective-permute-start(bf16[512,384]{1,0:T(8,128)(2,1)S(1)} %get-tuple-element.311), channel_id=1, source_target_pairs={{0,2},{1,3},{2,0},{3,1},{4,6},{5,7},{6,4},{7,5},{8,10},{9,11},{10,... | collective-permute-start | bytes 1179656 | tf_op jit(solution)/shard_map/ppermute | solution.py:44
  182.5 18.0 %collective-permute-start.20 = (bf16[512,384]{1,0:T(8,128)(2,1)S(1)}, bf16[512,384]{1,0:T(8,128)(2,1)S(1)}, u32[]{:S(2)}, u32[]{:S(2)}) collective-permute-start(bf16[512,384]{1,0:T(8,128)(2,1)S(1)} %get-tuple-element.310), channel_id=1, source_target_pairs={{0,3},{1,2},{2,1},{3,0},{4,7},{5,6},{6,5},{7,4},{8,11},{9,10},{10,... | collective-permute-start | bytes 1179656 | tf_op jit(solution)/shard_map/ppermute | solution.py:44
  229.3 20.5 %collective-permute-start.22 = (bf16[512,768]{1,0:T(8,128)(2,1)S(1)}, bf16[512,768]{1,0:T(8,128)(2,1)S(1)}, u32[]{:S(2)}, u32[]{:S(2)}) collective-permute-start(bf16[512,768]{1,0:T(8,128)(2,1)S(1)} %get-tuple-element.308), channel_id=1, source_target_pairs={{0,2},{1,3},{2,0},{3,1},{4,6},{5,7},{6,4},{7,5},{8,10},{9,11},{10,... | collective-permute-start | bytes 2359304 | tf_op jit(solution)/shard_map/ppermute | solution.py:44
  230.8 35.1 %collective-permute-start.23 = (bf16[512,768]{1,0:T(8,128)(2,1)S(1)}, bf16[512,768]{1,0:T(8,128)(2,1)S(1)}, u32[]{:S(2)}, u32[]{:S(2)}) collective-permute-start(bf16[512,768]{1,0:T(8,128)(2,1)S(1)} %get-tuple-element.309), channel_id=1, source_target_pairs={{0,2},{1,3},{2,0},{3,1},{4,6},{5,7},{6,4},{7,5},{8,10},{9,11},{10,... | collective-permute-start | bytes 2359304 | tf_op jit(solution)/shard_map/ppermute | solution.py:44
  231.4 39.6 %collective-permute-start.21 = (bf16[1024,768]{1,0:T(8,128)(2,1)S(1)}, bf16[1024,768]{1,0:T(8,128)(2,1)}, u32[]{:S(2)}, u32[]{:S(2)}) collective-permute-start(bf16[1024,768]{1,0:T(8,128)(2,1)S(1)} %bitcast.97), channel_id=1, source_target_pairs={{0,1},{1,0},{2,3},{3,2},{4,5},{5,4},{6,7},{7,6},{8,9},{9,8},{10,11... | collective-permute-start | bytes 4718600 | tf_op jit(solution)/shard_map/ppermute | solution.py:44
  249.8 18.3 %collective-permute-start.24 = (bf16[512,768]{1,0:T(8,128)(2,1)S(1)}, bf16[512,768]{1,0:T(8,128)(2,1)}, u32[]{:S(2)}, u32[]{:S(2)}) collective-permute-start(bf16[512,768]{1,0:T(8,128)(2,1)S(1)} %collective-permute-done.22), channel_id=1, source_target_pairs={{0,1},{1,0},{2,3},{3,2},{4,5},{5,4},{6,7},{7,6},{8,9},{9,8},{10,11... | collective-permute-start | bytes 2359304 | tf_op jit(solution)/shard_map/ppermute | solution.py:44
  271.0 377.1 %reduce-scatter.3.cloned.1.call-start = ((), (), s32[]{:S(2)}) async-start(), calls=%async_computation.5 | async-start | bytes 11354112 | tf_op jit(solution)/shard_map/reduce_scatter | solution.py:692
  357.5 12.0 %collective-permute-start.27 = (bf16[512,384]{1,0:T(8,128)(2,1)S(1)}, bf16[512,384]{1,0:T(8,128)(2,1)S(1)}, u32[]{:S(2)}, u32[]{:S(2)}) collective-permute-start(bf16[512,384]{1,0:T(8,128)(2,1)S(1)} %get-tuple-element.305), channel_id=1, source_target_pairs={{0,2},{1,3},{2,0},{3,1},{4,6},{5,7},{6,4},{7,5},{8,10},{9,11},{10,... | collective-permute-start | bytes 1179656 | tf_op jit(solution)/shard_map/ppermute | solution.py:44
  359.0 17.6 %collective-permute-start.28 = (bf16[512,384]{1,0:T(8,128)(2,1)S(1)}, bf16[512,384]{1,0:T(8,128)(2,1)S(1)}, u32[]{:S(2)}, u32[]{:S(2)}) collective-permute-start(bf16[512,384]{1,0:T(8,128)(2,1)S(1)} %get-tuple-element.304), channel_id=1, source_target_pairs={{0,3},{1,2},{2,1},{3,0},{4,7},{5,6},{6,5},{7,4},{8,11},{9,10},{10,... | collective-permute-start | bytes 1179656 | tf_op jit(solution)/shard_map/ppermute | solution.py:44
  432.3 20.8 %collective-permute-start.29 = (bf16[512,384]{1,0:T(8,128)(2,1)}, bf16[512,384]{1,0:T(8,128)(2,1)S(1)}, u32[]{:S(2)}, u32[]{:S(2)}) collective-permute-start(bf16[512,384]{1,0:T(8,128)(2,1)} %get-tuple-element.159), channel_id=1, source_target_pairs={{0,1},{1,0},{2,3},{3,2},{4,5},{5,4},{6,7},{7,6},{8,9},{9,8},{10,11... | collective-permute-start | bytes 1179656 | tf_op jit(solution)/shard_map/ppermute | solution.py:44
  432.9 20.2 %collective-permute-start.30 = (bf16[512,384]{1,0:T(8,128)(2,1)}, bf16[512,384]{1,0:T(8,128)(2,1)S(1)}, u32[]{:S(2)}, u32[]{:S(2)}) collective-permute-start(bf16[512,384]{1,0:T(8,128)(2,1)} %get-tuple-element.160), channel_id=1, source_target_pairs={{0,2},{1,3},{2,0},{3,1},{4,6},{5,7},{6,4},{7,5},{8,10},{9,11},{10,... | collective-permute-start | bytes 1179656 | tf_op jit(solution)/shard_map/ppermute | solution.py:44
  434.4 18.8 %collective-permute-start.31 = (bf16[512,384]{1,0:T(8,128)(2,1)}, bf16[512,384]{1,0:T(8,128)(2,1)S(1)}, u32[]{:S(2)}, u32[]{:S(2)}) collective-permute-start(bf16[512,384]{1,0:T(8,128)(2,1)} %get-tuple-element.161), channel_id=1, source_target_pairs={{0,3},{1,2},{2,1},{3,0},{4,7},{5,6},{6,5},{7,4},{8,11},{9,10},{10,... | collective-permute-start | bytes 1179656 | tf_op jit(solution)/shard_map/ppermute | solution.py:44
  600.5 22.2 %collective-permute-start.32 = (bf16[1024,768]{1,0:T(8,128)(2,1)}, bf16[1024,768]{1,0:T(8,128)(2,1)}, u32[]{:S(2)}, u32[]{:S(2)}) collective-permute-start(bf16[1024,768]{1,0:T(8,128)(2,1)} %get-tuple-element.175), channel_id=1, source_target_pairs={{0,1},{1,0},{2,3},{3,2},{4,5},{5,4},{6,7},{7,6},{8,9},{9,8},{10,11... | collective-permute-start | bytes 4718600 | tf_op jit(solution)/shard_map/ppermute | solution.py:44
  606.7 37.0 %collective-permute-start.34 = (bf16[1024,768]{1,0:T(8,128)(2,1)}, bf16[1024,768]{1,0:T(8,128)(2,1)}, u32[]{:S(2)}, u32[]{:S(2)}) collective-permute-start(bf16[1024,768]{1,0:T(8,128)(2,1)} %add_convert_fusion.1), channel_id=1, source_target_pairs={{0,2},{1,3},{2,0},{3,1},{4,6},{5,7},{6,4},{7,5},{8,10},{9,11},{10,... | collective-permute-start | bytes 4718600 | tf_op jit(solution)/shard_map/ppermute | solution.py:44
  650.0 60.8 %all-to-all-start = ((bf16[8,112,576]{2,1,0:T(8,128)(2,1)}), bf16[8,112,576]{2,1,0:T(8,128)(2,1)S(1)}, u32[]{:S(2)}, u32[]{:S(2)}) async-start(bf16[8,112,576]{2,1,0:T(8,128)(2,1)} %pad_maximum_fusion.2), calls=%async_computation.1 | async-start | bytes 2293760 | tf_op jit(solution)/shard_map/all_to_all | solution.py:686
  661.9 227.7 %reduce-scatter.5.cloned.1.call-start = ((), (), s32[]{:S(2)}) async-start(), calls=%async_computation.6 | async-start | bytes 11354112 | tf_op jit(solution)/shard_map/reduce_scatter | solution.py:692
  687.0 22.4 %collective-permute-start.39 = (f32[32,768]{1,0:T(8,128)S(1)}, f32[32,768]{1,0:T(8,128)S(1)}, u32[]{:S(2)}, u32[]{:S(2)}) collective-permute-start(f32[32,768]{1,0:T(8,128)S(1)} %constant_dynamic-update-slice_fusion.4), channel_id=1, source_target_pairs={{0,2},{1,3},{2,0},{3,1},{4,6},{5,7},{6,4},{7,5},{8,10},{9,11},{10,... | collective-permute-start | bytes 294920 | tf_op jit(solution)/shard_map/ppermute | solution.py:73
  688.5 21.0 %collective-permute-start.40 = (f32[32,768]{1,0:T(8,128)S(1)}, f32[32,768]{1,0:T(8,128)S(1)}, u32[]{:S(2)}, u32[]{:S(2)}) collective-permute-start(f32[32,768]{1,0:T(8,128)S(1)} %constant_dynamic-update-slice_fusion.4), channel_id=1, source_target_pairs={{0,3},{1,2},{2,1},{3,0},{4,7},{5,6},{6,5},{7,4},{8,11},{9,10},{10,... | collective-permute-start | bytes 294920 | tf_op jit(solution)/shard_map/ppermute | solution.py:73
  688.9 20.5 %collective-permute-start.35 = (bf16[512,384]{1,0:T(8,128)(2,1)}, bf16[512,384]{1,0:T(8,128)(2,1)S(1)}, u32[]{:S(2)}, u32[]{:S(2)}) collective-permute-start(bf16[512,384]{1,0:T(8,128)(2,1)} %get-tuple-element.190), channel_id=1, source_target_pairs={{0,1},{1,0},{2,3},{3,2},{4,5},{5,4},{6,7},{7,6},{8,9},{9,8},{10,11... | collective-permute-start | bytes 1179656 | tf_op jit(solution)/shard_map/ppermute | solution.py:44
  689.2 20.3 %collective-permute-start.36 = (bf16[512,384]{1,0:T(8,128)(2,1)}, bf16[512,384]{1,0:T(8,128)(2,1)S(1)}, u32[]{:S(2)}, u32[]{:S(2)}) collective-permute-start(bf16[512,384]{1,0:T(8,128)(2,1)} %get-tuple-element.191), channel_id=1, source_target_pairs={{0,2},{1,3},{2,0},{3,1},{4,6},{5,7},{6,4},{7,5},{8,10},{9,11},{10,... | collective-permute-start | bytes 1179656 | tf_op jit(solution)/shard_map/ppermute | solution.py:44
  690.6 20.1 %collective-permute-start.37 = (bf16[512,384]{1,0:T(8,128)(2,1)}, bf16[512,384]{1,0:T(8,128)(2,1)S(1)}, u32[]{:S(2)}, u32[]{:S(2)}) collective-permute-start(bf16[512,384]{1,0:T(8,128)(2,1)} %get-tuple-element.192), channel_id=1, source_target_pairs={{0,3},{1,2},{2,1},{3,0},{4,7},{5,6},{6,5},{7,4},{8,11},{9,10},{10,... | collective-permute-start | bytes 1179656 | tf_op jit(solution)/shard_map/ppermute | solution.py:44
  711.5 7.9 collective-permute-start.41
  713.4 9.3 collective-permute-start.42
  714.9 142.3 %collective-permute-start.43 = (f32[32,768]{1,0:T(8,128)}, f32[32,768]{1,0:T(8,128)}, u32[]{:S(2)}, u32[]{:S(2)}) collective-permute-start(f32[32,768]{1,0:T(8,128)} %add_add_fusion.1), channel_id=1, source_target_pairs={{0,12},{4,8},{8,4},{12,0},{16,28},{20,24},{24,20},{28,16},{1,13},{... | collective-permute-start | bytes 294920 | tf_op jit(solution)/shard_map/ppermute | solution.py:73
  715.0 142.2 %collective-permute-start.44 = (f32[32,768]{1,0:T(8,128)}, f32[32,768]{1,0:T(8,128)}, u32[]{:S(2)}, u32[]{:S(2)}) collective-permute-start(f32[32,768]{1,0:T(8,128)} %add_add_fusion.1), channel_id=1, source_target_pairs={{0,16},{4,20},{8,24},{12,28},{16,0},{20,4},{24,8},{28,12},{1,17},{... | collective-permute-start | bytes 294920 | tf_op jit(solution)/shard_map/ppermute | solution.py:73
  717.8 139.3 %collective-permute-start.45 = (f32[32,768]{1,0:T(8,128)}, f32[32,768]{1,0:T(8,128)}, u32[]{:S(2)}, u32[]{:S(2)}) collective-permute-start(f32[32,768]{1,0:T(8,128)} %add_add_fusion.1), channel_id=1, source_target_pairs={{0,20},{4,16},{8,28},{12,24},{16,4},{20,0},{24,12},{28,8},{1,21},{... | collective-permute-start | bytes 294920 | tf_op jit(solution)/shard_map/ppermute | solution.py:73
  719.4 137.8 %collective-permute-start.46 = (f32[32,768]{1,0:T(8,128)}, f32[32,768]{1,0:T(8,128)}, u32[]{:S(2)}, u32[]{:S(2)}) collective-permute-start(f32[32,768]{1,0:T(8,128)} %add_add_fusion.1), channel_id=1, source_target_pairs={{0,24},{4,28},{8,16},{12,20},{16,8},{20,12},{24,0},{28,4},{1,25},{... | collective-permute-start | bytes 294920 | tf_op jit(solution)/shard_map/ppermute | solution.py:73
  722.7 134.5 %collective-permute-start.47 = (f32[32,768]{1,0:T(8,128)}, f32[32,768]{1,0:T(8,128)}, u32[]{:S(2)}, u32[]{:S(2)}) collective-permute-start(f32[32,768]{1,0:T(8,128)} %add_add_fusion.1), channel_id=1, source_target_pairs={{0,28},{4,24},{8,20},{12,16},{16,12},{20,8},{24,4},{28,0},{1,29},{... | collective-permute-start | bytes 294920 | tf_op jit(solution)/shard_map/ppermute | solution.py:73
  870.1 15.0 %collective-permute-start.49 = (bf16[1024,768]{1,0:T(8,128)(2,1)}, bf16[1024,768]{1,0:T(8,128)(2,1)}, u32[]{:S(2)}, u32[]{:S(2)}) collective-permute-start(bf16[1024,768]{1,0:T(8,128)(2,1)} %get-tuple-element.217), channel_id=1, source_target_pairs={{0,1},{1,0},{2,3},{3,2},{4,5},{5,4},{6,7},{7,6},{8,9},{9,8},{10,11... | collective-permute-start | bytes 4718600 | tf_op jit(solution)/shard_map/ppermute | solution.py:44
  884.5 20.7 %collective-permute-start.48 = (bf16[1024,768]{1,0:T(8,128)(2,1)}, bf16[1024,768]{1,0:T(8,128)(2,1)}, u32[]{:S(2)}, u32[]{:S(2)}) collective-permute-start(bf16[1024,768]{1,0:T(8,128)(2,1)} %get-tuple-element.215), channel_id=1, source_target_pairs={{0,1},{1,0},{2,3},{3,2},{4,5},{5,4},{6,7},{7,6},{8,9},{9,8},{10,11... | collective-permute-start | bytes 4718600 | tf_op jit(solution)/shard_map/ppermute | solution.py:44
  886.9 36.5 %collective-permute-start.50 = (bf16[1024,768]{1,0:T(8,128)(2,1)S(1)}, bf16[1024,768]{1,0:T(8,128)(2,1)}, u32[]{:S(2)}, u32[]{:S(2)}) collective-permute-start(bf16[1024,768]{1,0:T(8,128)(2,1)S(1)} %add_convert_fusion), channel_id=1, source_target_pairs={{0,2},{1,3},{2,0},{3,1},{4,6},{5,7},{6,4},{7,5},{8,10},{9,11},{10,... | collective-permute-start | bytes 4718600 | tf_op jit(solution)/shard_map/ppermute | solution.py:44
  890.6 40.0 %all-to-all-start.1 = ((bf16[8,112,576]{2,1,0:T(8,128)(2,1)}), bf16[8,112,576]{2,1,0:T(8,128)(2,1)S(1)}, u32[]{:S(2)}, u32[]{:S(2)}) async-start(bf16[8,112,576]{2,1,0:T(8,128)(2,1)} %pad_maximum_fusion.3), calls=%async_computation.3 | async-start | bytes 2293760 | tf_op jit(solution)/shard_map/all_to_all | solution.py:708
  (62 other events, 804.6 us)
Sparse Core Ops, SparseCore 0:
  10.8 50.8 all-gather.5
  64.7 87.4 all-gather.7
  271.1 89.4 all-gather.9
  453.3 147.1 reduce-scatter.2
  719.4 143.9 reduce-scatter.4

commit v3 on v2

--- a/solution.py
+++ b/solution.py
@@ -149,67 +149,65 @@
     half_blocks = half // TILE
     group = heads * HEAD_DIM
 
-    def body(
-        low_ref, high_ref, place_ref, q_ref, k_ref, v_ref, ctx_ref, ql_ref, score, peak, total
-    ):
+    def body(low_ref, high_ref, place_ref, q_ref, k_ref, v_ref, ctx_ref, ql_ref, *scratch):
+        peak, fade, total, score = scratch
         block = pl.program_id(0)
         own = place_ref[0]
         first = low_ref[block]
         last = high_ref[block]
         peak[...] = jnp.full_like(peak, -3e38)
         total[...] = jnp.zeros_like(total)
-        q_heads = [q_ref[:, h * LANES : (h + 1) * LANES] for h in range(heads)]
 
         def where_is(j):
             spot = ((j // per_chunk) ^ own) * per_chunk + j % per_chunk
             return pl.multiple_of(spot * TILE, TILE)
 
-        def score_step(j, carry):
+        def rows_step(j):
             at = where_is(j)
             for h in range(heads):
-                s = dot_nt(q_heads[h], k_ref[pl.ds(at, TILE), h * LANES : (h + 1) * LANES])
-                score[h, j - first] = s
-                top = s[:, 0:LANES]
-                for c in range(1, TILE // LANES):
-                    top = jnp.maximum(top, s[:, c * LANES : (c + 1) * LANES])
-                peak[h] = jnp.maximum(peak[h], top)
-            return carry
-
-        lax.fori_loop(first, last, score_step, 0)
-        tops = []
-        for h in range(heads):
-            top = jnp.max(peak[h], axis=1, keepdims=True)
-            tops.append(top)
-            peak[h] = jnp.broadcast_to(top, (TILE, LANES))
-
-        def sum_step(j, carry):
+                to = slice(h * LANES, (h + 1) * LANES)
+                s = dot_nt(k_ref[pl.ds(at, TILE), to], q_ref[:, to])
+                old = peak[h, 0:1, :]
+                top = jnp.maximum(old, jnp.max(s, axis=0, keepdims=True))
+                peak[h, 0:1, :] = top
+                fade[h, 0:1, :] = jnp.exp(old - top)
+                score[h] = s
+
+        def sum_step(j):
             at = where_is(j)
             for h in range(heads):
-                top = peak[h]
-                parts = [
-                    jnp.exp(score[h, j - first, :, c * LANES : (c + 1) * LANES] - top)
-                    for c in range(TILE // LANES)
-                ]
-                p = jnp.concatenate(parts, axis=1).astype(bf16)
-                total[h] += dot_nn(p, v_ref[pl.ds(at, TILE), h * LANES : (h + 1) * LANES])
+                v = v_ref[pl.ds(at, TILE), h * LANES : (h + 1) * LANES]
+                p = jnp.exp(score[h] - peak[h, 0:1, :]).astype(bf16)
+                total[h] = total[h] * fade[h, 0:1, :] + dot_tn(v, p)
+
+        def step(j, carry):
+            sum_step(j - 1)
+            rows_step(j)
             return carry
 
-        lax.fori_loop(first, last, sum_step, 0)
+        rows_step(first)
+        lax.fori_loop(first + 1, last, step, 0)
+        sum_step(last - 1)
+        feature = lax.broadcasted_iota(jnp.int32, (LANES, TILE), 0)
         lane = lax.broadcasted_iota(jnp.int32, (TILE, LANES), 1)
+        mark = HEAD_DIM + SEGMENTS
         outs = []
         for h in range(heads):
             acc = total[h]
-            norm = acc[:, HEAD_DIM : HEAD_DIM + 1]
-            outs.append((acc[:, 0:HEAD_DIM] * (1.0 / norm)).astype(bf16))
-            shift = -(tops[h] + jnp.log(norm))
+            norm = acc[HEAD_DIM : HEAD_DIM + 1, :]
+            shift = -(peak[h, 0:1, :] + jnp.log(norm))
             one = shift.astype(bf16).astype(f32)
             two = (shift - one).astype(bf16).astype(f32)
             three = shift - one - two
-            q = q_heads[h].astype(f32)
-            q = jnp.where(lane == HEAD_DIM + SEGMENTS, one, q)
-            q = jnp.where(lane == HEAD_DIM + SEGMENTS + 1, two, q)
-            q = jnp.where(lane == HEAD_DIM + SEGMENTS + 2, three, q)
-            ql_ref[:, h * LANES : (h + 1) * LANES] = q.astype(bf16)
+            both = acc * (1.0 / norm)
+            both = jnp.where(feature == mark, one, both)
+            both = jnp.where(feature == mark + 1, two, both)
+            both = jnp.where(feature == mark + 2, three, both)
+            both = both.T.astype(bf16)
+            outs.append(both[:, 0:HEAD_DIM])
+            to = slice(h * LANES, (h + 1) * LANES)
+            inside = (lane >= mark) & (lane < mark + 3)
+            ql_ref[:, to] = jnp.where(inside, both, q_ref[:, to])
         ctx = jnp.concatenate(outs, axis=1)
         inside = block % per_chunk
         at = pl.multiple_of((inside % half_blocks) * TILE, TILE)
@@ -234,9 +232,10 @@
                 row_spec,
             ],
             scratch_shapes=[
-                pltpu.VMEM((heads, count, TILE, TILE), f32),
-                pltpu.VMEM((heads, TILE, LANES), f32),
-                pltpu.VMEM((heads, TILE, LANES), f32),
+                pltpu.VMEM((heads, 8, TILE), f32),
+                pltpu.VMEM((heads, 8, TILE), f32),
+                pltpu.VMEM((heads, LANES, TILE), f32),
+                pltpu.VMEM((heads, TILE, TILE), f32),
             ],
         ),
         out_shape=[
@@ -259,7 +258,7 @@
     group = heads * HEAD_DIM
 
     def body(low_ref, high_ref, place_ref, q_ref, k_ref, v_ref, c_ref, g0, g1, g2, g3, *rest):
-        dq_ref, dk_ref, dv_ref, do_all, dq_all, acc_k, acc_v = rest
+        dq_ref, dk_ref, dv_ref, do_all, dq_all, acc_k, acc_v, prob, slope = rest
         block = pl.program_id(0)
         own = place_ref[0]
         first = low_ref[block]
@@ -295,22 +294,36 @@
         acc_k[...] = jnp.zeros_like(acc_k)
         acc_v[...] = jnp.zeros_like(acc_v)
 
-        def step(j, carry):
+        def where_is(j):
             spot = ((j // per_chunk) ^ own) * per_chunk + j % per_chunk
-            at = pl.multiple_of(spot * TILE, TILE)
+            return pl.multiple_of(spot * TILE, TILE)
+
+        def rows_step(j):
+            at = where_is(j)
             for h in range(heads):
                 to = slice(h * LANES, (h + 1) * LANES)
-                q = q_ref[pl.ds(at, TILE), to]
-                k = k_ref[:, to]
-                do = do_all[pl.ds(at, TILE), to]
-                p = jnp.exp(dot_nt(k, q))
-                ds = (p * dot_nt(v_ref[:, to], do)).astype(bf16)
-                acc_v[h] += dot_nn(p.astype(bf16), do)
-                acc_k[h] += dot_nn(ds, q)
-                dq_all[pl.ds(at, TILE), to] += dot_tn(ds, k)
+                p = jnp.exp(dot_nt(k_ref[:, to], q_ref[pl.ds(at, TILE), to]))
+                dp = dot_nt(v_ref[:, to], do_all[pl.ds(at, TILE), to])
+                prob[h] = p.astype(bf16)
+                slope[h] = (p * dp).astype(bf16)
+
+        def grad_step(j):
+            at = where_is(j)
+            for h in range(heads):
+                to = slice(h * LANES, (h + 1) * LANES)
+                ds = slope[h]
+                acc_v[h] += dot_nn(prob[h], do_all[pl.ds(at, TILE), to])
+                acc_k[h] += dot_nn(ds, q_ref[pl.ds(at, TILE), to])
+                dq_all[at // TILE, h] += dot_tn(k_ref[:, to], ds)
+
+        def step(j, carry):
+            grad_step(j - 1)
+            rows_step(j)
             return carry
 
-        lax.fori_loop(first, last, step, 0)
+        rows_step(first)
+        lax.fori_loop(first + 1, last, step, 0)
+        grad_step(last - 1)
         dk = [acc_k[h, :, 0:HEAD_DIM] for h in range(heads)]
         dv = [acc_v[h, :, 0:HEAD_DIM] for h in range(heads)]
         dk_ref[...] = jnp.concatenate(dk, axis=1).astype(bf16)
@@ -320,10 +333,8 @@
         def _():
             def finish(b, carry):
                 at = pl.multiple_of(b * TILE, TILE)
-                dq = [
-                    dq_all[pl.ds(at, TILE), h * LANES : h * LANES + HEAD_DIM] for h in range(heads)
-                ]
-                dq = jnp.concatenate(dq, axis=1) * HEAD_DIM ** (-0.5)
+                dq = [dq_all[b, h, 0:HEAD_DIM, :] for h in range(heads)]
+                dq = jnp.concatenate(dq, axis=0).T * HEAD_DIM ** (-0.5)
                 dq_ref[pl.ds(at, TILE), :] = dq.astype(bf16)
                 return carry
 
@@ -341,9 +352,11 @@
             out_specs=[WHOLE, out_spec, out_spec],
             scratch_shapes=[
                 pltpu.VMEM((rows, wide), bf16),
-                pltpu.VMEM((rows, wide), f32),
+                pltpu.VMEM((count, heads, LANES, TILE), f32),
                 pltpu.VMEM((heads, TILE, LANES), f32),
                 pltpu.VMEM((heads, TILE, LANES), f32),
+                pltpu.VMEM((heads, TILE, TILE), bf16),
+                pltpu.VMEM((heads, TILE, TILE), bf16),
             ],
         ),
         out_shape=[out] * 3,
@@ -781,12 +794,10 @@
 
     mask_rows = valid_mask.astype(f32)
     valid_total = jnp.full((8, LANES), jnp.sum(mask_rows), f32)
-    valid_total = sum_over(sum_over(valid_total, "tensor"), "dp")
-    ask_matrix, up_all, valid_total = tie(ask_matrix, up_all, valid_total)
-    valid_total = valid_total[0, 0]
+    valid_around = send_around(valid_total, "tensor", 1, 4)
     all_rows = rows * lax.axis_size("dp") * lax.axis_size("tensor")
 
-    middle, middle_low, ask_saved, doc_matrix = layer_forward(
+    middle, middle_low, ask_saved, (doc_matrix, valid_around) = layer_forward(
         tokens,
         gather_chunks(tokens),
         context,
@@ -794,13 +805,22 @@
         ask_matrix,
         ask_weights,
         up_all[:, 0],
-        doc_matrix,
-    )
+        (doc_matrix, valid_around),
+    )
+    valid_total = sum_over(add_up(valid_total, valid_around), "dp")
     doc_chunks, doc_pack = tie(gather_chunks(middle_low), pack_local(doc_params))
     doc_weights = gather_all(doc_pack)
-    final, final_low, doc_saved, _ = layer_forward(
-        middle, doc_chunks, context, doc_params, doc_matrix, doc_weights, up_all[:, 1]
-    )
+    final, final_low, doc_saved, valid_total = layer_forward(
+        middle,
+        doc_chunks,
+        context,
+        doc_params,
+        doc_matrix,
+        doc_weights,
+        up_all[:, 1],
+        valid_total,
+    )
+    valid_total = valid_total[0, 0]
     grad_final = mask_rows[:, None] * (final - teacher.astype(f32)) * (all_rows / valid_total)
     grad_middle, doc_wide, pending = layer_backward(
         grad_final, context, doc_matrix, doc_weights, doc_saved

time: 952 us -> 822 us (0.86)
  Pallas kernels: 620 us -> 481 us
  waiting for transfers between devices: 117 us -> 143 us
  starting transfers between devices: 68.8 us -> 54.5 us
    pallas_call x2, Pallas kernels: 269 us -> 171 us  [attention_backward(): pl.pallas_call(body, grid_spec=pltpu.PrefetchScalarGridSpec(num_scalar_pr...]
    pallas_call x2, Pallas kernels: 145 us -> 103 us  [attention_forward(): pl.pallas_call(body, grid_spec=pltpu.PrefetchScalarGridSpec(num_scalar_pr...]
    reduce_scatter x2, waiting for transfers between devices: 0.01 us -> 25.2 us  [layer_backward(): lax.psum_scatter(packed.reshape(4 * width, -1), ('tensor', 'dp'), scatter...]
    all_to_all x1, waiting for transfers between devices: 0.01 us -> 11.4 us  [layer_backward(): both = lax.all_to_all(both, 'dp', 0, 0, tiled=True)]
  transfers between devices with their start and end apart: 58 -> 58, of which waited for: 17 -> 16; matrix products, arithmetic and copies ran while one was open for 7% -> 8% of each run, Pallas kernels for 58% -> 50%
where the time goes in v3:
time: 822 us; the launch traced here: 810 us
  Pallas kernels  481 us (59%)
  waiting for transfers between devices  143 us (17%)
  starting transfers between devices  54.5 us (7%)
  other arithmetic  45.1 us (5%)
  blocking collectives  37.8 us (5%)
  local copies, waits for them, and re-layouts  32.8 us (4%)
  between operations  16 us (2%)
    pallas_call x2, Pallas kernels, attention_backward(): pl.pallas_call(body, grid_spec=pltpu.PrefetchScalarGridSpec(num_scalar_pr...  171 us
    pallas_call x2, Pallas kernels, attention_forward(): pl.pallas_call(body, grid_spec=pltpu.PrefetchScalarGridSpec(num_scalar_pr...  103 us
    ppermute x31, waiting for transfers between devices, flip(): return lax.ppermute(values, 'tensor', [(i, i ^ bit) for i in range(size)])  101 us
    pallas_call x2, Pallas kernels, tokens_forward(): pl.pallas_call(body, grid_spec=pltpu.PrefetchScalarGridSpec(num_scalar_pr...  53 us
    pallas_call x2, Pallas kernels, tokens_backward(): pl.pallas_call(body, grid_spec=pltpu.PrefetchScalarGridSpec(num_scalar_pr...  48.6 us
    pallas_call x2, Pallas kernels, weight_grads(): pl.pallas_call(body, grid_spec=pltpu.PrefetchScalarGridSpec(num_scalar_pr...  38 us
    all_gather x1, blocking collectives, on_device(): lax.all_gather(jnp.concatenate(ask_params[0:3], axis=1), 'dp', axis=0, ti...  37.8 us
    ppermute x20, starting transfers between devices, send_around(): lax.ppermute(values, axis, [(i, i ^ step * r) for i in range(size)])  26.5 us
  transfers between devices with their start and end apart: 58, of which 16 were waited for; matrix products, arithmetic and copies ran while one was open for 8% of the time, Pallas kernels for 50%

profile of v3, /device:TPU:0, one launch (start us, length us, event | category | flops | bytes accessed | tf_op | source)
XLA Modules:
  0.0 810.1 jit_solution(11023517970164769796)
XLA Ops:
  13.7 2.6 collective-permute-start.12
  26.2 37.8 %all_gather.18.mat = bf16[768,576]{1,0:T(8,128)(2,1)} all-gather(bf16[96,576]{1,0:T(8,128)(2,1)S(1)} %pad_maximum_fusion.6), channel_id=1, replica_groups=mesh['dp'=8,'tensor'=4] {'dp'}, dimensions={0}, use_global_device_ids=true | all-gather | bytes 995328 | tf_op jit(solution)/shard_map/all_gather | solution.py:783
  69.3 2.0 collective-permute-start.6
  74.0 10.7 %project.2 = (bf16[4096,384]{1,0:T(8,128)(2,1)}, bf16[4096,384]{1,0:T(8,128)(2,1)}, bf16[4096,384]{1,0:T(8,128)(2,1)}) custom-call(bf16[1024,768]{1,0:T(8,128)(2,1)} %p0.3, bf16[1024,768]{1,0:T(8,128)(2,1)} %collective-permute-done.p1, bf16[1024,768]{1,0:T(8,128)(2,1)} %copy-done.12, bf16[1024,768]{1,0:T(8,128)(2,1)} %copy-done.11, ...), custom_call_target="tpu_custom_call" | custom-call | flops 10871635968 | tf_op jit(solution)/shard_map/project/pallas_call | solution.py:131
  84.7 51.3 %attention_forward.2 = (bf16[4,512,384]{2,1,0:T(8,128)(2,1)}, bf16[4096,384]{1,0:T(8,128)(2,1)}) custom-call(s32[16]{0:T(128)} %squeeze.83.low_ref, s32[16]{0:T(128)} %squeeze.84.high_ref, s32[1]{0:T(128)} %bitcast.place_ref, bf16[4096,384]{1,0:T(8,128)(2,1)} %get-tuple-element.131.q_ref, bf16[4096,384]{1,0:T(8,128)(2,1)} %get-tuple-element.132.k_ref, ...), custom_call_target="tpu_custom_call" | custom-call | flops 77309411328 | tf_op jit(solution)/shard_map/attention_forward/pallas_call | solution.py:224
  136.0 2.3 slice.266.mat
  142.1 8.4 %collective-permute-done.10.c3 = bf16[512,384]{1,0:T(8,128)(2,1)S(1)} collective-permute-done((bf16[512,384]{1,0:T(8,128)(2,1)S(1)}, bf16[512,384]{1,0:T(8,128)(2,1)S(1)}, u32[]{:S(2)}, u32[]{:S(2)}) %collective-permute-start.10) | collective-permute-done | bytes 393248 | tf_op jit(solution)/shard_map/ppermute | solution.py:44
  150.5 8.6 %collective-permute-done.9.c2 = bf16[512,384]{1,0:T(8,128)(2,1)S(1)} collective-permute-done((bf16[512,384]{1,0:T(8,128)(2,1)S(1)}, bf16[512,384]{1,0:T(8,128)(2,1)S(1)}, u32[]{:S(2)}, u32[]{:S(2)}) %collective-permute-start.9) | collective-permute-done | bytes 393248 | tf_op jit(solution)/shard_map/ppermute | solution.py:44
  159.9 26.4 %tokens_forward.2 = (f32[2,512,768]{2,1,0:T(8,128)}, bf16[2,512,768]{2,1,0:T(8,128)(2,1)}, bf16[2,512,768]{2,1,0:T(8,128)(2,1)}, bf16[2,512,3072]{2,1,0:T(8,128)...) custom-call(s32[1]{0:T(128)} %bitcast.place_ref, ...), custom_call_target="tpu_custom_call" | custom-call | flops 14495514624 | tf_op jit(solution)/shard_map/tokens_forward/pallas_call | solution.py:426
  190.0 18.4 %collective-permute-done.15 = bf16[512,768]{1,0:T(8,128)(2,1)S(1)} collective-permute-done((bf16[512,768]{1,0:T(8,128)(2,1)S(1)}, bf16[512,768]{1,0:T(8,128)(2,1)S(1)}, u32[]{:S(2)}, u32[]{:S(2)}) %collective-permute-start.15) | collective-permute-done | bytes 786464 | tf_op jit(solution)/shard_map/ppermute | solution.py:44
  208.4 15.6 %collective-permute-done.16 = bf16[512,768]{1,0:T(8,128)(2,1)S(1)} collective-permute-done((bf16[512,768]{1,0:T(8,128)(2,1)S(1)}, bf16[512,768]{1,0:T(8,128)(2,1)S(1)}, u32[]{:S(2)}, u32[]{:S(2)}) %collective-permute-start.16) | collective-permute-done | bytes 786464 | tf_op jit(solution)/shard_map/ppermute | solution.py:44
  226.4 2.6 pad_maximum_fusion.1.p3
  230.9 2.5 collective-permute-start.21
  235.8 3.5 collective-permute-start.24
  241.3 4.4 collective-permute-done.25
  245.7 11.2 %project.3 = (bf16[4096,384]{1,0:T(8,128)(2,1)}, bf16[4096,384]{1,0:T(8,128)(2,1)}, bf16[4096,384]{1,0:T(8,128)(2,1)}) custom-call(bf16[1024,768]{1,0:T(8,128)(2,1)} %bitcast.95, bf16[1024,768]{1,0:T(8,128)(2,1)} %collective-permute-done.14.p1, bf16[1024,768]{1,0:T(8,128)(2,1)} %pad_maximum_fusion.p2, bf16[1024,768]{1,0:T(8,128)(2,1)} %pad_maximum_fusion.1.p3, ...), custom_call_target="tpu_custom_call" | custom-call | flops 10871635968 | tf_op jit(solution)/shard_map/project/pallas_call | solution.py:131
  256.9 51.3 %attention_forward.3 = (bf16[4,512,384]{2,1,0:T(8,128)(2,1)}, bf16[4096,384]{1,0:T(8,128)(2,1)}) custom-call(s32[16]{0:T(128)} %squeeze.83.low_ref, s32[16]{0:T(128)} %squeeze.84.high_ref, s32[1]{0:T(128)} %bitcast.place_ref, bf16[4096,384]{1,0:T(8,128)(2,1)} %get-tuple-element.143.q_ref, bf16[4096,384]{1,0:T(8,128)(2,1)} %get-tuple-element.144.k_ref, ...), custom_call_target="tpu_custom_call" | custom-call | flops 77309411328 | tf_op jit(solution)/shard_map/attention_forward/pallas_call | solution.py:224
  308.3 2.3 slice_bitcast_fusion.2
  314.5 8.1 %collective-permute-done.27.c2 = bf16[512,384]{1,0:T(8,128)(2,1)S(1)} collective-permute-done((bf16[512,384]{1,0:T(8,128)(2,1)S(1)}, bf16[512,384]{1,0:T(8,128)(2,1)S(1)}, u32[]{:S(2)}, u32[]{:S(2)}) %collective-permute-start.27) | collective-permute-done | bytes 393248 | tf_op jit(solution)/shard_map/ppermute | solution.py:44
  322.6 7.5 collective-permute-done.28.c3
  330.8 26.7 %tokens_forward.3 = (f32[2,512,768]{2,1,0:T(8,128)}, bf16[2,512,768]{2,1,0:T(8,128)(2,1)}, bf16[2,512,768]{2,1,0:T(8,128)(2,1)}, bf16[2,512,3072]{2,1,0:T(8,128)...) custom-call(s32[1]{0:T(128)} %bitcast.place_ref, ...), custom_call_target="tpu_custom_call" | custom-call | flops 14495514624 | tf_op jit(solution)/shard_map/tokens_forward/pallas_call | solution.py:426
  357.5 4.0 fusion.1
  361.5 24.3 %tokens_backward.2 = (bf16[2,512,768]{2,1,0:T(8,128)(2,1)}, bf16[2,512,3072]{2,1,0:T(8,128)(2,1)}, f32[2,512,768]{2,1,0:T(8,128)}, bf16[2,512,768]{2,1,0:T(8,128...) custom-call(s32[1]{0:T(128)} %bitcast.place_ref, ...), custom_call_target="tpu_custom_call" | custom-call | flops 14495514624 | tf_op jit(solution)/shard_map/tokens_backward/pallas_call | solution.py:531
  387.8 19.0 %weight_grads.2 = bf16[4,768,1728]{2,1,0:T(8,128)(2,1)} custom-call(s32[1]{0:T(128)} %bitcast.place_ref, bf16[1024,768]{1,0:T(8,128)(2,1)} %bitcast.132, bf16[1024,3072]{1,0:T(8,128)(2,1)} %bitcast.127, bf16[1024,768]{1,0:T(8,128)(2,1)} %bitcast.133, bf16[1024,3072]{1,0:T(8,128)(2,1)} %bitcast.126, bf16[1024,768]{1,0:T(8,128)(2,1)} %bitcast.134, ...), custom_call_target="tpu_custom_call" | custom-call | flops 14495514624 | tf_op jit(solution)/shard_map/weight_grads/pallas_call | solution.py:580
  407.8 85.6 %attention_backward.2 = (bf16[4096,192]{1,0:T(8,128)(2,1)}, bf16[4096,192]{1,0:T(8,128)(2,1)}, bf16[4096,192]{1,0:T(8,128)(2,1)}) custom-call(s32[16]{0:T(128)} %squeeze.83.low_ref, s32[16]{0:T(128)} %squeeze.84.high_ref, s32[1]{0:T(128)} %bitcast.place_ref, bf16[4096,384]{1,0:T(8,128)(2,1)} %get-tuple-element.161.q_ref, ...), custom_call_target="tpu_custom_call" | custom-call | flops 154618822656 | tf_op jit(solution)/shard_map/attention_backward/pallas_call | solution.py:346
  493.3 11.8 %input_grads.2 = (bf16[1024,768]{1,0:T(8,128)(2,1)}, bf16[1024,768]{1,0:T(8,128)(2,1)}, bf16[1024,768]{1,0:T(8,128)(2,1)}, bf16[1024,768]{1,0:T(8,128)(2,1)}) custom-call(bf16[4096,192]{1,0:T(8,128)(2,1)} %get-tuple-element.175.q_ref, bf16[4096,192]{1,0:T(8,128)(2,1)} %get-tuple-element.176.k_ref, bf16[4096,192]{1,0:T(8,128)(2,1)} %get-tuple-element.177.v_ref, ...), custom_call_target="tpu_custom_call" | custom-call | flops 10871635968 | tf_op jit(solution)/shard_map/input_grads/pallas_call | solution.py:612
  506.0 3.1 collective-permute-done.33
  509.1 3.1 add_convert_fusion.1
  513.6 11.2 %projection_grads.2 = (bf16[768,576]{1,0:T(8,128)(2,1)}, f32[8,192]{1,0:T(8,128)}) custom-call(bf16[1024,768]{1,0:T(8,128)(2,1)} %bitcast.96, bf16[1024,768]{1,0:T(8,128)(2,1)} %collective-permute-done.14.p1, bf16[1024,768]{1,0:T(8,128)(2,1)} %pad_maximum_fusion.p2, bf16[1024,768]{1,0:T(8,128)(2,1)} %pad_maximum_fusion.1.p3, ...), custom_call_target="tpu_custom_call" | custom-call | flops 10871635968 | tf_op jit(solution)/shard_map/projection_grads/pallas_call | solution.py:637
  525.7 2.4 pad_maximum_fusion.2
  528.2 27.5 %collective-permute-done.34 = bf16[1024,768]{1,0:T(8,128)(2,1)} collective-permute-done((bf16[1024,768]{1,0:T(8,128)(2,1)}, bf16[1024,768]{1,0:T(8,128)(2,1)}, u32[]{:S(2)}, u32[]{:S(2)}) %collective-permute-start.34) | collective-permute-done | bytes 1572896 | tf_op jit(solution)/shard_map/ppermute | solution.py:44
  555.7 4.5 bitcast_add_fusion.1
  561.2 1.9 convert_element_type.150
  563.1 4.5 all-to-all-start
  567.6 24.3 %tokens_backward.3 = (bf16[2,512,768]{2,1,0:T(8,128)(2,1)}, bf16[2,512,3072]{2,1,0:T(8,128)(2,1)}, f32[2,512,768]{2,1,0:T(8,128)}, bf16[2,512,768]{2,1,0:T(8,128...) custom-call(s32[1]{0:T(128)} %bitcast.place_ref, ...), custom_call_target="tpu_custom_call" | custom-call | flops 14495514624 | tf_op jit(solution)/shard_map/tokens_backward/pallas_call | solution.py:531
  596.4 19.0 %weight_grads.3 = bf16[4,768,1728]{2,1,0:T(8,128)(2,1)} custom-call(s32[1]{0:T(128)} %bitcast.place_ref, bf16[1024,768]{1,0:T(8,128)(2,1)} %bitcast.129, bf16[1024,3072]{1,0:T(8,128)(2,1)} %bitcast.125, bf16[1024,768]{1,0:T(8,128)(2,1)} %bitcast.130, bf16[1024,3072]{1,0:T(8,128)(2,1)} %bitcast.124, bf16[1024,768]{1,0:T(8,128)(2,1)} %bitcast.131, ...), custom_call_target="tpu_custom_call" | custom-call | flops 14495514624 | tf_op jit(solution)/shard_map/weight_grads/pallas_call | solution.py:580
  617.1 2.0 collective-permute-start.41
  620.6 2.9 collective-permute-start.44
  625.0 3.3 collective-permute-start.46
  628.5 85.6 %attention_backward.3 = (bf16[4096,192]{1,0:T(8,128)(2,1)}, bf16[4096,192]{1,0:T(8,128)(2,1)}, bf16[4096,192]{1,0:T(8,128)(2,1)}) custom-call(s32[16]{0:T(128)} %squeeze.83.low_ref, s32[16]{0:T(128)} %squeeze.84.high_ref, s32[1]{0:T(128)} %bitcast.place_ref, bf16[4096,384]{1,0:T(8,128)(2,1)} %get-tuple-element.192.q_ref, ...), custom_call_target="tpu_custom_call" | custom-call | flops 154618822656 | tf_op jit(solution)/shard_map/attention_backward/pallas_call | solution.py:346
  715.4 11.7 %input_grads.3 = (bf16[1024,768]{1,0:T(8,128)(2,1)}, bf16[1024,768]{1,0:T(8,128)(2,1)}, bf16[1024,768]{1,0:T(8,128)(2,1)}, bf16[1024,768]{1,0:T(8,128)(2,1)}) custom-call(bf16[4096,192]{1,0:T(8,128)(2,1)} %get-tuple-element.215.q_ref, bf16[4096,192]{1,0:T(8,128)(2,1)} %get-tuple-element.216.k_ref, bf16[4096,192]{1,0:T(8,128)(2,1)} %get-tuple-element.217.v_ref, ...), custom_call_target="tpu_custom_call" | custom-call | flops 10871635968 | tf_op jit(solution)/shard_map/input_grads/pallas_call | solution.py:612
  729.7 11.1 %projection_grads.3 = (bf16[768,576]{1,0:T(8,128)(2,1)}, f32[8,192]{1,0:T(8,128)}) custom-call(bf16[1024,768]{1,0:T(8,128)(2,1)} %p0.3, bf16[1024,768]{1,0:T(8,128)(2,1)} %collective-permute-done.p1, bf16[1024,768]{1,0:T(8,128)(2,1)} %copy-done.12, bf16[1024,768]{1,0:T(8,128)(2,1)} %copy-done.11, bf16[4096,192]{1,0:T(8,128)(2,1)} %get-tuple-element.215.q_ref, ...), custom_call_target="tpu_custom_call" | custom-call | flops 10871635968 | tf_op jit(solution)/shard_map/projection_grads/pallas_call | solution.py:637
  742.1 1.9 add_convert_fusion
  745.7 24.1 %reduce-scatter.5.cloned.1.call-done = bf16[96,1728]{1,0:T(8,128)(2,1)} async-done(((bf16[3072,1728]{1,0:T(8,128)(2,1)}), bf16[96,1728]{1,0:T(8,128)(2,1)}) %reduce-scatter.5.cloned.1.call-update) | async-done | bytes 331792 | tf_op jit(solution)/shard_map/reduce_scatter | solution.py:705
  770.9 4.2 all-to-all-start.1
  780.1 2.9 collective-permute-done.50
  783.0 5.6 bitcast_add_fusion
  790.2 11.4 %all-to-all-done.1 = bf16[8,112,576]{2,1,0:T(8,128)(2,1)S(1)} async-done(((bf16[8,112,576]{2,1,0:T(8,128)(2,1)}), bf16[8,112,576]{2,1,0:T(8,128)(2,1)S(1)}, u32[]{:S(2)}, u32[]{:S(2)}) %all-to-all-start.1) | async-done | bytes 1032224 | tf_op jit(solution)/shard_map/all_to_all | solution.py:721
  (316 shorter events, 77.1 us)
Async XLA Ops:
  7.2 128.8 %all-gather.6.cloned.1.call-start = ((), (), s32[]{:S(2)}) async-start(), calls=%async_computation.4 | async-start | bytes 1327104 | tf_op jit(solution)/shard_map/all_gather | solution.py:790
  9.0 150.1 %all-gather.8.cloned.1.call-start = ((), (), s32[]{:S(2)}) async-start(), calls=%async_computation.7 | async-start | bytes 11354112 | tf_op jit(solution)/shard_map/all_gather | solution.py:656
  11.7 318.4 %all-gather.10.cloned.1.call-start = ((), (), s32[]{:S(2)}) async-start(), calls=%async_computation.8 | async-start | bytes 11354112 | tf_op jit(solution)/shard_map/all_gather | solution.py:656
  13.2 51.4 %collective-permute-start.11 = (f32[2,768]{1,0:T(2,128)S(1)}, f32[2,768]{1,0:T(2,128)S(1)}, u32[]{:S(2)}, u32[]{:S(2)}) collective-permute-start(f32[2,768]{1,0:T(2,128)S(1)} %get-tuple-element.345), channel_id=1, source_target_pairs={{0,1},{1,0},{2,3},{3,2},{4,5},{5,4},{6,7},{7,6},{8,9},{9,8},{10,11... | collective-permute-start | bytes 18440 | tf_op jit(solution)/shard_map/ppermute | solution.py:44
  13.7 54.7 %collective-permute-start.12 = (f32[2,768]{1,0:T(2,128)S(1)}, f32[2,768]{1,0:T(2,128)S(1)}, u32[]{:S(2)}, u32[]{:S(2)}) collective-permute-start(f32[2,768]{1,0:T(2,128)S(1)} %get-tuple-element.345), channel_id=1, source_target_pairs={{0,2},{1,3},{2,0},{3,1},{4,6},{5,7},{6,4},{7,5},{8,10},{9,11},{10,... | collective-permute-start | bytes 18440 | tf_op jit(solution)/shard_map/ppermute | solution.py:44
  16.3 57.7 %collective-permute-start = (bf16[1024,768]{1,0:T(8,128)(2,1)}, bf16[1024,768]{1,0:T(8,128)(2,1)}, u32[]{:S(2)}, u32[]{:S(2)}) collective-permute-start(bf16[1024,768]{1,0:T(8,128)(2,1)} %p0.3), channel_id=1, source_target_pairs={{0,1},{1,0},{2,3},{3,2},{4,5},{5,4},{6,7},{7,6},{8,9},{9,8},{10,11... | collective-permute-start | bytes 4718600 | tf_op jit(solution)/shard_map/ppermute | solution.py:44
  16.6 47.4 %collective-permute-start.1 = (bf16[512,768]{1,0:T(8,128)(2,1)S(1)}, bf16[512,768]{1,0:T(8,128)(2,1)S(1)}, u32[]{:S(2)}, u32[]{:S(2)}) collective-permute-start(bf16[512,768]{1,0:T(8,128)(2,1)S(1)} %get-tuple-element.319), channel_id=1, source_target_pairs={{0,2},{1,3},{2,0},{3,1},{4,6},{5,7},{6,4},{7,5},{8,10},{9,11},{10,... | collective-permute-start | bytes 2359304 | tf_op jit(solution)/shard_map/ppermute | solution.py:44
  16.9 47.1 %collective-permute-start.2 = (bf16[512,768]{1,0:T(8,128)(2,1)S(1)}, bf16[512,768]{1,0:T(8,128)(2,1)S(1)}, u32[]{:S(2)}, u32[]{:S(2)}) collective-permute-start(bf16[512,768]{1,0:T(8,128)(2,1)S(1)} %get-tuple-element.318), channel_id=1, source_target_pairs={{0,2},{1,3},{2,0},{3,1},{4,6},{5,7},{6,4},{7,5},{8,10},{9,11},{10,... | collective-permute-start | bytes 2359304 | tf_op jit(solution)/shard_map/ppermute | solution.py:44
  64.0 8.7 %collective-permute-start.4 = (bf16[512,768]{1,0:T(8,128)(2,1)S(1)}, bf16[512,768]{1,0:T(8,128)(2,1)S(1)}, u32[]{:S(2)}, u32[]{:S(2)}) collective-permute-start(bf16[512,768]{1,0:T(8,128)(2,1)S(1)} %collective-permute-done.2), channel_id=1, source_target_pairs={{0,1},{1,0},{2,3},{3,2},{4,5},{5,4},{6,7},{7,6},{8,9},{9,8},{10,11... | collective-permute-start | bytes 2359304 | tf_op jit(solution)/shard_map/ppermute | solution.py:44
  69.1 69.3 %collective-permute-start.5 = (f32[8,128]{1,0:T(8,128)S(1)}, f32[8,128]{1,0:T(8,128)S(1)}, u32[]{:S(2)}, u32[]{:S(2)}) collective-permute-start(f32[8,128]{1,0:T(8,128)S(1)} %broadcast_in_dim.57), channel_id=1, source_target_pairs={{0,1},{1,0},{2,3},{3,2},{4,5},{5,4},{6,7},{7,6},{8,9},{9,8},{10,11... | collective-permute-start | bytes 12296 | tf_op jit(solution)/shard_map/ppermute | solution.py:73
  69.3 69.0 %collective-permute-start.6 = (f32[8,128]{1,0:T(8,128)S(1)}, f32[8,128]{1,0:T(8,128)S(1)}, u32[]{:S(2)}, u32[]{:S(2)}) collective-permute-start(f32[8,128]{1,0:T(8,128)S(1)} %broadcast_in_dim.57), channel_id=1, source_target_pairs={{0,2},{1,3},{2,0},{3,1},{4,6},{5,7},{6,4},{7,5},{8,10},{9,11},{10,... | collective-permute-start | bytes 12296 | tf_op jit(solution)/shard_map/ppermute | solution.py:73
  72.7 65.6 %collective-permute-start.7 = (f32[8,128]{1,0:T(8,128)S(1)}, f32[8,128]{1,0:T(8,128)S(1)}, u32[]{:S(2)}, u32[]{:S(2)}) collective-permute-start(f32[8,128]{1,0:T(8,128)S(1)} %broadcast_in_dim.57), channel_id=1, source_target_pairs={{0,3},{1,2},{2,1},{3,0},{4,7},{5,6},{6,5},{7,4},{8,11},{9,10},{10,... | collective-permute-start | bytes 12296 | tf_op jit(solution)/shard_map/ppermute | solution.py:73
  139.3 11.2 %collective-permute-start.10 = (bf16[512,384]{1,0:T(8,128)(2,1)S(1)}, bf16[512,384]{1,0:T(8,128)(2,1)S(1)}, u32[]{:S(2)}, u32[]{:S(2)}) collective-permute-start(bf16[512,384]{1,0:T(8,128)(2,1)S(1)} %get-tuple-element.314), channel_id=1, source_target_pairs={{0,3},{1,2},{2,1},{3,0},{4,7},{5,6},{6,5},{7,4},{8,11},{9,10},{10,... | collective-permute-start | bytes 1179656 | tf_op jit(solution)/shard_map/ppermute | solution.py:44
  141.0 9.5 %collective-permute-start.8 = (bf16[512,384]{1,0:T(8,128)(2,1)S(1)}, bf16[512,384]{1,0:T(8,128)(2,1)S(1)}, u32[]{:S(2)}, u32[]{:S(2)}) collective-permute-start(bf16[512,384]{1,0:T(8,128)(2,1)S(1)} %get-tuple-element.316), channel_id=1, source_target_pairs={{0,1},{1,0},{2,3},{3,2},{4,5},{5,4},{6,7},{7,6},{8,9},{9,8},{10,11... | collective-permute-start | bytes 1179656 | tf_op jit(solution)/shard_map/ppermute | solution.py:44
  141.0 18.1 %collective-permute-start.9 = (bf16[512,384]{1,0:T(8,128)(2,1)S(1)}, bf16[512,384]{1,0:T(8,128)(2,1)S(1)}, u32[]{:S(2)}, u32[]{:S(2)}) collective-permute-start(bf16[512,384]{1,0:T(8,128)(2,1)S(1)} %get-tuple-element.315), channel_id=1, source_target_pairs={{0,2},{1,3},{2,0},{3,1},{4,6},{5,7},{6,4},{7,5},{8,10},{9,11},{10,... | collective-permute-start | bytes 1179656 | tf_op jit(solution)/shard_map/ppermute | solution.py:44
  187.9 20.5 %collective-permute-start.15 = (bf16[512,768]{1,0:T(8,128)(2,1)S(1)}, bf16[512,768]{1,0:T(8,128)(2,1)S(1)}, u32[]{:S(2)}, u32[]{:S(2)}) collective-permute-start(bf16[512,768]{1,0:T(8,128)(2,1)S(1)} %get-tuple-element.312), channel_id=1, source_target_pairs={{0,2},{1,3},{2,0},{3,1},{4,6},{5,7},{6,4},{7,5},{8,10},{9,11},{10,... | collective-permute-start | bytes 2359304 | tf_op jit(solution)/shard_map/ppermute | solution.py:44
  189.5 34.6 %collective-permute-start.16 = (bf16[512,768]{1,0:T(8,128)(2,1)S(1)}, bf16[512,768]{1,0:T(8,128)(2,1)S(1)}, u32[]{:S(2)}, u32[]{:S(2)}) collective-permute-start(bf16[512,768]{1,0:T(8,128)(2,1)S(1)} %get-tuple-element.313), channel_id=1, source_target_pairs={{0,2},{1,3},{2,0},{3,1},{4,6},{5,7},{6,4},{7,5},{8,10},{9,11},{10,... | collective-permute-start | bytes 2359304 | tf_op jit(solution)/shard_map/ppermute | solution.py:44
  190.0 39.1 %collective-permute-start.14 = (bf16[1024,768]{1,0:T(8,128)(2,1)S(1)}, bf16[1024,768]{1,0:T(8,128)(2,1)}, u32[]{:S(2)}, u32[]{:S(2)}) collective-permute-start(bf16[1024,768]{1,0:T(8,128)(2,1)S(1)} %bitcast.97), channel_id=1, source_target_pairs={{0,1},{1,0},{2,3},{3,2},{4,5},{5,4},{6,7},{7,6},{8,9},{9,8},{10,11... | collective-permute-start | bytes 4718600 | tf_op jit(solution)/shard_map/ppermute | solution.py:44
  208.4 17.8 %collective-permute-start.17 = (bf16[512,768]{1,0:T(8,128)(2,1)S(1)}, bf16[512,768]{1,0:T(8,128)(2,1)}, u32[]{:S(2)}, u32[]{:S(2)}) collective-permute-start(bf16[512,768]{1,0:T(8,128)(2,1)S(1)} %collective-permute-done.15), channel_id=1, source_target_pairs={{0,1},{1,0},{2,3},{3,2},{4,5},{5,4},{6,7},{7,6},{8,9},{9,8},{10,11... | collective-permute-start | bytes 2359304 | tf_op jit(solution)/shard_map/ppermute | solution.py:44
  229.1 332.1 %reduce-scatter.3.cloned.1.call-start = ((), (), s32[]{:S(2)}) async-start(), calls=%async_computation.5 | async-start | bytes 11354112 | tf_op jit(solution)/shard_map/reduce_scatter | solution.py:705
  229.9 9.4 %collective-permute-start.20 = (f32[8,128]{1,0:T(8,128)S(1)}, f32[8,128]{1,0:T(8,128)S(1)}, u32[]{:S(2)}, u32[]{:S(2)}) collective-permute-start(f32[8,128]{1,0:T(8,128)S(1)} %add_add_fusion.3), channel_id=1, source_target_pairs={{0,8},{4,12},{8,0},{12,4},{16,24},{20,28},{24,16},{28,20},{1,9},{5... | collective-permute-start | bytes 12296 | tf_op jit(solution)/shard_map/ppermute | solution.py:73
  230.9 10.1 %collective-permute-start.21 = (f32[8,128]{1,0:T(8,128)S(1)}, f32[8,128]{1,0:T(8,128)S(1)}, u32[]{:S(2)}, u32[]{:S(2)}) collective-permute-start(f32[8,128]{1,0:T(8,128)S(1)} %add_add_fusion.3), channel_id=1, source_target_pairs={{0,12},{4,8},{8,4},{12,0},{16,28},{20,24},{24,20},{28,16},{1,13},{... | collective-permute-start | bytes 12296 | tf_op jit(solution)/shard_map/ppermute | solution.py:73
  233.4 7.7 collective-permute-start.22
  310.6 12.0 %collective-permute-start.27 = (bf16[512,384]{1,0:T(8,128)(2,1)S(1)}, bf16[512,384]{1,0:T(8,128)(2,1)S(1)}, u32[]{:S(2)}, u32[]{:S(2)}) collective-permute-start(bf16[512,384]{1,0:T(8,128)(2,1)S(1)} %get-tuple-element.309), channel_id=1, source_target_pairs={{0,2},{1,3},{2,0},{3,1},{4,6},{5,7},{6,4},{7,5},{8,10},{9,11},{10,... | collective-permute-start | bytes 1179656 | tf_op jit(solution)/shard_map/ppermute | solution.py:44
  312.1 18.0 %collective-permute-start.28 = (bf16[512,384]{1,0:T(8,128)(2,1)S(1)}, bf16[512,384]{1,0:T(8,128)(2,1)S(1)}, u32[]{:S(2)}, u32[]{:S(2)}) collective-permute-start(bf16[512,384]{1,0:T(8,128)(2,1)S(1)} %get-tuple-element.308), channel_id=1, source_target_pairs={{0,3},{1,2},{2,1},{3,0},{4,7},{5,6},{6,5},{7,4},{8,11},{9,10},{10,... | collective-permute-start | bytes 1179656 | tf_op jit(solution)/shard_map/ppermute | solution.py:44
  385.8 20.9 %collective-permute-start.29 = (bf16[512,384]{1,0:T(8,128)(2,1)}, bf16[512,384]{1,0:T(8,128)(2,1)S(1)}, u32[]{:S(2)}, u32[]{:S(2)}) collective-permute-start(bf16[512,384]{1,0:T(8,128)(2,1)} %get-tuple-element.163), channel_id=1, source_target_pairs={{0,1},{1,0},{2,3},{3,2},{4,5},{5,4},{6,7},{7,6},{8,9},{9,8},{10,11... | collective-permute-start | bytes 1179656 | tf_op jit(solution)/shard_map/ppermute | solution.py:44
  386.2 20.6 %collective-permute-start.30 = (bf16[512,384]{1,0:T(8,128)(2,1)}, bf16[512,384]{1,0:T(8,128)(2,1)S(1)}, u32[]{:S(2)}, u32[]{:S(2)}) collective-permute-start(bf16[512,384]{1,0:T(8,128)(2,1)} %get-tuple-element.164), channel_id=1, source_target_pairs={{0,2},{1,3},{2,0},{3,1},{4,6},{5,7},{6,4},{7,5},{8,10},{9,11},{10,... | collective-permute-start | bytes 1179656 | tf_op jit(solution)/shard_map/ppermute | solution.py:44
  387.7 19.1 %collective-permute-start.31 = (bf16[512,384]{1,0:T(8,128)(2,1)}, bf16[512,384]{1,0:T(8,128)(2,1)S(1)}, u32[]{:S(2)}, u32[]{:S(2)}) collective-permute-start(bf16[512,384]{1,0:T(8,128)(2,1)} %get-tuple-element.165), channel_id=1, source_target_pairs={{0,3},{1,2},{2,1},{3,0},{4,7},{5,6},{6,5},{7,4},{8,11},{9,10},{10,... | collective-permute-start | bytes 1179656 | tf_op jit(solution)/shard_map/ppermute | solution.py:44
  506.0 22.2 %collective-permute-start.32 = (bf16[1024,768]{1,0:T(8,128)(2,1)}, bf16[1024,768]{1,0:T(8,128)(2,1)}, u32[]{:S(2)}, u32[]{:S(2)}) collective-permute-start(bf16[1024,768]{1,0:T(8,128)(2,1)} %get-tuple-element.179), channel_id=1, source_target_pairs={{0,1},{1,0},{2,3},{3,2},{4,5},{5,4},{6,7},{7,6},{8,9},{9,8},{10,11... | collective-permute-start | bytes 4718600 | tf_op jit(solution)/shard_map/ppermute | solution.py:44
  512.2 43.5 %collective-permute-start.34 = (bf16[1024,768]{1,0:T(8,128)(2,1)}, bf16[1024,768]{1,0:T(8,128)(2,1)}, u32[]{:S(2)}, u32[]{:S(2)}) collective-permute-start(bf16[1024,768]{1,0:T(8,128)(2,1)} %add_convert_fusion.1), channel_id=1, source_target_pairs={{0,2},{1,3},{2,0},{3,1},{4,6},{5,7},{6,4},{7,5},{8,10},{9,11},{10,... | collective-permute-start | bytes 4718600 | tf_op jit(solution)/shard_map/ppermute | solution.py:44
  563.1 53.3 %all-to-all-start = ((bf16[8,112,576]{2,1,0:T(8,128)(2,1)}), bf16[8,112,576]{2,1,0:T(8,128)(2,1)S(1)}, u32[]{:S(2)}, u32[]{:S(2)}) async-start(bf16[8,112,576]{2,1,0:T(8,128)(2,1)} %pad_maximum_fusion.2), calls=%async_computation.1 | async-start | bytes 2293760 | tf_op jit(solution)/shard_map/all_to_all | solution.py:699
  567.6 202.3 %reduce-scatter.5.cloned.1.call-start = ((), (), s32[]{:S(2)}) async-start(), calls=%async_computation.6 | async-start | bytes 11354112 | tf_op jit(solution)/shard_map/reduce_scatter | solution.py:705
  592.7 22.7 %collective-permute-start.39 = (f32[32,768]{1,0:T(8,128)S(1)}, f32[32,768]{1,0:T(8,128)S(1)}, u32[]{:S(2)}, u32[]{:S(2)}) collective-permute-start(f32[32,768]{1,0:T(8,128)S(1)} %constant_dynamic-update-slice_fusion.4), channel_id=1, source_target_pairs={{0,2},{1,3},{2,0},{3,1},{4,6},{5,7},{6,4},{7,5},{8,10},{9,11},{10,... | collective-permute-start | bytes 294920 | tf_op jit(solution)/shard_map/ppermute | solution.py:73
  593.2 22.2 %collective-permute-start.40 = (f32[32,768]{1,0:T(8,128)S(1)}, f32[32,768]{1,0:T(8,128)S(1)}, u32[]{:S(2)}, u32[]{:S(2)}) collective-permute-start(f32[32,768]{1,0:T(8,128)S(1)} %constant_dynamic-update-slice_fusion.4), channel_id=1, source_target_pairs={{0,3},{1,2},{2,1},{3,0},{4,7},{5,6},{6,5},{7,4},{8,11},{9,10},{10,... | collective-permute-start | bytes 294920 | tf_op jit(solution)/shard_map/ppermute | solution.py:73
  594.6 20.9 %collective-permute-start.35 = (bf16[512,384]{1,0:T(8,128)(2,1)}, bf16[512,384]{1,0:T(8,128)(2,1)S(1)}, u32[]{:S(2)}, u32[]{:S(2)}) collective-permute-start(bf16[512,384]{1,0:T(8,128)(2,1)} %get-tuple-element.194), channel_id=1, source_target_pairs={{0,1},{1,0},{2,3},{3,2},{4,5},{5,4},{6,7},{7,6},{8,9},{9,8},{10,11... | collective-permute-start | bytes 1179656 | tf_op jit(solution)/shard_map/ppermute | solution.py:44
  594.8 20.6 %collective-permute-start.36 = (bf16[512,384]{1,0:T(8,128)(2,1)}, bf16[512,384]{1,0:T(8,128)(2,1)S(1)}, u32[]{:S(2)}, u32[]{:S(2)}) collective-permute-start(bf16[512,384]{1,0:T(8,128)(2,1)} %get-tuple-element.195), channel_id=1, source_target_pairs={{0,2},{1,3},{2,0},{3,1},{4,6},{5,7},{6,4},{7,5},{8,10},{9,11},{10,... | collective-permute-start | bytes 1179656 | tf_op jit(solution)/shard_map/ppermute | solution.py:44
  595.4 21.0 %collective-permute-start.37 = (bf16[512,384]{1,0:T(8,128)(2,1)}, bf16[512,384]{1,0:T(8,128)(2,1)S(1)}, u32[]{:S(2)}, u32[]{:S(2)}) collective-permute-start(bf16[512,384]{1,0:T(8,128)(2,1)} %get-tuple-element.196), channel_id=1, source_target_pairs={{0,3},{1,2},{2,1},{3,0},{4,7},{5,6},{6,5},{7,4},{8,11},{9,10},{10,... | collective-permute-start | bytes 1179656 | tf_op jit(solution)/shard_map/ppermute | solution.py:44
  617.1 7.9 collective-permute-start.41
  619.1 9.3 %collective-permute-start.42 = (f32[32,768]{1,0:T(8,128)}, f32[32,768]{1,0:T(8,128)S(1)}, u32[]{:S(2)}, u32[]{:S(2)}) collective-permute-start(f32[32,768]{1,0:T(8,128)} %add_add_fusion.1), channel_id=1, source_target_pairs={{0,8},{4,12},{8,0},{12,4},{16,24},{20,28},{24,16},{28,20},{1,9},{5... | collective-permute-start | bytes 294920 | tf_op jit(solution)/shard_map/ppermute | solution.py:73
  620.6 93.5 %collective-permute-start.43 = (f32[32,768]{1,0:T(8,128)}, f32[32,768]{1,0:T(8,128)}, u32[]{:S(2)}, u32[]{:S(2)}) collective-permute-start(f32[32,768]{1,0:T(8,128)} %add_add_fusion.1), channel_id=1, source_target_pairs={{0,12},{4,8},{8,4},{12,0},{16,28},{20,24},{24,20},{28,16},{1,13},{... | collective-permute-start | bytes 294920 | tf_op jit(solution)/shard_map/ppermute | solution.py:73
  620.6 93.5 %collective-permute-start.44 = (f32[32,768]{1,0:T(8,128)}, f32[32,768]{1,0:T(8,128)}, u32[]{:S(2)}, u32[]{:S(2)}) collective-permute-start(f32[32,768]{1,0:T(8,128)} %add_add_fusion.1), channel_id=1, source_target_pairs={{0,16},{4,20},{8,24},{12,28},{16,0},{20,4},{24,8},{28,12},{1,17},{... | collective-permute-start | bytes 294920 | tf_op jit(solution)/shard_map/ppermute | solution.py:73
  623.5 90.6 %collective-permute-start.45 = (f32[32,768]{1,0:T(8,128)}, f32[32,768]{1,0:T(8,128)}, u32[]{:S(2)}, u32[]{:S(2)}) collective-permute-start(f32[32,768]{1,0:T(8,128)} %add_add_fusion.1), channel_id=1, source_target_pairs={{0,20},{4,16},{8,28},{12,24},{16,4},{20,0},{24,12},{28,8},{1,21},{... | collective-permute-start | bytes 294920 | tf_op jit(solution)/shard_map/ppermute | solution.py:73
  625.0 89.1 %collective-permute-start.46 = (f32[32,768]{1,0:T(8,128)}, f32[32,768]{1,0:T(8,128)}, u32[]{:S(2)}, u32[]{:S(2)}) collective-permute-start(f32[32,768]{1,0:T(8,128)} %add_add_fusion.1), channel_id=1, source_target_pairs={{0,24},{4,28},{8,16},{12,20},{16,8},{20,12},{24,0},{28,4},{1,25},{... | collective-permute-start | bytes 294920 | tf_op jit(solution)/shard_map/ppermute | solution.py:73
  628.4 85.8 %collective-permute-start.47 = (f32[32,768]{1,0:T(8,128)}, f32[32,768]{1,0:T(8,128)}, u32[]{:S(2)}, u32[]{:S(2)}) collective-permute-start(f32[32,768]{1,0:T(8,128)} %add_add_fusion.1), channel_id=1, source_target_pairs={{0,28},{4,24},{8,20},{12,16},{16,12},{20,8},{24,4},{28,0},{1,29},{... | collective-permute-start | bytes 294920 | tf_op jit(solution)/shard_map/ppermute | solution.py:73
  727.1 15.0 %collective-permute-start.49 = (bf16[1024,768]{1,0:T(8,128)(2,1)}, bf16[1024,768]{1,0:T(8,128)(2,1)}, u32[]{:S(2)}, u32[]{:S(2)}) collective-permute-start(bf16[1024,768]{1,0:T(8,128)(2,1)} %get-tuple-element.221), channel_id=1, source_target_pairs={{0,1},{1,0},{2,3},{3,2},{4,5},{5,4},{6,7},{7,6},{8,9},{9,8},{10,11... | collective-permute-start | bytes 4718600 | tf_op jit(solution)/shard_map/ppermute | solution.py:44
  741.6 38.5 %collective-permute-start.48 = (bf16[1024,768]{1,0:T(8,128)(2,1)}, bf16[1024,768]{1,0:T(8,128)(2,1)}, u32[]{:S(2)}, u32[]{:S(2)}) collective-permute-start(bf16[1024,768]{1,0:T(8,128)(2,1)} %get-tuple-element.219), channel_id=1, source_target_pairs={{0,1},{1,0},{2,3},{3,2},{4,5},{5,4},{6,7},{7,6},{8,9},{9,8},{10,11... | collective-permute-start | bytes 4718600 | tf_op jit(solution)/shard_map/ppermute | solution.py:44
  744.0 39.0 %collective-permute-start.50 = (bf16[1024,768]{1,0:T(8,128)(2,1)S(1)}, bf16[1024,768]{1,0:T(8,128)(2,1)}, u32[]{:S(2)}, u32[]{:S(2)}) collective-permute-start(bf16[1024,768]{1,0:T(8,128)(2,1)S(1)} %add_convert_fusion), channel_id=1, source_target_pairs={{0,2},{1,3},{2,0},{3,1},{4,6},{5,7},{6,4},{7,5},{8,10},{9,11},{10,... | collective-permute-start | bytes 4718600 | tf_op jit(solution)/shard_map/ppermute | solution.py:44
  770.9 30.8 %all-to-all-start.1 = ((bf16[8,112,576]{2,1,0:T(8,128)(2,1)}), bf16[8,112,576]{2,1,0:T(8,128)(2,1)S(1)}, u32[]{:S(2)}, u32[]{:S(2)}) async-start(bf16[8,112,576]{2,1,0:T(8,128)(2,1)} %pad_maximum_fusion.3), calls=%async_computation.3 | async-start | bytes 2293760 | tf_op jit(solution)/shard_map/all_to_all | solution.py:721
  (63 other events, 964.2 us)
Sparse Core Ops, SparseCore 0:
  10.8 51.5 all-gather.5
  65.4 87.4 all-gather.7
  229.2 87.9 all-gather.9
  406.9 154.2 reduce-scatter.2
  625.1 144.6 reduce-scatter.4

commit v4 on v3

--- a/solution.py
+++ b/solution.py
@@ -54,13 +54,6 @@
 
 def exchange_pieces(pieces):
     return [pieces[0]] + [flip(pieces[r], r) for r in range(1, 4)]
-
-
-def scatter_chunks(chunks):
-    crossing = chunks[2].astype(f32) + flip(chunks[3], 1).astype(f32)
-    near = flip(chunks[1], 1).astype(f32)
-    far = flip(crossing.astype(bf16), 2).astype(f32)
-    return chunks[0].astype(f32) + near + far
 
 
 def tie(*items):
@@ -140,7 +133,7 @@
     )(*pieces, matrix, query_bias[None], value_bias[None], query_marks, key_marks)
 
 
-def attention_forward(low, high, place, queries, keys, values):
+def attention_forward(low, high, place, queries, keys, values, base):
     rows, wide = queries.shape
     heads = wide // LANES
     count = rows // TILE
@@ -148,10 +141,11 @@
     half = rows // 8
     half_blocks = half // TILE
     group = heads * HEAD_DIM
+    skip = base * per_chunk
 
     def body(low_ref, high_ref, place_ref, q_ref, k_ref, v_ref, ctx_ref, ql_ref, *scratch):
         peak, fade, total, score = scratch
-        block = pl.program_id(0)
+        block = pl.program_id(0) + skip
         own = place_ref[0]
         first = low_ref[block]
         last = high_ref[block]
@@ -220,12 +214,12 @@
         def _():
             ctx_ref[0, pl.ds(at, TILE), group : 2 * group] = ctx
 
-    row_spec = pl.BlockSpec((TILE, wide), lambda i, *_: (i, 0))
+    row_spec = pl.BlockSpec((TILE, wide), lambda i, *_: (i + skip, 0))
     return pl.pallas_call(
         body,
         grid_spec=pltpu.PrefetchScalarGridSpec(
             num_scalar_prefetch=3,
-            grid=(count,),
+            grid=(count // 2,),
             in_specs=[row_spec, WHOLE, WHOLE],
             out_specs=[
                 pl.BlockSpec((1, half, 2 * group), lambda i, *_: (i // per_chunk, 0, 0)),
@@ -239,11 +233,12 @@
             ],
         ),
         out_shape=[
-            jax.ShapeDtypeStruct((4, half, 2 * group), bf16),
+            jax.ShapeDtypeStruct((2, half, 2 * group), bf16),
             jax.ShapeDtypeStruct((rows, wide), bf16),
         ],
         compiler_params=kernel_params(),
-        cost_estimate=cost(12 * rows * rows * wide),
+        input_output_aliases={3: 1},
+        cost_estimate=cost(4 * rows * rows * wide),
         name="attention_forward",
     )(low, high, place, queries, keys, values)
 
@@ -257,7 +252,7 @@
     half_blocks = half // TILE
     group = heads * HEAD_DIM
 
-    def body(low_ref, high_ref, place_ref, q_ref, k_ref, v_ref, c_ref, g0, g1, g2, g3, *rest):
+    def body(low_ref, high_ref, place_ref, q_ref, k_ref, v_ref, near, far, g0, g1, g2, g3, *rest):
         dq_ref, dk_ref, dv_ref, do_all, dq_all, acc_k, acc_v, prob, slope = rest
         block = pl.program_id(0)
         own = place_ref[0]
@@ -269,13 +264,14 @@
             dq_all[...] = jnp.zeros_like(dq_all)
             lane = lax.broadcasted_iota(jnp.int32, (TILE, HEAD_DIM), 1)
             for chunk, g_ref in enumerate((g0, g1, g2, g3)):
-
-                def prepare(b, carry, chunk=chunk, g_ref=g_ref):
+                c_ref = (near, far)[chunk // 2]
+
+                def prepare(b, carry, chunk=chunk, g_ref=g_ref, c_ref=c_ref):
                     at = pl.multiple_of(b * TILE, TILE)
                     for side in range(2):
                         cols = slice(side * group, (side + 1) * group)
                         row = pl.multiple_of((2 * chunk + side) * half + at, TILE)
-                        c = c_ref[chunk, pl.ds(at, TILE), cols].astype(f32)
+                        c = c_ref[chunk % 2, pl.ds(at, TILE), cols].astype(f32)
                         g = g_ref[pl.ds(at, TILE), cols].astype(f32)
                         for h in range(heads):
                             lo = h * HEAD_DIM
@@ -348,7 +344,7 @@
         grid_spec=pltpu.PrefetchScalarGridSpec(
             num_scalar_prefetch=3,
             grid=(count,),
-            in_specs=[WHOLE, row_spec, row_spec] + [WHOLE] * 5,
+            in_specs=[WHOLE, row_spec, row_spec] + [WHOLE] * 6,
             out_specs=[WHOLE, out_spec, out_spec],
             scratch_shapes=[
                 pltpu.VMEM((rows, wide), bf16),
@@ -363,7 +359,7 @@
         compiler_params=kernel_params(),
         cost_estimate=cost(24 * rows * rows * wide),
         name="attention_backward",
-    )(low, high, place, queries, keys, values, contexts, *grads)
+    )(low, high, place, queries, keys, values, *contexts, *grads)
 
 
 SQRT_HALF = 0.7071067811865476
@@ -592,31 +588,31 @@
     )(place, sent, inner, branch, act, attn, *pieces)
 
 
-def input_grads(grad_q, grad_k, grad_v, matrix):
+def input_grads(grad_q, grad_k, grad_v, matrix, base, number):
     rows, group = grad_q.shape
     width = matrix.shape[0]
     chunk = rows // 4
 
-    def body(q_ref, k_ref, v_ref, mat, o0, o1, o2, o3):
+    def body(q_ref, k_ref, v_ref, mat, *outs):
         full = dot_nt(q_ref[...], mat[:, 0:group])
         full = full + dot_nt(k_ref[...], mat[:, group : 2 * group])
         full = (full + dot_nt(v_ref[...], mat[:, 2 * group : 3 * group])).astype(bf16)
-        for r, o_ref in enumerate((o0, o1, o2, o3)):
-
-            @pl.when(pl.program_id(0) == r)
+        for r, o_ref in enumerate(outs):
+
+            @pl.when(pl.program_id(0) == number - 1 - r)
             def _(o_ref=o_ref):
                 o_ref[...] = full
 
-    spec = pl.BlockSpec((chunk, group), lambda i: (i, 0))
+    spec = pl.BlockSpec((chunk, group), lambda i: (base + number - 1 - i, 0))
     out = jax.ShapeDtypeStruct((chunk, width), bf16)
     return pl.pallas_call(
         body,
-        grid=(4,),
+        grid=(number,),
         in_specs=[spec] * 3 + [WHOLE],
-        out_specs=[WHOLE] * 4,
-        out_shape=[out] * 4,
+        out_specs=[WHOLE] * number,
+        out_shape=[out] * number,
         compiler_params=kernel_params(),
-        cost_estimate=cost(6 * rows * width * 3 * group),
+        cost_estimate=cost(6 * number * chunk * width * 3 * group),
         name="input_grads",
     )(grad_q, grad_k, grad_v, matrix)
 
@@ -654,7 +650,20 @@
 
 def gather_all(local):
     parts = lax.all_gather(local, ("tensor", "dp"), axis=0, tiled=False)
-    return parts.reshape(4, -1, local.shape[1])
+    return parts, parts.reshape(4, -1, local.shape[1])
+
+
+def with_count(local, count):
+    high = count // LANES
+    digits = jnp.stack([high, count - high * LANES]).astype(bf16)
+    digits = jnp.concatenate([digits, jnp.zeros((HEAD_DIM - 2,), bf16)])
+    spare = jnp.broadcast_to(digits[None], (local.shape[0], HEAD_DIM))
+    return jnp.concatenate([local, spare], axis=1)
+
+
+def count_of(parts, column):
+    digits = parts[:, 0, column : column + 2].astype(f32)
+    return jnp.sum(digits[:, 0]) * LANES + jnp.sum(digits[:, 1])
 
 
 def layer_forward(hidden, chunks, context, params, matrix, weights, up_bias, ahead=None):
@@ -664,9 +673,12 @@
     queries, keys, values = project(
         chunks, matrix, params[3], params[4], query_marks, key_marks
     )
-    contexts, queries = attention_forward(low, high, place, queries, keys, values)
-    contexts, ahead = tie(contexts, ahead)
-    pieces = exchange_pieces([contexts[r] for r in range(4)])
+    far, queries = attention_forward(low, high, place, queries, keys, values, 2)
+    sent = [flip(far[r], 2 + r) for r in range(2)]
+    near, queries = attention_forward(low, high, place, queries, keys, values, 0)
+    near, sent, ahead = tie(near, sent, ahead)
+    pieces = [near[0], flip(near[1], 1)] + sent
+    contexts = (near, far)
     out, out_low, normed, act, slope, y1, y2, r1, r2 = tokens_forward(
         place, hidden, pieces, weights, up_bias, vectors
     )
@@ -701,7 +713,7 @@
     packed = weight_grads(place, normed, inner, branch, act, attn, pieces)
     grads, packed, around, narrow = tie(grads, packed, around, narrow)
     if earlier is not None:
-        sums = sum_over(add_up(sums, around), "dp")
+        sums = add_up(sums, around)
     wide = lax.psum_scatter(
         packed.reshape(4 * width, -1), ("tensor", "dp"), scatter_dimension=0, tiled=True
     ).astype(f32)
@@ -710,15 +722,21 @@
     )
     if earlier is not None:
         grad_q, grad_k, grad_v, sums = tie(grad_q, grad_k, grad_v, sums)
-    partial = input_grads(grad_q, grad_k, grad_v, matrix)
-    grad_in = first + scatter_chunks(partial)
+    (beyond,) = input_grads(grad_q, grad_k, grad_v, matrix, 3, 1)
+    (across,) = input_grads(grad_q, grad_k, grad_v, matrix, 2, 1)
+    crossing = (across.astype(f32) + flip(beyond, 1).astype(f32)).astype(bf16)
+    crossing, grad_q, grad_k, grad_v = tie(crossing, grad_q, grad_k, grad_v)
+    crossing = flip(crossing, 2)
+    here, beside = input_grads(grad_q, grad_k, grad_v, matrix, 0, 2)
+    grad_in = here.astype(f32) + flip(beside, 1).astype(f32) + crossing.astype(f32)
+    grad_in = first + grad_in
     proj, proj_bias = projection_grads(chunks, grad_q, grad_k, grad_v)
     both = with_bias(proj, proj_bias[0:3].reshape(-1), parts)
     if earlier is None:
         grad_in, wide, both = tie(grad_in, wide, both)
         return grad_in, wide, (sums, both)
-    both, wide = tie(both, wide)
     both = lax.all_to_all(both, "dp", 0, 0, tiled=True)
+    both, grad_in, wide, sums = tie(both, grad_in, wide, sum_over(sums, "dp"))
     return grad_in, wide, (sums, both, narrow)
 
 
@@ -786,18 +804,19 @@
     doc_local = jnp.concatenate(doc_params[0:3], axis=1)
     group3 = doc_local.shape[1]
     doc_local = jnp.pad(doc_local, ((0, 0), (0, LANES)))
-    ask_weights = gather_all(pack_local(ask_params))
+    _, ask_weights = gather_all(pack_local(ask_params))
     doc_matrix = lax.all_gather(doc_local, "dp", axis=0, tiled=True)[:, :group3]
     up_local = jnp.stack([ask_params[10], doc_params[10]])
     up_all = jnp.stack([up_local] + [flip(up_local, r) for r in range(1, 4)])
     up_all = reorder(up_all, place, 0)
 
     mask_rows = valid_mask.astype(f32)
-    valid_total = jnp.full((8, LANES), jnp.sum(mask_rows), f32)
-    valid_around = send_around(valid_total, "tensor", 1, 4)
+    doc_pack = pack_local(doc_params)
+    column = doc_pack.shape[1]
+    doc_pack = with_count(doc_pack, jnp.sum(valid_mask))
     all_rows = rows * lax.axis_size("dp") * lax.axis_size("tensor")
 
-    middle, middle_low, ask_saved, (doc_matrix, valid_around) = layer_forward(
+    middle, middle_low, ask_saved, doc_matrix = layer_forward(
         tokens,
         gather_chunks(tokens),
         context,
@@ -805,12 +824,11 @@
         ask_matrix,
         ask_weights,
         up_all[:, 0],
-        (doc_matrix, valid_around),
-    )
-    valid_total = sum_over(add_up(valid_total, valid_around), "dp")
-    doc_chunks, doc_pack = tie(gather_chunks(middle_low), pack_local(doc_params))
-    doc_weights = gather_all(doc_pack)
-    final, final_low, doc_saved, valid_total = layer_forward(
+        doc_matrix,
+    )
+    doc_chunks, doc_pack = tie(gather_chunks(middle_low), doc_pack)
+    doc_parts, doc_weights = gather_all(doc_pack)
+    final, final_low, doc_saved, _ = layer_forward(
         middle,
         doc_chunks,
         context,
@@ -818,9 +836,8 @@
         doc_matrix,
         doc_weights,
         up_all[:, 1],
-        valid_total,
-    )
-    valid_total = valid_total[0, 0]
+    )
+    valid_total = count_of(doc_parts, column)
     grad_final = mask_rows[:, None] * (final - teacher.astype(f32)) * (all_rows / valid_total)
     grad_middle, doc_wide, pending = layer_backward(
         grad_final, context, doc_matrix, doc_weights, doc_saved

time: 822 us -> 841 us (1.023); the launches traced: 810 us -> 839 us
  Pallas kernels: 481 us -> 499 us
    all_gather x2, waiting for transfers between devices: 0.01 us -> 39.1 us  [gather_all(): parts = lax.all_gather(local, ('tensor', 'dp'), axis=0, tiled=False)]
    ppermute x31, waiting for transfers between devices: 101 us -> 69 us  [flip(): return lax.ppermute(values, 'tensor', [(i, i ^ bit) for i in range(size)])]
    ppermute x20 -> x10, waiting for transfers between devices: 4.72 us -> 32.8 us  [send_around(): lax.ppermute(values, axis, [(i, i ^ step * r) for i in range(size)])]
    reduce_scatter x2, waiting for transfers between devices: 25.2 us -> 3.26 us  [layer_backward(): lax.psum_scatter(packed.reshape(4 * width, -1), ('tensor', 'dp'), scatter...]
    all_to_all x1, waiting for transfers between devices: 11.4 us -> 0.01 us  [layer_backward(): both = lax.all_to_all(both, 'dp', 0, 0, tiled=True)]
    pallas_call x2 -> x4, Pallas kernels: 103 us -> 112 us  [attention_forward(): pl.pallas_call(body, grid_spec=pltpu.PrefetchScalarGridSpec(num_scalar_pr...]
    pallas_call x2 -> x6, Pallas kernels: 23.5 us -> 31.7 us  [input_grads(): pl.pallas_call(body, grid=(number,), in_specs=[spec] * 3 + [WHOLE], out_s...]
    ppermute x20 -> x10, starting transfers between devices: 26.5 us -> 23.3 us  [send_around(): lax.ppermute(values, axis, [(i, i ^ step * r) for i in range(size)])]
  transfers between devices with their start and end apart: 58 -> 48, of which waited for: 16 -> 14; matrix products, arithmetic and copies ran while one was open for 8% -> 8% of each run, Pallas kernels for 50% -> 50%
where the time goes in v4:
time: 841 us; the launch traced here: 839 us
  Pallas kernels  499 us (59%)
  waiting for transfers between devices  144 us (17%)
  starting transfers between devices  53.6 us (6%)
  other arithmetic  43.9 us (5%)
  local copies, waits for them, and re-layouts  40.5 us (5%)
  blocking collectives  38.5 us (5%)
  between operations  19.7 us (2%)
    pallas_call x2, Pallas kernels, attention_backward(): pl.pallas_call(body, grid_spec=pltpu.PrefetchScalarGridSpec(num_scalar_pr...  171 us
    pallas_call x4, Pallas kernels, attention_forward(): pl.pallas_call(body, grid_spec=pltpu.PrefetchScalarGridSpec(num_scalar_pr...  112 us
    ppermute x31, waiting for transfers between devices, flip(): return lax.ppermute(values, 'tensor', [(i, i ^ bit) for i in range(size)])  69 us
    pallas_call x2, Pallas kernels, tokens_forward(): pl.pallas_call(body, grid_spec=pltpu.PrefetchScalarGridSpec(num_scalar_pr...  53.2 us
    pallas_call x2, Pallas kernels, tokens_backward(): pl.pallas_call(body, grid_spec=pltpu.PrefetchScalarGridSpec(num_scalar_pr...  48.6 us
    all_gather x2, waiting for transfers between devices, gather_all(): parts = lax.all_gather(local, ('tensor', 'dp'), axis=0, tiled=False)  39.1 us
    all_gather x1, blocking collectives, on_device(): lax.all_gather(jnp.concatenate(ask_params[0:3], axis=1), 'dp', axis=0, ti...  38.5 us
    pallas_call x2, Pallas kernels, weight_grads(): pl.pallas_call(body, grid_spec=pltpu.PrefetchScalarGridSpec(num_scalar_pr...  37.4 us
  transfers between devices with their start and end apart: 48, of which 14 were waited for; matrix products, arithmetic and copies ran while one was open for 8% of the time, Pallas kernels for 50%

profile of v4, /device:TPU:0, one launch (start us, length us, event | category | flops | bytes accessed | tf_op | source)
XLA Modules:
  0.0 838.9 jit_solution(5564380613954182008)
XLA Ops:
  13.8 2.4 collective-permute-start.10
  31.4 38.5 %all_gather.18.mat = bf16[768,576]{1,0:T(8,128)(2,1)} all-gather(bf16[96,576]{1,0:T(8,128)(2,1)S(1)} %pad_maximum_fusion.5), channel_id=1, replica_groups=mesh['dp'=8,'tensor'=4] {'dp'}, dimensions={0}, use_global_device_ids=true | all-gather | bytes 995328 | tf_op jit(solution)/shard_map/all_gather | solution.py:801
  78.4 10.7 %project.2 = (bf16[4096,384]{1,0:T(8,128)(2,1)}, bf16[4096,384]{1,0:T(8,128)(2,1)}, bf16[4096,384]{1,0:T(8,128)(2,1)}) custom-call(bf16[1024,768]{1,0:T(8,128)(2,1)} %p0.3, bf16[1024,768]{1,0:T(8,128)(2,1)} %collective-permute-done.p1, bf16[1024,768]{1,0:T(8,128)(2,1)} %copy-done.12, bf16[1024,768]{1,0:T(8,128)(2,1)} %copy-done.11, ...), custom_call_target="tpu_custom_call" | custom-call | flops 10871635968 | tf_op jit(solution)/shard_map/project/pallas_call | solution.py:124
  89.1 28.6 %attention_forward.4 = (bf16[2,512,384]{2,1,0:T(8,128)(2,1)}, bf16[4096,384]{1,0:T(8,128)(2,1)}) custom-call(s32[16]{0:T(128)} %squeeze.85.low_ref, s32[16]{0:T(128)} %squeeze.86.high_ref, s32[1]{0:T(128)} %bitcast.place_ref, bf16[4096,384]{1,0:T(8,128)(2,1)} %get-tuple-element.141.q_ref, ...), custom_call_target="tpu_custom_call", output_to_operand_aliasing={{1}: (3, {})} | custom-call | flops 25769803776 | tf_op jit(solution)/shard_map/attention_forward/pallas_call | solution.py:218
  121.1 27.1 %attention_forward.5 = (bf16[2,512,384]{2,1,0:T(8,128)(2,1)}, bf16[4096,384]{1,0:T(8,128)(2,1)}) custom-call(s32[16]{0:T(128)} %squeeze.85.low_ref, s32[16]{0:T(128)} %squeeze.86.high_ref, s32[1]{0:T(128)} %bitcast.place_ref, bf16[4096,384]{1,0:T(8,128)(2,1)} %get-tuple-element.144.q_ref, ...), custom_call_target="tpu_custom_call", output_to_operand_aliasing={{1}: (3, {})} | custom-call | flops 25769803776 | tf_op jit(solution)/shard_map/attention_forward/pallas_call | solution.py:218
  148.2 2.3 slice.274.mat
  150.6 5.3 collective-permute-done.6.c3
  159.1 8.1 all-gather.8.cloned.1.call-done
  167.1 26.5 %tokens_forward.2 = (f32[2,512,768]{2,1,0:T(8,128)}, bf16[2,512,768]{2,1,0:T(8,128)(2,1)}, bf16[2,512,768]{2,1,0:T(8,128)(2,1)}, bf16[2,512,3072]{2,1,0:T(8,128)...) custom-call(s32[1]{0:T(128)} %bitcast.place_ref, ...), custom_call_target="tpu_custom_call" | custom-call | flops 14495514624 | tf_op jit(solution)/shard_map/tokens_forward/pallas_call | solution.py:422
  197.4 18.4 %collective-permute-done.13 = bf16[512,768]{1,0:T(8,128)(2,1)S(1)} collective-permute-done((bf16[512,768]{1,0:T(8,128)(2,1)S(1)}, bf16[512,768]{1,0:T(8,128)(2,1)S(1)}, u32[]{:S(2)}, u32[]{:S(2)}) %collective-permute-start.13) | collective-permute-done | bytes 786464 | tf_op jit(solution)/shard_map/ppermute | solution.py:44
  215.8 16.1 %collective-permute-done.12 = bf16[512,768]{1,0:T(8,128)(2,1)S(1)} collective-permute-done((bf16[512,768]{1,0:T(8,128)(2,1)S(1)}, bf16[512,768]{1,0:T(8,128)(2,1)S(1)}, u32[]{:S(2)}, u32[]{:S(2)}) %collective-permute-start.12) | collective-permute-done | bytes 786464 | tf_op jit(solution)/shard_map/ppermute | solution.py:44
  238.1 2.6 pad_maximum_fusion.1.p3
  240.8 11.3 %project.3 = (bf16[4096,384]{1,0:T(8,128)(2,1)}, bf16[4096,384]{1,0:T(8,128)(2,1)}, bf16[4096,384]{1,0:T(8,128)(2,1)}) custom-call(bf16[1024,768]{1,0:T(8,128)(2,1)} %bitcast.100, bf16[1024,768]{1,0:T(8,128)(2,1)} %collective-permute-done.11.p1, bf16[1024,768]{1,0:T(8,128)(2,1)} %pad_maximum_fusion.p2, bf16[1024,768]{1,0:T(8,128)(2,1)} %pad_maximum_fusion.1.p3, ...), custom_call_target="tpu_custom_call" | custom-call | flops 10871635968 | tf_op jit(solution)/shard_map/project/pallas_call | solution.py:124
  252.1 28.8 %attention_forward.6 = (bf16[2,512,384]{2,1,0:T(8,128)(2,1)}, bf16[4096,384]{1,0:T(8,128)(2,1)}) custom-call(s32[16]{0:T(128)} %squeeze.85.low_ref, s32[16]{0:T(128)} %squeeze.86.high_ref, s32[1]{0:T(128)} %bitcast.place_ref, bf16[4096,384]{1,0:T(8,128)(2,1)} %get-tuple-element.157.q_ref, ...), custom_call_target="tpu_custom_call", output_to_operand_aliasing={{1}: (3, {})} | custom-call | flops 25769803776 | tf_op jit(solution)/shard_map/attention_forward/pallas_call | solution.py:218
  284.0 27.2 %attention_forward.7 = (bf16[2,512,384]{2,1,0:T(8,128)(2,1)}, bf16[4096,384]{1,0:T(8,128)(2,1)}) custom-call(s32[16]{0:T(128)} %squeeze.85.low_ref, s32[16]{0:T(128)} %squeeze.86.high_ref, s32[1]{0:T(128)} %bitcast.place_ref, bf16[4096,384]{1,0:T(8,128)(2,1)} %get-tuple-element.160.q_ref, ...), custom_call_target="tpu_custom_call", output_to_operand_aliasing={{1}: (3, {})} | custom-call | flops 25769803776 | tf_op jit(solution)/shard_map/attention_forward/pallas_call | solution.py:218
  311.2 2.2 slice_bitcast_fusion.2
  314.5 31.0 %all-gather.10.cloned.1.call-done = bf16[3072,1792]{1,0:T(8,128)(2,1)} async-done(((bf16[96,1792]{1,0:T(8,128)(2,1)}), bf16[3072,1792]{1,0:T(8,128)(2,1)}) %all-gather.10.cloned.1.call-update) | async-done | bytes 11010064 | tf_op jit(solution)/shard_map/all_gather | solution.py:652
  349.2 26.7 %tokens_forward.3 = (f32[2,512,768]{2,1,0:T(8,128)}, bf16[2,512,768]{2,1,0:T(8,128)(2,1)}, bf16[2,512,768]{2,1,0:T(8,128)(2,1)}, bf16[2,512,3072]{2,1,0:T(8,128)...) custom-call(s32[1]{0:T(128)} %bitcast.place_ref, ...), custom_call_target="tpu_custom_call" | custom-call | flops 14495514624 | tf_op jit(solution)/shard_map/tokens_forward/pallas_call | solution.py:422
  375.9 4.0 fusion.1
  379.9 24.3 %tokens_backward.2 = (bf16[2,512,768]{2,1,0:T(8,128)(2,1)}, bf16[2,512,3072]{2,1,0:T(8,128)(2,1)}, f32[2,512,768]{2,1,0:T(8,128)}, bf16[2,512,768]{2,1,0:T(8,128...) custom-call(s32[1]{0:T(128)} %bitcast.place_ref, ...), custom_call_target="tpu_custom_call" | custom-call | flops 14495514624 | tf_op jit(solution)/shard_map/tokens_backward/pallas_call | solution.py:527
  406.1 18.7 %weight_grads.2 = bf16[4,768,1728]{2,1,0:T(8,128)(2,1)} custom-call(s32[1]{0:T(128)} %bitcast.place_ref, bf16[1024,768]{1,0:T(8,128)(2,1)} %bitcast.137, bf16[1024,3072]{1,0:T(8,128)(2,1)} %bitcast.132, bf16[1024,768]{1,0:T(8,128)(2,1)} %bitcast.138, bf16[1024,3072]{1,0:T(8,128)(2,1)} %bitcast.131, bf16[1024,768]{1,0:T(8,128)(2,1)} %bitcast.139, ...), custom_call_target="tpu_custom_call" | custom-call | flops 14495514624 | tf_op jit(solution)/shard_map/weight_grads/pallas_call | solution.py:576
  425.9 85.5 %attention_backward.2 = (bf16[4096,192]{1,0:T(8,128)(2,1)}, bf16[4096,192]{1,0:T(8,128)(2,1)}, bf16[4096,192]{1,0:T(8,128)(2,1)}) custom-call(s32[16]{0:T(128)} %squeeze.85.low_ref, s32[16]{0:T(128)} %squeeze.86.high_ref, s32[1]{0:T(128)} %bitcast.place_ref, bf16[4096,384]{1,0:T(8,128)(2,1)} %get-tuple-element.176.q_ref, ...), custom_call_target="tpu_custom_call" | custom-call | flops 154618822656 | tf_op jit(solution)/shard_map/attention_backward/pallas_call | solution.py:342
  511.4 4.5 input_grads.7
  516.5 4.4 input_grads.6
  520.8 3.0 add_convert_fusion.1
  524.5 7.0 input_grads.8
  531.6 11.2 %projection_grads.2 = (bf16[768,576]{1,0:T(8,128)(2,1)}, f32[8,192]{1,0:T(8,128)}) custom-call(bf16[1024,768]{1,0:T(8,128)(2,1)} %bitcast.101, bf16[1024,768]{1,0:T(8,128)(2,1)} %collective-permute-done.11.p1, bf16[1024,768]{1,0:T(8,128)(2,1)} %pad_maximum_fusion.p2, bf16[1024,768]{1,0:T(8,128)(2,1)} %pad_maximum_fusion.1.p3, ...), custom_call_target="tpu_custom_call" | custom-call | flops 10871635968 | tf_op jit(solution)/shard_map/projection_grads/pallas_call | solution.py:633
  543.7 2.4 pad_maximum_fusion.2
  546.1 26.7 %collective-permute-done.24 = bf16[1024,768]{1,0:T(8,128)(2,1)} collective-permute-done((bf16[1024,768]{1,0:T(8,128)(2,1)}, bf16[1024,768]{1,0:T(8,128)(2,1)}, u32[]{:S(2)}, u32[]{:S(2)}) %collective-permute-start.24) | collective-permute-done | bytes 1572896 | tf_op jit(solution)/shard_map/ppermute | solution.py:44
  572.8 4.6 bitcast_add_fusion.1
  577.4 3.3 reduce-scatter.3.cloned.1.call-done
  580.7 1.9 convert_element_type.159
  582.5 3.9 all-to-all-start
  586.4 24.3 %tokens_backward.3 = (bf16[2,512,768]{2,1,0:T(8,128)(2,1)}, bf16[2,512,3072]{2,1,0:T(8,128)(2,1)}, f32[2,512,768]{2,1,0:T(8,128)}, bf16[2,512,768]{2,1,0:T(8,128...) custom-call(s32[1]{0:T(128)} %bitcast.place_ref, ...), custom_call_target="tpu_custom_call" | custom-call | flops 14495514624 | tf_op jit(solution)/shard_map/tokens_backward/pallas_call | solution.py:527
  615.3 18.7 %weight_grads.3 = bf16[4,768,1728]{2,1,0:T(8,128)(2,1)} custom-call(s32[1]{0:T(128)} %bitcast.place_ref, bf16[1024,768]{1,0:T(8,128)(2,1)} %bitcast.134, bf16[1024,3072]{1,0:T(8,128)(2,1)} %bitcast.130, bf16[1024,768]{1,0:T(8,128)(2,1)} %bitcast.135, bf16[1024,3072]{1,0:T(8,128)(2,1)} %bitcast.129, bf16[1024,768]{1,0:T(8,128)(2,1)} %bitcast.136, ...), custom_call_target="tpu_custom_call" | custom-call | flops 14495514624 | tf_op jit(solution)/shard_map/weight_grads/pallas_call | solution.py:576
  637.1 85.7 %attention_backward.3 = (bf16[4096,192]{1,0:T(8,128)(2,1)}, bf16[4096,192]{1,0:T(8,128)(2,1)}, bf16[4096,192]{1,0:T(8,128)(2,1)}) custom-call(s32[16]{0:T(128)} %squeeze.85.low_ref, s32[16]{0:T(128)} %squeeze.86.high_ref, s32[1]{0:T(128)} %bitcast.place_ref, bf16[4096,384]{1,0:T(8,128)(2,1)} %get-tuple-element.168.q_ref, ...), custom_call_target="tpu_custom_call" | custom-call | flops 154618822656 | tf_op jit(solution)/shard_map/attention_backward/pallas_call | solution.py:342
  722.8 4.4 input_grads.10
  728.2 4.5 input_grads.9
  732.7 2.9 add_convert_fusion
  735.6 11.6 %projection_grads.3 = (bf16[768,576]{1,0:T(8,128)(2,1)}, f32[8,192]{1,0:T(8,128)}) custom-call(bf16[1024,768]{1,0:T(8,128)(2,1)} %p0.3, bf16[1024,768]{1,0:T(8,128)(2,1)} %collective-permute-done.p1, bf16[1024,768]{1,0:T(8,128)(2,1)} %copy-done.12, bf16[1024,768]{1,0:T(8,128)(2,1)} %copy-done.11, bf16[4096,192]{1,0:T(8,128)(2,1)} %get-tuple-element.233.q_ref, ...), custom_call_target="tpu_custom_call" | custom-call | flops 10871635968 | tf_op jit(solution)/shard_map/projection_grads/pallas_call | solution.py:633
  748.5 6.9 input_grads.11
  756.9 7.8 all-to-all-start.1
  765.6 4.7 collective-permute-start.40
  772.4 25.6 %collective-permute-done.40 = f32[32,768]{1,0:T(8,128)S(1)} collective-permute-done((f32[32,768]{1,0:T(8,128)S(1)}, f32[32,768]{1,0:T(8,128)S(1)}, u32[]{:S(2)}, u32[]{:S(2)}) %collective-permute-start.40) | collective-permute-done | bytes 98336 | tf_op jit(solution)/shard_map/ppermute | solution.py:66
  797.9 11.9 %collective-permute-start.37 = (f32[32,768]{1,0:T(8,128)S(1)}, f32[32,768]{1,0:T(8,128)S(1)}, u32[]{:S(2)}, u32[]{:S(2)}) collective-permute-start(f32[32,768]{1,0:T(8,128)S(1)} %copy-done.13), channel_id=1, source_target_pairs={{0,16},{4,20},{8,24},{12,28},{16,0},{20,4},{24,8},{28,12},{1,17},{... | collective-permute-start | bytes 294920 | tf_op jit(solution)/shard_map/ppermute | solution.py:66
  809.8 2.2 collective-permute-start.36
  812.0 3.4 collective-permute-done.38
  821.4 4.7 bitcast_add_fusion
  (303 shorter events, 80.8 us)
Async XLA Ops:
  7.2 141.0 %all-gather.6.cloned.1.call-start = ((), (), s32[]{:S(2)}) async-start(), calls=%async_computation.4 | async-start | bytes 1327104 | tf_op jit(solution)/shard_map/all_gather | solution.py:808
  9.0 158.1 %all-gather.8.cloned.1.call-start = ((), (), s32[]{:S(2)}) async-start(), calls=%async_computation.7 | async-start | bytes 11354112 | tf_op jit(solution)/shard_map/all_gather | solution.py:652
  11.7 333.8 %all-gather.10.cloned.1.call-start = ((), (), s32[]{:S(2)}) async-start(), calls=%async_computation.8 | async-start | bytes 11354112 | tf_op jit(solution)/shard_map/all_gather | solution.py:652
  13.8 60.8 %collective-permute-start.10 = (f32[2,768]{1,0:T(2,128)}, f32[2,768]{1,0:T(2,128)}, u32[]{:S(2)}, u32[]{:S(2)}) collective-permute-start(f32[2,768]{1,0:T(2,128)} %get-tuple-element.367), channel_id=1, source_target_pairs={{0,3},{1,2},{2,1},{3,0},{4,7},{5,6},{6,5},{7,4},{8,11},{9,10},{10,... | collective-permute-start | bytes 18440 | tf_op jit(solution)/shard_map/ppermute | solution.py:44
  16.2 54.3 %collective-permute-start.9 = (f32[2,768]{1,0:T(2,128)}, f32[2,768]{1,0:T(2,128)}, u32[]{:S(2)}, u32[]{:S(2)}) collective-permute-start(f32[2,768]{1,0:T(2,128)} %get-tuple-element.367), channel_id=1, source_target_pairs={{0,2},{1,3},{2,0},{3,1},{4,6},{5,7},{6,4},{7,5},{8,10},{9,11},{10,... | collective-permute-start | bytes 18440 | tf_op jit(solution)/shard_map/ppermute | solution.py:44
  16.8 60.5 %collective-permute-start = (bf16[1024,768]{1,0:T(8,128)(2,1)}, bf16[1024,768]{1,0:T(8,128)(2,1)}, u32[]{:S(2)}, u32[]{:S(2)}) collective-permute-start(bf16[1024,768]{1,0:T(8,128)(2,1)} %p0.3), channel_id=1, source_target_pairs={{0,1},{1,0},{2,3},{3,2},{4,5},{5,4},{6,7},{7,6},{8,9},{9,8},{10,11... | collective-permute-start | bytes 4718600 | tf_op jit(solution)/shard_map/ppermute | solution.py:44
  17.9 52.1 %collective-permute-start.1 = (bf16[512,768]{1,0:T(8,128)(2,1)S(1)}, bf16[512,768]{1,0:T(8,128)(2,1)S(1)}, u32[]{:S(2)}, u32[]{:S(2)}) collective-permute-start(bf16[512,768]{1,0:T(8,128)(2,1)S(1)} %get-tuple-element.333), channel_id=1, source_target_pairs={{0,2},{1,3},{2,0},{3,1},{4,6},{5,7},{6,4},{7,5},{8,10},{9,11},{10,... | collective-permute-start | bytes 2359304 | tf_op jit(solution)/shard_map/ppermute | solution.py:44
  19.6 50.3 %collective-permute-start.2 = (bf16[512,768]{1,0:T(8,128)(2,1)}, bf16[512,768]{1,0:T(8,128)(2,1)S(1)}, u32[]{:S(2)}, u32[]{:S(2)}) collective-permute-start(bf16[512,768]{1,0:T(8,128)(2,1)} %get-tuple-element.332), channel_id=1, source_target_pairs={{0,2},{1,3},{2,0},{3,1},{4,6},{5,7},{6,4},{7,5},{8,10},{9,11},{10,... | collective-permute-start | bytes 2359304 | tf_op jit(solution)/shard_map/ppermute | solution.py:44
  69.9 5.5 collective-permute-start.3
  70.0 5.5 collective-permute-start.4
  70.6 4.0 collective-permute-start.8
  119.2 31.4 %collective-permute-start.5 = (bf16[512,384]{1,0:T(8,128)(2,1)S(1)}, bf16[512,384]{1,0:T(8,128)(2,1)S(1)}, u32[]{:S(2)}, u32[]{:S(2)}) collective-permute-start(bf16[512,384]{1,0:T(8,128)(2,1)S(1)} %get-tuple-element.341), channel_id=1, source_target_pairs={{0,2},{1,3},{2,0},{3,1},{4,6},{5,7},{6,4},{7,5},{8,10},{9,11},{10,... | collective-permute-start | bytes 1179656 | tf_op jit(solution)/shard_map/ppermute | solution.py:44
  119.3 36.6 %collective-permute-start.6 = (bf16[512,384]{1,0:T(8,128)(2,1)S(1)}, bf16[512,384]{1,0:T(8,128)(2,1)S(1)}, u32[]{:S(2)}, u32[]{:S(2)}) collective-permute-start(bf16[512,384]{1,0:T(8,128)(2,1)S(1)} %get-tuple-element.340), channel_id=1, source_target_pairs={{0,3},{1,2},{2,1},{3,0},{4,7},{5,6},{6,5},{7,4},{8,11},{9,10},{10,... | collective-permute-start | bytes 1179656 | tf_op jit(solution)/shard_map/ppermute | solution.py:44
  156.8 2.3 collective-permute-start.7
  195.3 20.5 %collective-permute-start.13 = (bf16[512,768]{1,0:T(8,128)(2,1)S(1)}, bf16[512,768]{1,0:T(8,128)(2,1)S(1)}, u32[]{:S(2)}, u32[]{:S(2)}) collective-permute-start(bf16[512,768]{1,0:T(8,128)(2,1)S(1)} %get-tuple-element.331), channel_id=1, source_target_pairs={{0,2},{1,3},{2,0},{3,1},{4,6},{5,7},{6,4},{7,5},{8,10},{9,11},{10,... | collective-permute-start | bytes 2359304 | tf_op jit(solution)/shard_map/ppermute | solution.py:44
  195.8 36.1 %collective-permute-start.12 = (bf16[512,768]{1,0:T(8,128)(2,1)S(1)}, bf16[512,768]{1,0:T(8,128)(2,1)S(1)}, u32[]{:S(2)}, u32[]{:S(2)}) collective-permute-start(bf16[512,768]{1,0:T(8,128)(2,1)S(1)} %get-tuple-element.330), channel_id=1, source_target_pairs={{0,2},{1,3},{2,0},{3,1},{4,6},{5,7},{6,4},{7,5},{8,10},{9,11},{10,... | collective-permute-start | bytes 2359304 | tf_op jit(solution)/shard_map/ppermute | solution.py:44
  197.4 43.3 %collective-permute-start.11 = (bf16[1024,768]{1,0:T(8,128)(2,1)S(1)}, bf16[1024,768]{1,0:T(8,128)(2,1)}, u32[]{:S(2)}, u32[]{:S(2)}) collective-permute-start(bf16[1024,768]{1,0:T(8,128)(2,1)S(1)} %bitcast.102), channel_id=1, source_target_pairs={{0,1},{1,0},{2,3},{3,2},{4,5},{5,4},{6,7},{7,6},{8,9},{9,8},{10,11... | collective-permute-start | bytes 4718600 | tf_op jit(solution)/shard_map/ppermute | solution.py:44
  215.8 22.3 %collective-permute-start.15 = (bf16[512,768]{1,0:T(8,128)(2,1)S(1)}, bf16[512,768]{1,0:T(8,128)(2,1)}, u32[]{:S(2)}, u32[]{:S(2)}) collective-permute-start(bf16[512,768]{1,0:T(8,128)(2,1)S(1)} %collective-permute-done.13), channel_id=1, source_target_pairs={{0,1},{1,0},{2,3},{3,2},{4,5},{5,4},{6,7},{7,6},{8,9},{9,8},{10,11... | collective-permute-start | bytes 2359304 | tf_op jit(solution)/shard_map/ppermute | solution.py:44
  231.9 6.2 collective-permute-start.14
  240.7 339.9 %reduce-scatter.3.cloned.1.call-start = ((), (), s32[]{:S(2)}) async-start(), calls=%async_computation.5 | async-start | bytes 11354112 | tf_op jit(solution)/shard_map/reduce_scatter | solution.py:717
  282.0 29.2 %collective-permute-start.16 = (bf16[512,384]{1,0:T(8,128)(2,1)S(1)}, bf16[512,384]{1,0:T(8,128)(2,1)S(1)}, u32[]{:S(2)}, u32[]{:S(2)}) collective-permute-start(bf16[512,384]{1,0:T(8,128)(2,1)S(1)} %get-tuple-element.337), channel_id=1, source_target_pairs={{0,2},{1,3},{2,0},{3,1},{4,6},{5,7},{6,4},{7,5},{8,10},{9,11},{10,... | collective-permute-start | bytes 1179656 | tf_op jit(solution)/shard_map/ppermute | solution.py:44
  282.1 29.1 %collective-permute-start.17 = (bf16[512,384]{1,0:T(8,128)(2,1)S(1)}, bf16[512,384]{1,0:T(8,128)(2,1)S(1)}, u32[]{:S(2)}, u32[]{:S(2)}) collective-permute-start(bf16[512,384]{1,0:T(8,128)(2,1)S(1)} %get-tuple-element.336), channel_id=1, source_target_pairs={{0,3},{1,2},{2,1},{3,0},{4,7},{5,6},{6,5},{7,4},{8,11},{9,10},{10,... | collective-permute-start | bytes 1179656 | tf_op jit(solution)/shard_map/ppermute | solution.py:44
  313.4 35.0 %collective-permute-start.18 = (bf16[512,384]{1,0:T(8,128)(2,1)S(1)}, bf16[512,384]{1,0:T(8,128)(2,1)S(1)}, u32[]{:S(2)}, u32[]{:S(2)}) collective-permute-start(bf16[512,384]{1,0:T(8,128)(2,1)S(1)} %get-tuple-element.334), channel_id=1, source_target_pairs={{0,1},{1,0},{2,3},{3,2},{4,5},{5,4},{6,7},{7,6},{8,9},{9,8},{10,11... | collective-permute-start | bytes 1179656 | tf_op jit(solution)/shard_map/ppermute | solution.py:44
  404.2 20.7 %collective-permute-start.19 = (bf16[512,384]{1,0:T(8,128)(2,1)}, bf16[512,384]{1,0:T(8,128)(2,1)S(1)}, u32[]{:S(2)}, u32[]{:S(2)}) collective-permute-start(bf16[512,384]{1,0:T(8,128)(2,1)} %get-tuple-element.178), channel_id=1, source_target_pairs={{0,1},{1,0},{2,3},{3,2},{4,5},{5,4},{6,7},{7,6},{8,9},{9,8},{10,11... | collective-permute-start | bytes 1179656 | tf_op jit(solution)/shard_map/ppermute | solution.py:44
  404.5 20.3 %collective-permute-start.20 = (bf16[512,384]{1,0:T(8,128)(2,1)}, bf16[512,384]{1,0:T(8,128)(2,1)S(1)}, u32[]{:S(2)}, u32[]{:S(2)}) collective-permute-start(bf16[512,384]{1,0:T(8,128)(2,1)} %get-tuple-element.179), channel_id=1, source_target_pairs={{0,2},{1,3},{2,0},{3,1},{4,6},{5,7},{6,4},{7,5},{8,10},{9,11},{10,... | collective-permute-start | bytes 1179656 | tf_op jit(solution)/shard_map/ppermute | solution.py:44
  405.2 19.6 %collective-permute-start.21 = (bf16[512,384]{1,0:T(8,128)(2,1)}, bf16[512,384]{1,0:T(8,128)(2,1)S(1)}, u32[]{:S(2)}, u32[]{:S(2)}) collective-permute-start(bf16[512,384]{1,0:T(8,128)(2,1)} %get-tuple-element.180), channel_id=1, source_target_pairs={{0,3},{1,2},{2,1},{3,0},{4,7},{5,6},{6,5},{7,4},{8,11},{9,10},{10,... | collective-permute-start | bytes 1179656 | tf_op jit(solution)/shard_map/ppermute | solution.py:44
  515.9 4.9 collective-permute-start.22
  523.8 49.0 %collective-permute-start.24 = (bf16[1024,768]{1,0:T(8,128)(2,1)}, bf16[1024,768]{1,0:T(8,128)(2,1)}, u32[]{:S(2)}, u32[]{:S(2)}) collective-permute-start(bf16[1024,768]{1,0:T(8,128)(2,1)} %add_convert_fusion.1), channel_id=1, source_target_pairs={{0,2},{1,3},{2,0},{3,1},{4,6},{5,7},{6,4},{7,5},{8,10},{9,11},{10,... | collective-permute-start | bytes 4718600 | tf_op jit(solution)/shard_map/ppermute | solution.py:44
  531.5 41.3 %collective-permute-start.23 = (bf16[1024,768]{1,0:T(8,128)(2,1)}, bf16[1024,768]{1,0:T(8,128)(2,1)}, u32[]{:S(2)}, u32[]{:S(2)}) collective-permute-start(bf16[1024,768]{1,0:T(8,128)(2,1)} %get-tuple-element.197), channel_id=1, source_target_pairs={{0,1},{1,0},{2,3},{3,2},{4,5},{5,4},{6,7},{7,6},{8,9},{9,8},{10,11... | collective-permute-start | bytes 4718600 | tf_op jit(solution)/shard_map/ppermute | solution.py:44
  582.5 52.7 %all-to-all-start = ((bf16[8,112,576]{2,1,0:T(8,128)(2,1)}), bf16[8,112,576]{2,1,0:T(8,128)(2,1)S(1)}, u32[]{:S(2)}, u32[]{:S(2)}) async-start(bf16[8,112,576]{2,1,0:T(8,128)(2,1)} %pad_maximum_fusion.2), calls=%async_computation.1 | async-start | bytes 2293760 | tf_op jit(solution)/shard_map/all_to_all | solution.py:711
  586.4 239.7 %reduce-scatter.5.cloned.1.call-start = ((), (), s32[]{:S(2)}) async-start(), calls=%async_computation.6 | async-start | bytes 11354112 | tf_op jit(solution)/shard_map/reduce_scatter | solution.py:717
  611.6 2.7 collective-permute-start.28
  611.6 22.4 %collective-permute-start.29 = (f32[32,768]{1,0:T(8,128)S(1)}, f32[32,768]{1,0:T(8,128)S(1)}, u32[]{:S(2)}, u32[]{:S(2)}) collective-permute-start(f32[32,768]{1,0:T(8,128)S(1)} %constant_dynamic-update-slice_fusion.4), channel_id=1, source_target_pairs={{0,2},{1,3},{2,0},{3,1},{4,6},{5,7},{6,4},{7,5},{8,10},{9,11},{10,... | collective-permute-start | bytes 294920 | tf_op jit(solution)/shard_map/ppermute | solution.py:66
  612.1 21.8 %collective-permute-start.30 = (f32[32,768]{1,0:T(8,128)S(1)}, f32[32,768]{1,0:T(8,128)S(1)}, u32[]{:S(2)}, u32[]{:S(2)}) collective-permute-start(f32[32,768]{1,0:T(8,128)S(1)} %constant_dynamic-update-slice_fusion.4), channel_id=1, source_target_pairs={{0,3},{1,2},{2,1},{3,0},{4,7},{5,6},{6,5},{7,4},{8,11},{9,10},{10,... | collective-permute-start | bytes 294920 | tf_op jit(solution)/shard_map/ppermute | solution.py:66
  613.4 20.5 %collective-permute-start.25 = (bf16[512,384]{1,0:T(8,128)(2,1)}, bf16[512,384]{1,0:T(8,128)(2,1)S(1)}, u32[]{:S(2)}, u32[]{:S(2)}) collective-permute-start(bf16[512,384]{1,0:T(8,128)(2,1)} %get-tuple-element.209), channel_id=1, source_target_pairs={{0,1},{1,0},{2,3},{3,2},{4,5},{5,4},{6,7},{7,6},{8,9},{9,8},{10,11... | collective-permute-start | bytes 1179656 | tf_op jit(solution)/shard_map/ppermute | solution.py:44
  613.7 20.3 %collective-permute-start.26 = (bf16[512,384]{1,0:T(8,128)(2,1)}, bf16[512,384]{1,0:T(8,128)(2,1)S(1)}, u32[]{:S(2)}, u32[]{:S(2)}) collective-permute-start(bf16[512,384]{1,0:T(8,128)(2,1)} %get-tuple-element.210), channel_id=1, source_target_pairs={{0,2},{1,3},{2,0},{3,1},{4,6},{5,7},{6,4},{7,5},{8,10},{9,11},{10,... | collective-permute-start | bytes 1179656 | tf_op jit(solution)/shard_map/ppermute | solution.py:44
  614.3 21.0 %collective-permute-start.27 = (bf16[512,384]{1,0:T(8,128)(2,1)}, bf16[512,384]{1,0:T(8,128)(2,1)S(1)}, u32[]{:S(2)}, u32[]{:S(2)}) collective-permute-start(bf16[512,384]{1,0:T(8,128)(2,1)} %get-tuple-element.211), channel_id=1, source_target_pairs={{0,3},{1,2},{2,1},{3,0},{4,7},{5,6},{6,5},{7,4},{8,11},{9,10},{10,... | collective-permute-start | bytes 1179656 | tf_op jit(solution)/shard_map/ppermute | solution.py:44
  727.2 5.5 collective-permute-start.31
  748.0 73.3 %collective-permute-start.33 = (bf16[1024,768]{1,0:T(8,128)(2,1)}, bf16[1024,768]{1,0:T(8,128)(2,1)}, u32[]{:S(2)}, u32[]{:S(2)}) collective-permute-start(bf16[1024,768]{1,0:T(8,128)(2,1)} %add_convert_fusion), channel_id=1, source_target_pairs={{0,2},{1,3},{2,0},{3,1},{4,6},{5,7},{6,4},{7,5},{8,10},{9,11},{10,... | collective-permute-start | bytes 4718600 | tf_op jit(solution)/shard_map/ppermute | solution.py:44
  755.4 66.0 %collective-permute-start.32 = (bf16[1024,768]{1,0:T(8,128)(2,1)}, bf16[1024,768]{1,0:T(8,128)(2,1)}, u32[]{:S(2)}, u32[]{:S(2)}) collective-permute-start(bf16[1024,768]{1,0:T(8,128)(2,1)} %get-tuple-element.240), channel_id=1, source_target_pairs={{0,1},{1,0},{2,3},{3,2},{4,5},{5,4},{6,7},{7,6},{8,9},{9,8},{10,11... | collective-permute-start | bytes 4718600 | tf_op jit(solution)/shard_map/ppermute | solution.py:44
  756.9 70.3 %all-to-all-start.1 = ((bf16[8,112,576]{2,1,0:T(8,128)(2,1)}), bf16[8,112,576]{2,1,0:T(8,128)(2,1)S(1)}, u32[]{:S(2)}, u32[]{:S(2)}) async-start(bf16[8,112,576]{2,1,0:T(8,128)(2,1)} %pad_maximum_fusion.3), calls=%async_computation.2 | async-start | bytes 2293760 | tf_op jit(solution)/shard_map/all_to_all | solution.py:738
  765.6 32.3 %collective-permute-start.40 = (f32[32,768]{1,0:T(8,128)S(1)}, f32[32,768]{1,0:T(8,128)S(1)}, u32[]{:S(2)}, u32[]{:S(2)}) collective-permute-start(f32[32,768]{1,0:T(8,128)S(1)} %copy-done.13), channel_id=1, source_target_pairs={{0,28},{4,24},{8,20},{12,16},{16,12},{20,8},{24,4},{28,0},{1,29},{... | collective-permute-start | bytes 294920 | tf_op jit(solution)/shard_map/ppermute | solution.py:66
  770.3 39.5 %collective-permute-start.39 = (f32[32,768]{1,0:T(8,128)S(1)}, f32[32,768]{1,0:T(8,128)S(1)}, u32[]{:S(2)}, u32[]{:S(2)}) collective-permute-start(f32[32,768]{1,0:T(8,128)S(1)} %copy-done.13), channel_id=1, source_target_pairs={{0,24},{4,28},{8,16},{12,20},{16,8},{20,12},{24,0},{28,4},{1,25},{... | collective-permute-start | bytes 294920 | tf_op jit(solution)/shard_map/ppermute | solution.py:66
  770.9 44.6 %collective-permute-start.38 = (f32[32,768]{1,0:T(8,128)S(1)}, f32[32,768]{1,0:T(8,128)S(1)}, u32[]{:S(2)}, u32[]{:S(2)}) collective-permute-start(f32[32,768]{1,0:T(8,128)S(1)} %copy-done.13), channel_id=1, source_target_pairs={{0,20},{4,16},{8,28},{12,24},{16,4},{20,0},{24,12},{28,8},{1,21},{... | collective-permute-start | bytes 294920 | tf_op jit(solution)/shard_map/ppermute | solution.py:66
  797.9 18.8 %collective-permute-start.37 = (f32[32,768]{1,0:T(8,128)S(1)}, f32[32,768]{1,0:T(8,128)S(1)}, u32[]{:S(2)}, u32[]{:S(2)}) collective-permute-start(f32[32,768]{1,0:T(8,128)S(1)} %copy-done.13), channel_id=1, source_target_pairs={{0,16},{4,20},{8,24},{12,28},{16,0},{20,4},{24,8},{28,12},{1,17},{... | collective-permute-start | bytes 294920 | tf_op jit(solution)/shard_map/ppermute | solution.py:66
  809.8 8.9 %collective-permute-start.36 = (f32[32,768]{1,0:T(8,128)S(1)}, f32[32,768]{1,0:T(8,128)S(1)}, u32[]{:S(2)}, u32[]{:S(2)}) collective-permute-start(f32[32,768]{1,0:T(8,128)S(1)} %copy-done.13), channel_id=1, source_target_pairs={{0,12},{4,8},{8,4},{12,0},{16,28},{20,24},{24,20},{28,16},{1,13},{... | collective-permute-start | bytes 294920 | tf_op jit(solution)/shard_map/ppermute | solution.py:66
  815.4 4.6 collective-permute-start.35
  816.7 4.6 collective-permute-start.34
  (52 other events, 1075.6 us)
Sparse Core Ops, SparseCore 0:
  10.8 52.1 all-gather.5
  66.0 101.1 all-gather.7
  240.9 104.5 all-gather.9
  425.0 155.5 reduce-scatter.2
  635.4 150.2 reduce-scatter.4

commit v5 on v4

--- a/solution.py
+++ b/solution.py
@@ -44,12 +44,14 @@
     return lax.ppermute(values, "tensor", [(i, i ^ bit) for i in range(size)])
 
 
-def gather_chunks(own):
+def gather_chunks(own, also=None):
     half = own.shape[0] // 2
     near = flip(own, 1)
     far = [flip(own[:half], 2), flip(own[half:], 2)]
+    if also is not None:
+        far, also = lax.optimization_barrier((far, also))
     last = [flip(part, 1) for part in far]
-    return own, near, jnp.concatenate(far, axis=0), jnp.concatenate(last, axis=0)
+    return (own, near, jnp.concatenate(far, axis=0), jnp.concatenate(last, axis=0)), also
 
 
 def exchange_pieces(pieces):
@@ -676,8 +678,9 @@
     far, queries = attention_forward(low, high, place, queries, keys, values, 2)
     sent = [flip(far[r], 2 + r) for r in range(2)]
     near, queries = attention_forward(low, high, place, queries, keys, values, 0)
-    near, sent, ahead = tie(near, sent, ahead)
+    near, sent = tie(near, sent)
     pieces = [near[0], flip(near[1], 1)] + sent
+    pieces, ahead = tie(pieces, ahead)
     contexts = (near, far)
     out, out_low, normed, act, slope, y1, y2, r1, r2 = tokens_forward(
         place, hidden, pieces, weights, up_bias, vectors
@@ -713,7 +716,7 @@
     packed = weight_grads(place, normed, inner, branch, act, attn, pieces)
     grads, packed, around, narrow = tie(grads, packed, around, narrow)
     if earlier is not None:
-        sums = add_up(sums, around)
+        sums = sum_over(add_up(sums, around), "dp")
     wide = lax.psum_scatter(
         packed.reshape(4 * width, -1), ("tensor", "dp"), scatter_dimension=0, tiled=True
     ).astype(f32)
@@ -736,7 +739,7 @@
         grad_in, wide, both = tie(grad_in, wide, both)
         return grad_in, wide, (sums, both)
     both = lax.all_to_all(both, "dp", 0, 0, tiled=True)
-    both, grad_in, wide, sums = tie(both, grad_in, wide, sum_over(sums, "dp"))
+    both, grad_in, wide = tie(both, grad_in, wide)
     return grad_in, wide, (sums, both, narrow)
 
 
@@ -805,7 +808,6 @@
     group3 = doc_local.shape[1]
     doc_local = jnp.pad(doc_local, ((0, 0), (0, LANES)))
     _, ask_weights = gather_all(pack_local(ask_params))
-    doc_matrix = lax.all_gather(doc_local, "dp", axis=0, tiled=True)[:, :group3]
     up_local = jnp.stack([ask_params[10], doc_params[10]])
     up_all = jnp.stack([up_local] + [flip(up_local, r) for r in range(1, 4)])
     up_all = reorder(up_all, place, 0)
@@ -816,17 +818,20 @@
     doc_pack = with_count(doc_pack, jnp.sum(valid_mask))
     all_rows = rows * lax.axis_size("dp") * lax.axis_size("tensor")
 
-    middle, middle_low, ask_saved, doc_matrix = layer_forward(
+    ask_chunks, ask_matrix = gather_chunks(tokens, ask_matrix)
+    doc_matrix = lax.all_gather(doc_local, "dp", axis=0, tiled=True)[:, :group3]
+    middle, middle_low, ask_saved, doc_pack = layer_forward(
         tokens,
-        gather_chunks(tokens),
+        ask_chunks,
         context,
         ask_params,
         ask_matrix,
         ask_weights,
         up_all[:, 0],
-        doc_matrix,
-    )
-    doc_chunks, doc_pack = tie(gather_chunks(middle_low), doc_pack)
+        doc_pack,
+    )
+    middle_low, doc_matrix = tie(middle_low, doc_matrix)
+    doc_chunks, _ = gather_chunks(middle_low)
     doc_parts, doc_weights = gather_all(doc_pack)
     final, final_low, doc_saved, _ = layer_forward(
         middle,

time: 841 us -> 834 us (level)
  waiting for transfers between devices: 144 us -> 129 us
  starting transfers between devices: 53.6 us -> 65.9 us
    ppermute x31, waiting for transfers between devices: 69 us -> 116 us  [flip(): return lax.ppermute(values, 'tensor', [(i, i ^ bit) for i in range(size)])]
    all_gather x2, waiting for transfers between devices: 39.1 us -> 0.01 us  [gather_all(): parts = lax.all_gather(local, ('tensor', 'dp'), axis=0, tiled=False)]
    ppermute x10, waiting for transfers between devices: 32.8 us -> 0.03 us  [send_around(): lax.ppermute(values, axis, [(i, i ^ step * r) for i in range(size)])]
    ppermute x31, starting transfers between devices: 18.4 us -> 35.5 us  [flip(): return lax.ppermute(values, 'tensor', [(i, i ^ bit) for i in range(size)])]
    reduce_scatter x2, waiting for transfers between devices: 3.26 us -> 13.3 us  [layer_backward(): lax.psum_scatter(packed.reshape(4 * width, -1), ('tensor', 'dp'), scatter...]
  transfers between devices with their start and end apart: 48 -> 48, of which waited for: 14 -> 13; matrix products, arithmetic and copies ran while one was open for 8% -> 7% of each run, Pallas kernels for 50% -> 54%
where the time goes in v5:
time: 834 us; the launch traced here: 828 us
  Pallas kernels  499 us (60%)
  waiting for transfers between devices  129 us (15%)
  starting transfers between devices  65.9 us (8%)
  other arithmetic  40.3 us (5%)
  blocking collectives  38.7 us (5%)
  local copies, waits for them, and re-layouts  35.8 us (4%)
  between operations  19.7 us (2%)
    pallas_call x2, Pallas kernels, attention_backward(): pl.pallas_call(body, grid_spec=pltpu.PrefetchScalarGridSpec(num_scalar_pr...  171 us
    ppermute x31, waiting for transfers between devices, flip(): return lax.ppermute(values, 'tensor', [(i, i ^ bit) for i in range(size)])  116 us
    pallas_call x4, Pallas kernels, attention_forward(): pl.pallas_call(body, grid_spec=pltpu.PrefetchScalarGridSpec(num_scalar_pr...  112 us
    pallas_call x2, Pallas kernels, tokens_forward(): pl.pallas_call(body, grid_spec=pltpu.PrefetchScalarGridSpec(num_scalar_pr...  53 us
    pallas_call x2, Pallas kernels, tokens_backward(): pl.pallas_call(body, grid_spec=pltpu.PrefetchScalarGridSpec(num_scalar_pr...  49.1 us
    all_gather x1, blocking collectives, on_device(): lax.all_gather(jnp.concatenate(ask_params[0:3], axis=1), 'dp', axis=0, ti...  38.7 us
    pallas_call x2, Pallas kernels, weight_grads(): pl.pallas_call(body, grid_spec=pltpu.PrefetchScalarGridSpec(num_scalar_pr...  37.4 us
    ppermute x31, starting transfers between devices, flip(): return lax.ppermute(values, 'tensor', [(i, i ^ bit) for i in range(size)])  35.5 us
  transfers between devices with their start and end apart: 48, of which 13 were waited for; matrix products, arithmetic and copies ran while one was open for 7% of the time, Pallas kernels for 54%

profile of v5, /device:TPU:0, one launch (start us, length us, event | category | flops | bytes accessed | tf_op | source)
XLA Modules:
  0.0 828.2 jit_solution(18205001696834742577)
XLA Ops:
  13.3 2.5 collective-permute-start.1
  23.9 38.7 %all_gather.18.mat = bf16[768,576]{1,0:T(8,128)(2,1)} all-gather(bf16[96,576]{1,0:T(8,128)(2,1)S(1)} %pad_maximum_fusion.3), channel_id=1, replica_groups=mesh['dp'=8,'tensor'=4] {'dp'}, dimensions={0}, use_global_device_ids=true | all-gather | bytes 995328 | tf_op jit(solution)/shard_map/all_gather | solution.py:804
  68.7 10.7 %project.2 = (bf16[4096,384]{1,0:T(8,128)(2,1)}, bf16[4096,384]{1,0:T(8,128)(2,1)}, bf16[4096,384]{1,0:T(8,128)(2,1)}) custom-call(bf16[1024,768]{1,0:T(8,128)(2,1)} %p0.3, bf16[1024,768]{1,0:T(8,128)(2,1)} %collective-permute-done.p1, bf16[1024,768]{1,0:T(8,128)(2,1)} %copy-done.12, bf16[1024,768]{1,0:T(8,128)(2,1)} %copy-done.10, ...), custom_call_target="tpu_custom_call" | custom-call | flops 10871635968 | tf_op jit(solution)/shard_map/project/pallas_call | solution.py:126
  79.4 35.7 %attention_forward.4 = (bf16[2,512,384]{2,1,0:T(8,128)(2,1)}, bf16[4096,384]{1,0:T(8,128)(2,1)}) custom-call(s32[16]{0:T(128)} %squeeze.85.low_ref, s32[16]{0:T(128)} %squeeze.86.high_ref, s32[1]{0:T(128)} %bitcast.place_ref, bf16[4096,384]{1,0:T(8,128)(2,1)} %get-tuple-element.151.q_ref, ...), custom_call_target="tpu_custom_call", output_to_operand_aliasing={{1}: (3, {})} | custom-call | flops 25769803776 | tf_op jit(solution)/shard_map/attention_forward/pallas_call | solution.py:220
  117.7 20.2 %attention_forward.5 = (bf16[2,512,384]{2,1,0:T(8,128)(2,1)}, bf16[4096,384]{1,0:T(8,128)(2,1)}) custom-call(s32[16]{0:T(128)} %squeeze.85.low_ref, s32[16]{0:T(128)} %squeeze.86.high_ref, s32[1]{0:T(128)} %bitcast.place_ref, bf16[4096,384]{1,0:T(8,128)(2,1)} %get-tuple-element.154.q_ref, ...), custom_call_target="tpu_custom_call", output_to_operand_aliasing={{1}: (3, {})} | custom-call | flops 25769803776 | tf_op jit(solution)/shard_map/attention_forward/pallas_call | solution.py:220
  138.0 13.0 %collective-permute-done.6.c3 = bf16[512,384]{1,0:T(8,128)(2,1)S(1)} collective-permute-done((bf16[512,384]{1,0:T(8,128)(2,1)S(1)}, bf16[512,384]{1,0:T(8,128)(2,1)S(1)}, u32[]{:S(2)}, u32[]{:S(2)}) %collective-permute-start.6) | collective-permute-done | bytes 393248 | tf_op jit(solution)/shard_map/ppermute | solution.py:44
  151.0 2.1 slice_bitcast_fusion.4
  160.7 2.5 collective-permute-start.9
  167.0 2.3 slice.267.mat
  169.2 26.2 %tokens_forward.2 = (f32[2,512,768]{2,1,0:T(8,128)}, bf16[2,512,768]{2,1,0:T(8,128)(2,1)}, bf16[2,512,768]{2,1,0:T(8,128)(2,1)}, bf16[2,512,3072]{2,1,0:T(8,128)...) custom-call(s32[1]{0:T(128)} %bitcast.place_ref, ...), custom_call_target="tpu_custom_call" | custom-call | flops 14495514624 | tf_op jit(solution)/shard_map/tokens_forward/pallas_call | solution.py:424
  199.1 22.9 %collective-permute-done.12 = bf16[512,768]{1,0:T(8,128)(2,1)S(1)} collective-permute-done((bf16[512,768]{1,0:T(8,128)(2,1)S(1)}, bf16[512,768]{1,0:T(8,128)(2,1)S(1)}, u32[]{:S(2)}, u32[]{:S(2)}) %collective-permute-start.12) | collective-permute-done | bytes 786464 | tf_op jit(solution)/shard_map/ppermute | solution.py:44
  222.1 29.7 %collective-permute-done.13 = bf16[512,768]{1,0:T(8,128)(2,1)S(1)} collective-permute-done((bf16[512,768]{1,0:T(8,128)(2,1)S(1)}, bf16[512,768]{1,0:T(8,128)(2,1)S(1)}, u32[]{:S(2)}, u32[]{:S(2)}) %collective-permute-start.13) | collective-permute-done | bytes 786464 | tf_op jit(solution)/shard_map/ppermute | solution.py:44
  252.0 2.1 collective-permute-done.15
  255.8 10.8 %project.3 = (bf16[4096,384]{1,0:T(8,128)(2,1)}, bf16[4096,384]{1,0:T(8,128)(2,1)}, bf16[4096,384]{1,0:T(8,128)(2,1)}) custom-call(bf16[1024,768]{1,0:T(8,128)(2,1)} %bitcast.97, bf16[1024,768]{1,0:T(8,128)(2,1)} %copy-done.40, bf16[1024,768]{1,0:T(8,128)(2,1)} %copy-done.13, bf16[1024,768]{1,0:T(8,128)(2,1)} %copy-done.11, bf16[768,576]{1,0:T(8,128)(2,1)} %slice.267.mat, ...), custom_call_target="tpu_custom_call" | custom-call | flops 10871635968 | tf_op jit(solution)/shard_map/project/pallas_call | solution.py:126
  266.6 35.8 %attention_forward.6 = (bf16[2,512,384]{2,1,0:T(8,128)(2,1)}, bf16[4096,384]{1,0:T(8,128)(2,1)}) custom-call(s32[16]{0:T(128)} %squeeze.85.low_ref, s32[16]{0:T(128)} %squeeze.86.high_ref, s32[1]{0:T(128)} %bitcast.place_ref, bf16[4096,384]{1,0:T(8,128)(2,1)} %get-tuple-element.168.q_ref, ...), custom_call_target="tpu_custom_call", output_to_operand_aliasing={{1}: (3, {})} | custom-call | flops 25769803776 | tf_op jit(solution)/shard_map/attention_forward/pallas_call | solution.py:220
  305.2 20.2 %attention_forward.7 = (bf16[2,512,384]{2,1,0:T(8,128)(2,1)}, bf16[4096,384]{1,0:T(8,128)(2,1)}) custom-call(s32[16]{0:T(128)} %squeeze.85.low_ref, s32[16]{0:T(128)} %squeeze.86.high_ref, s32[1]{0:T(128)} %bitcast.place_ref, bf16[4096,384]{1,0:T(8,128)(2,1)} %get-tuple-element.171.q_ref, ...), custom_call_target="tpu_custom_call", output_to_operand_aliasing={{1}: (3, {})} | custom-call | flops 25769803776 | tf_op jit(solution)/shard_map/attention_forward/pallas_call | solution.py:220
  325.5 2.2 slice_bitcast_fusion
  332.7 26.8 %tokens_forward.3 = (f32[2,512,768]{2,1,0:T(8,128)}, bf16[2,512,768]{2,1,0:T(8,128)(2,1)}, bf16[2,512,768]{2,1,0:T(8,128)(2,1)}, bf16[2,512,3072]{2,1,0:T(8,128)...) custom-call(s32[1]{0:T(128)} %bitcast.place_ref, ...), custom_call_target="tpu_custom_call" | custom-call | flops 14495514624 | tf_op jit(solution)/shard_map/tokens_forward/pallas_call | solution.py:424
  359.5 4.0 fusion.1
  363.5 24.5 %tokens_backward.2 = (bf16[2,512,768]{2,1,0:T(8,128)(2,1)}, bf16[2,512,3072]{2,1,0:T(8,128)(2,1)}, f32[2,512,768]{2,1,0:T(8,128)}, bf16[2,512,768]{2,1,0:T(8,128...) custom-call(s32[1]{0:T(128)} %bitcast.place_ref, ...), custom_call_target="tpu_custom_call" | custom-call | flops 14495514624 | tf_op jit(solution)/shard_map/tokens_backward/pallas_call | solution.py:529
  388.4 15.6 %collective-permute-start.20 = (bf16[512,384]{1,0:T(8,128)(2,1)}, bf16[512,384]{1,0:T(8,128)(2,1)S(1)}, u32[]{:S(2)}, u32[]{:S(2)}) collective-permute-start(bf16[512,384]{1,0:T(8,128)(2,1)} %get-tuple-element.194), channel_id=1, source_target_pairs={{0,2},{1,3},{2,0},{3,1},{4,6},{5,7},{6,4},{7,5},{8,10},{9,11},{10,... | collective-permute-start | bytes 1179656 | tf_op jit(solution)/shard_map/ppermute | solution.py:44
  404.0 18.8 %weight_grads.2 = bf16[4,768,1728]{2,1,0:T(8,128)(2,1)} custom-call(s32[1]{0:T(128)} %bitcast.place_ref, bf16[1024,768]{1,0:T(8,128)(2,1)} %bitcast.135, bf16[1024,3072]{1,0:T(8,128)(2,1)} %bitcast.130, bf16[1024,768]{1,0:T(8,128)(2,1)} %bitcast.136, bf16[1024,3072]{1,0:T(8,128)(2,1)} %bitcast.129, bf16[1024,768]{1,0:T(8,128)(2,1)} %bitcast.137, ...), custom_call_target="tpu_custom_call" | custom-call | flops 14495514624 | tf_op jit(solution)/shard_map/weight_grads/pallas_call | solution.py:578
  423.8 85.3 %attention_backward.2 = (bf16[4096,192]{1,0:T(8,128)(2,1)}, bf16[4096,192]{1,0:T(8,128)(2,1)}, bf16[4096,192]{1,0:T(8,128)(2,1)}) custom-call(s32[16]{0:T(128)} %squeeze.85.low_ref, s32[16]{0:T(128)} %squeeze.86.high_ref, s32[1]{0:T(128)} %bitcast.place_ref, bf16[4096,384]{1,0:T(8,128)(2,1)} %get-tuple-element.191.q_ref, ...), custom_call_target="tpu_custom_call" | custom-call | flops 154618822656 | tf_op jit(solution)/shard_map/attention_backward/pallas_call | solution.py:344
  509.2 4.5 input_grads.7
  513.7 4.3 input_grads.6
  518.1 2.9 add_convert_fusion.1
  521.0 2.1 collective-permute-start.24
  523.1 7.1 input_grads.8
  530.3 11.8 %projection_grads.2 = (bf16[768,576]{1,0:T(8,128)(2,1)}, f32[8,192]{1,0:T(8,128)}) custom-call(bf16[1024,768]{1,0:T(8,128)(2,1)} %bitcast.98, bf16[1024,768]{1,0:T(8,128)(2,1)} %copy-done.40, bf16[1024,768]{1,0:T(8,128)(2,1)} %copy-done.13, bf16[1024,768]{1,0:T(8,128)(2,1)} %copy-done.11, bf16[4096,192]{1,0:T(8,128)(2,1)} %get-tuple-element.208.q_ref, ...), custom_call_target="tpu_custom_call" | custom-call | flops 10871635968 | tf_op jit(solution)/shard_map/projection_grads/pallas_call | solution.py:635
  543.0 2.4 pad_maximum_fusion
  545.4 22.7 %collective-permute-done.24 = bf16[1024,768]{1,0:T(8,128)(2,1)} collective-permute-done((bf16[1024,768]{1,0:T(8,128)(2,1)}, bf16[1024,768]{1,0:T(8,128)(2,1)}, u32[]{:S(2)}, u32[]{:S(2)}) %collective-permute-start.24) | collective-permute-done | bytes 1572896 | tf_op jit(solution)/shard_map/ppermute | solution.py:44
  568.1 4.5 bitcast_add_fusion.1
  572.6 13.3 %reduce-scatter.3.cloned.1.call-done = bf16[96,1728]{1,0:T(8,128)(2,1)} async-done(((bf16[3072,1728]{1,0:T(8,128)(2,1)}), bf16[96,1728]{1,0:T(8,128)(2,1)}) %reduce-scatter.3.cloned.1.call-update) | async-done | bytes 331792 | tf_op jit(solution)/shard_map/reduce_scatter | solution.py:720
  587.7 4.4 all-to-all-start
  592.2 24.6 %tokens_backward.3 = (bf16[2,512,768]{2,1,0:T(8,128)(2,1)}, bf16[2,512,3072]{2,1,0:T(8,128)(2,1)}, f32[2,512,768]{2,1,0:T(8,128)}, bf16[2,512,768]{2,1,0:T(8,128...) custom-call(s32[1]{0:T(128)} %bitcast.place_ref, ...), custom_call_target="tpu_custom_call" | custom-call | flops 14495514624 | tf_op jit(solution)/shard_map/tokens_backward/pallas_call | solution.py:529
  621.3 18.6 %weight_grads.3 = bf16[4,768,1728]{2,1,0:T(8,128)(2,1)} custom-call(s32[1]{0:T(128)} %bitcast.place_ref, bf16[1024,768]{1,0:T(8,128)(2,1)} %bitcast.132, bf16[1024,3072]{1,0:T(8,128)(2,1)} %bitcast.128, bf16[1024,768]{1,0:T(8,128)(2,1)} %bitcast.133, bf16[1024,3072]{1,0:T(8,128)(2,1)} %bitcast.127, bf16[1024,768]{1,0:T(8,128)(2,1)} %bitcast.134, ...), custom_call_target="tpu_custom_call" | custom-call | flops 14495514624 | tf_op jit(solution)/shard_map/weight_grads/pallas_call | solution.py:578
  642.0 4.7 collective-permute-start.37
  649.7 2.3 collective-permute-start.33
  652.0 7.2 collective-permute-start.32
  660.7 85.8 %attention_backward.3 = (bf16[4096,192]{1,0:T(8,128)(2,1)}, bf16[4096,192]{1,0:T(8,128)(2,1)}, bf16[4096,192]{1,0:T(8,128)(2,1)}) custom-call(s32[16]{0:T(128)} %squeeze.85.low_ref, s32[16]{0:T(128)} %squeeze.86.high_ref, s32[1]{0:T(128)} %bitcast.place_ref, bf16[4096,384]{1,0:T(8,128)(2,1)} %get-tuple-element.183.q_ref, ...), custom_call_target="tpu_custom_call" | custom-call | flops 154618822656 | tf_op jit(solution)/shard_map/attention_backward/pallas_call | solution.py:344
  747.9 4.4 input_grads.10
  753.1 4.5 input_grads.9
  757.6 2.9 add_convert_fusion
  760.5 11.1 %projection_grads.3 = (bf16[768,576]{1,0:T(8,128)(2,1)}, f32[8,192]{1,0:T(8,128)}) custom-call(bf16[1024,768]{1,0:T(8,128)(2,1)} %p0.3, bf16[1024,768]{1,0:T(8,128)(2,1)} %collective-permute-done.p1, bf16[1024,768]{1,0:T(8,128)(2,1)} %copy-done.12, bf16[1024,768]{1,0:T(8,128)(2,1)} %copy-done.10, bf16[4096,192]{1,0:T(8,128)(2,1)} %get-tuple-element.248.q_ref, ...), custom_call_target="tpu_custom_call" | custom-call | flops 10871635968 | tf_op jit(solution)/shard_map/projection_grads/pallas_call | solution.py:635
  773.3 6.9 input_grads.11
  782.0 4.7 all-to-all-start.1
  790.9 21.0 %collective-permute-done.40 = bf16[1024,768]{1,0:T(8,128)(2,1)} collective-permute-done((bf16[1024,768]{1,0:T(8,128)(2,1)}, bf16[1024,768]{1,0:T(8,128)(2,1)}, u32[]{:S(2)}, u32[]{:S(2)}) %collective-permute-start.40) | collective-permute-done | bytes 1572896 | tf_op jit(solution)/shard_map/ppermute | solution.py:44
  811.9 5.2 bitcast_add_fusion
  (307 shorter events, 72.2 us)
Async XLA Ops:
  7.2 159.7 %all-gather.6.cloned.1.call-start = ((), (), s32[]{:S(2)}) async-start(), calls=%async_computation.4 | async-start | bytes 1327104 | tf_op jit(solution)/shard_map/all_gather | solution.py:822
  9.0 160.2 %all-gather.8.cloned.1.call-start = ((), (), s32[]{:S(2)}) async-start(), calls=%async_computation.7 | async-start | bytes 11354112 | tf_op jit(solution)/shard_map/all_gather | solution.py:654
  11.7 317.9 %all-gather.10.cloned.1.call-start = ((), (), s32[]{:S(2)}) async-start(), calls=%async_computation.8 | async-start | bytes 11354112 | tf_op jit(solution)/shard_map/all_gather | solution.py:654
  11.8 55.8 %collective-permute-start = (bf16[1024,768]{1,0:T(8,128)(2,1)}, bf16[1024,768]{1,0:T(8,128)(2,1)}, u32[]{:S(2)}, u32[]{:S(2)}) collective-permute-start(bf16[1024,768]{1,0:T(8,128)(2,1)} %p0.3), channel_id=1, source_target_pairs={{0,1},{1,0},{2,3},{3,2},{4,5},{5,4},{6,7},{7,6},{8,9},{9,8},{10,11... | collective-permute-start | bytes 4718600 | tf_op jit(solution)/shard_map/ppermute | solution.py:44
  13.3 49.3 %collective-permute-start.1 = (bf16[512,768]{1,0:T(8,128)(2,1)}, bf16[512,768]{1,0:T(8,128)(2,1)S(1)}, u32[]{:S(2)}, u32[]{:S(2)}) collective-permute-start(bf16[512,768]{1,0:T(8,128)(2,1)} %get-tuple-element.347), channel_id=1, source_target_pairs={{0,2},{1,3},{2,0},{3,1},{4,6},{5,7},{6,4},{7,5},{8,10},{9,11},{10,... | collective-permute-start | bytes 2359304 | tf_op jit(solution)/shard_map/ppermute | solution.py:44
  15.9 46.8 %collective-permute-start.2 = (bf16[512,768]{1,0:T(8,128)(2,1)S(1)}, bf16[512,768]{1,0:T(8,128)(2,1)S(1)}, u32[]{:S(2)}, u32[]{:S(2)}) collective-permute-start(bf16[512,768]{1,0:T(8,128)(2,1)S(1)} %get-tuple-element.346), channel_id=1, source_target_pairs={{0,2},{1,3},{2,0},{3,1},{4,6},{5,7},{6,4},{7,5},{8,10},{9,11},{10,... | collective-permute-start | bytes 2359304 | tf_op jit(solution)/shard_map/ppermute | solution.py:44
  62.6 3.2 collective-permute-start.3
  62.7 3.5 collective-permute-start.4
  116.3 21.8 %collective-permute-start.5 = (bf16[512,384]{1,0:T(8,128)(2,1)S(1)}, bf16[512,384]{1,0:T(8,128)(2,1)S(1)}, u32[]{:S(2)}, u32[]{:S(2)}) collective-permute-start(bf16[512,384]{1,0:T(8,128)(2,1)S(1)} %get-tuple-element.355), channel_id=1, source_target_pairs={{0,2},{1,3},{2,0},{3,1},{4,6},{5,7},{6,4},{7,5},{8,10},{9,11},{10,... | collective-permute-start | bytes 1179656 | tf_op jit(solution)/shard_map/ppermute | solution.py:44
  116.3 34.6 %collective-permute-start.6 = (bf16[512,384]{1,0:T(8,128)(2,1)S(1)}, bf16[512,384]{1,0:T(8,128)(2,1)S(1)}, u32[]{:S(2)}, u32[]{:S(2)}) collective-permute-start(bf16[512,384]{1,0:T(8,128)(2,1)S(1)} %get-tuple-element.354), channel_id=1, source_target_pairs={{0,3},{1,2},{2,1},{3,0},{4,7},{5,6},{6,5},{7,4},{8,11},{9,10},{10,... | collective-permute-start | bytes 1179656 | tf_op jit(solution)/shard_map/ppermute | solution.py:44
  153.1 6.9 collective-permute-start.7
  160.0 425.8 %reduce-scatter.3.cloned.1.call-start = ((), (), s32[]{:S(2)}) async-start(), calls=%async_computation.5 | async-start | bytes 11354112 | tf_op jit(solution)/shard_map/reduce_scatter | solution.py:720
  160.7 4.1 collective-permute-start.9
  163.1 1.6 collective-permute-start.8
  163.2 3.1 collective-permute-start.10
  197.0 25.0 %collective-permute-start.12 = (bf16[512,768]{1,0:T(8,128)(2,1)S(1)}, bf16[512,768]{1,0:T(8,128)(2,1)S(1)}, u32[]{:S(2)}, u32[]{:S(2)}) collective-permute-start(bf16[512,768]{1,0:T(8,128)(2,1)S(1)} %get-tuple-element.345), channel_id=1, source_target_pairs={{0,2},{1,3},{2,0},{3,1},{4,6},{5,7},{6,4},{7,5},{8,10},{9,11},{10,... | collective-permute-start | bytes 2359304 | tf_op jit(solution)/shard_map/ppermute | solution.py:44
  197.7 54.1 %collective-permute-start.13 = (bf16[512,768]{1,0:T(8,128)(2,1)S(1)}, bf16[512,768]{1,0:T(8,128)(2,1)S(1)}, u32[]{:S(2)}, u32[]{:S(2)}) collective-permute-start(bf16[512,768]{1,0:T(8,128)(2,1)S(1)} %get-tuple-element.344), channel_id=1, source_target_pairs={{0,2},{1,3},{2,0},{3,1},{4,6},{5,7},{6,4},{7,5},{8,10},{9,11},{10,... | collective-permute-start | bytes 2359304 | tf_op jit(solution)/shard_map/ppermute | solution.py:44
  199.1 55.0 %collective-permute-start.11 = (bf16[1024,768]{1,0:T(8,128)(2,1)S(1)}, bf16[1024,768]{1,0:T(8,128)(2,1)S(1)}, u32[]{:S(2)}, u32[]{:S(2)}) collective-permute-start(bf16[1024,768]{1,0:T(8,128)(2,1)S(1)} %bitcast.99), channel_id=1, source_target_pairs={{0,1},{1,0},{2,3},{3,2},{4,5},{5,4},{6,7},{7,6},{8,9},{9,8},{10,11... | collective-permute-start | bytes 4718600 | tf_op jit(solution)/shard_map/ppermute | solution.py:44
  222.1 29.8 %collective-permute-start.14 = (bf16[512,768]{1,0:T(8,128)(2,1)S(1)}, bf16[512,768]{1,0:T(8,128)(2,1)S(1)}, u32[]{:S(2)}, u32[]{:S(2)}) collective-permute-start(bf16[512,768]{1,0:T(8,128)(2,1)S(1)} %collective-permute-done.12), channel_id=1, source_target_pairs={{0,1},{1,0},{2,3},{3,2},{4,5},{5,4},{6,7},{7,6},{8,9},{9,8},{10,11... | collective-permute-start | bytes 2359304 | tf_op jit(solution)/shard_map/ppermute | solution.py:44
  251.8 2.3 collective-permute-start.15
  303.5 21.9 %collective-permute-start.16 = (bf16[512,384]{1,0:T(8,128)(2,1)S(1)}, bf16[512,384]{1,0:T(8,128)(2,1)S(1)}, u32[]{:S(2)}, u32[]{:S(2)}) collective-permute-start(bf16[512,384]{1,0:T(8,128)(2,1)S(1)} %get-tuple-element.351), channel_id=1, source_target_pairs={{0,2},{1,3},{2,0},{3,1},{4,6},{5,7},{6,4},{7,5},{8,10},{9,11},{10,... | collective-permute-start | bytes 1179656 | tf_op jit(solution)/shard_map/ppermute | solution.py:44
  303.6 21.8 %collective-permute-start.17 = (bf16[512,384]{1,0:T(8,128)(2,1)S(1)}, bf16[512,384]{1,0:T(8,128)(2,1)S(1)}, u32[]{:S(2)}, u32[]{:S(2)}) collective-permute-start(bf16[512,384]{1,0:T(8,128)(2,1)S(1)} %get-tuple-element.350), channel_id=1, source_target_pairs={{0,3},{1,2},{2,1},{3,0},{4,7},{5,6},{6,5},{7,4},{8,11},{9,10},{10,... | collective-permute-start | bytes 1179656 | tf_op jit(solution)/shard_map/ppermute | solution.py:44
  327.7 1.9 collective-permute-start.18
  388.0 34.8 %collective-permute-start.19 = (bf16[512,384]{1,0:T(8,128)(2,1)}, bf16[512,384]{1,0:T(8,128)(2,1)S(1)}, u32[]{:S(2)}, u32[]{:S(2)}) collective-permute-start(bf16[512,384]{1,0:T(8,128)(2,1)} %get-tuple-element.193), channel_id=1, source_target_pairs={{0,1},{1,0},{2,3},{3,2},{4,5},{5,4},{6,7},{7,6},{8,9},{9,8},{10,11... | collective-permute-start | bytes 1179656 | tf_op jit(solution)/shard_map/ppermute | solution.py:44
  388.4 34.4 %collective-permute-start.20 = (bf16[512,384]{1,0:T(8,128)(2,1)}, bf16[512,384]{1,0:T(8,128)(2,1)S(1)}, u32[]{:S(2)}, u32[]{:S(2)}) collective-permute-start(bf16[512,384]{1,0:T(8,128)(2,1)} %get-tuple-element.194), channel_id=1, source_target_pairs={{0,2},{1,3},{2,0},{3,1},{4,6},{5,7},{6,4},{7,5},{8,10},{9,11},{10,... | collective-permute-start | bytes 1179656 | tf_op jit(solution)/shard_map/ppermute | solution.py:44
  404.0 18.8 %collective-permute-start.21 = (bf16[512,384]{1,0:T(8,128)(2,1)}, bf16[512,384]{1,0:T(8,128)(2,1)S(1)}, u32[]{:S(2)}, u32[]{:S(2)}) collective-permute-start(bf16[512,384]{1,0:T(8,128)(2,1)} %get-tuple-element.195), channel_id=1, source_target_pairs={{0,3},{1,2},{2,1},{3,0},{4,7},{5,6},{6,5},{7,4},{8,11},{9,10},{10,... | collective-permute-start | bytes 1179656 | tf_op jit(solution)/shard_map/ppermute | solution.py:44
  513.6 4.4 collective-permute-start.22
  521.0 47.1 %collective-permute-start.24 = (bf16[1024,768]{1,0:T(8,128)(2,1)}, bf16[1024,768]{1,0:T(8,128)(2,1)}, u32[]{:S(2)}, u32[]{:S(2)}) collective-permute-start(bf16[1024,768]{1,0:T(8,128)(2,1)} %add_convert_fusion.1), channel_id=1, source_target_pairs={{0,2},{1,3},{2,0},{3,1},{4,6},{5,7},{6,4},{7,5},{8,10},{9,11},{10,... | collective-permute-start | bytes 4718600 | tf_op jit(solution)/shard_map/ppermute | solution.py:44
  530.2 37.9 %collective-permute-start.23 = (bf16[1024,768]{1,0:T(8,128)(2,1)}, bf16[1024,768]{1,0:T(8,128)(2,1)}, u32[]{:S(2)}, u32[]{:S(2)}) collective-permute-start(bf16[1024,768]{1,0:T(8,128)(2,1)} %get-tuple-element.212), channel_id=1, source_target_pairs={{0,1},{1,0},{2,3},{3,2},{4,5},{5,4},{6,7},{7,6},{8,9},{9,8},{10,11... | collective-permute-start | bytes 4718600 | tf_op jit(solution)/shard_map/ppermute | solution.py:44
  587.7 53.5 %all-to-all-start = ((bf16[8,112,576]{2,1,0:T(8,128)(2,1)}), bf16[8,112,576]{2,1,0:T(8,128)(2,1)S(1)}, u32[]{:S(2)}, u32[]{:S(2)}) async-start(bf16[8,112,576]{2,1,0:T(8,128)(2,1)} %pad_maximum_fusion), calls=%async_computation.1 | async-start | bytes 2293760 | tf_op jit(solution)/shard_map/all_to_all | solution.py:714
  592.1 225.0 %reduce-scatter.5.cloned.1.call-start = ((), (), s32[]{:S(2)}) async-start(), calls=%async_computation.6 | async-start | bytes 11354112 | tf_op jit(solution)/shard_map/reduce_scatter | solution.py:720
  617.6 2.8 collective-permute-start.28
  617.6 22.4 %collective-permute-start.29 = (f32[32,768]{1,0:T(8,128)S(1)}, f32[32,768]{1,0:T(8,128)S(1)}, u32[]{:S(2)}, u32[]{:S(2)}) collective-permute-start(f32[32,768]{1,0:T(8,128)S(1)} %constant_dynamic-update-slice_fusion.8), channel_id=1, source_target_pairs={{0,2},{1,3},{2,0},{3,1},{4,6},{5,7},{6,4},{7,5},{8,10},{9,11},{10,... | collective-permute-start | bytes 294920 | tf_op jit(solution)/shard_map/ppermute | solution.py:68
  618.3 21.7 %collective-permute-start.30 = (f32[32,768]{1,0:T(8,128)S(1)}, f32[32,768]{1,0:T(8,128)S(1)}, u32[]{:S(2)}, u32[]{:S(2)}) collective-permute-start(f32[32,768]{1,0:T(8,128)S(1)} %constant_dynamic-update-slice_fusion.8), channel_id=1, source_target_pairs={{0,3},{1,2},{2,1},{3,0},{4,7},{5,6},{6,5},{7,4},{8,11},{9,10},{10,... | collective-permute-start | bytes 294920 | tf_op jit(solution)/shard_map/ppermute | solution.py:68
  619.4 20.5 %collective-permute-start.25 = (bf16[512,384]{1,0:T(8,128)(2,1)}, bf16[512,384]{1,0:T(8,128)(2,1)S(1)}, u32[]{:S(2)}, u32[]{:S(2)}) collective-permute-start(bf16[512,384]{1,0:T(8,128)(2,1)} %get-tuple-element.224), channel_id=1, source_target_pairs={{0,1},{1,0},{2,3},{3,2},{4,5},{5,4},{6,7},{7,6},{8,9},{9,8},{10,11... | collective-permute-start | bytes 1179656 | tf_op jit(solution)/shard_map/ppermute | solution.py:44
  619.7 20.3 %collective-permute-start.26 = (bf16[512,384]{1,0:T(8,128)(2,1)}, bf16[512,384]{1,0:T(8,128)(2,1)S(1)}, u32[]{:S(2)}, u32[]{:S(2)}) collective-permute-start(bf16[512,384]{1,0:T(8,128)(2,1)} %get-tuple-element.225), channel_id=1, source_target_pairs={{0,2},{1,3},{2,0},{3,1},{4,6},{5,7},{6,4},{7,5},{8,10},{9,11},{10,... | collective-permute-start | bytes 1179656 | tf_op jit(solution)/shard_map/ppermute | solution.py:44
  620.4 20.9 %collective-permute-start.27 = (bf16[512,384]{1,0:T(8,128)(2,1)}, bf16[512,384]{1,0:T(8,128)(2,1)S(1)}, u32[]{:S(2)}, u32[]{:S(2)}) collective-permute-start(bf16[512,384]{1,0:T(8,128)(2,1)} %get-tuple-element.226), channel_id=1, source_target_pairs={{0,3},{1,2},{2,1},{3,0},{4,7},{5,6},{6,5},{7,4},{8,11},{9,10},{10,... | collective-permute-start | bytes 1179656 | tf_op jit(solution)/shard_map/ppermute | solution.py:44
  642.0 10.0 %collective-permute-start.37 = (f32[32,768]{1,0:T(8,128)}, f32[32,768]{1,0:T(8,128)S(1)}, u32[]{:S(2)}, u32[]{:S(2)}) collective-permute-start(f32[32,768]{1,0:T(8,128)} %add_add_fusion.1), channel_id=1, source_target_pairs={{0,28},{4,24},{8,20},{12,16},{16,12},{20,8},{24,4},{28,0},{1,29},{... | collective-permute-start | bytes 294920 | tf_op jit(solution)/shard_map/ppermute | solution.py:68
  646.7 12.5 %collective-permute-start.36 = (f32[32,768]{1,0:T(8,128)}, f32[32,768]{1,0:T(8,128)S(1)}, u32[]{:S(2)}, u32[]{:S(2)}) collective-permute-start(f32[32,768]{1,0:T(8,128)} %add_add_fusion.1), channel_id=1, source_target_pairs={{0,24},{4,28},{8,16},{12,20},{16,8},{20,12},{24,0},{28,4},{1,25},{... | collective-permute-start | bytes 294920 | tf_op jit(solution)/shard_map/ppermute | solution.py:68
  647.2 99.3 %collective-permute-start.35 = (f32[32,768]{1,0:T(8,128)}, f32[32,768]{1,0:T(8,128)}, u32[]{:S(2)}, u32[]{:S(2)}) collective-permute-start(f32[32,768]{1,0:T(8,128)} %add_add_fusion.1), channel_id=1, source_target_pairs={{0,20},{4,16},{8,28},{12,24},{16,4},{20,0},{24,12},{28,8},{1,21},{... | collective-permute-start | bytes 294920 | tf_op jit(solution)/shard_map/ppermute | solution.py:68
  647.8 98.8 %collective-permute-start.34 = (f32[32,768]{1,0:T(8,128)}, f32[32,768]{1,0:T(8,128)}, u32[]{:S(2)}, u32[]{:S(2)}) collective-permute-start(f32[32,768]{1,0:T(8,128)} %add_add_fusion.1), channel_id=1, source_target_pairs={{0,16},{4,20},{8,24},{12,28},{16,0},{20,4},{24,8},{28,12},{1,17},{... | collective-permute-start | bytes 294920 | tf_op jit(solution)/shard_map/ppermute | solution.py:68
  649.7 96.9 %collective-permute-start.33 = (f32[32,768]{1,0:T(8,128)}, f32[32,768]{1,0:T(8,128)}, u32[]{:S(2)}, u32[]{:S(2)}) collective-permute-start(f32[32,768]{1,0:T(8,128)} %add_add_fusion.1), channel_id=1, source_target_pairs={{0,12},{4,8},{8,4},{12,0},{16,28},{20,24},{24,20},{28,16},{1,13},{... | collective-permute-start | bytes 294920 | tf_op jit(solution)/shard_map/ppermute | solution.py:68
  652.0 94.5 %collective-permute-start.32 = (f32[32,768]{1,0:T(8,128)}, f32[32,768]{1,0:T(8,128)}, u32[]{:S(2)}, u32[]{:S(2)}) collective-permute-start(f32[32,768]{1,0:T(8,128)} %add_add_fusion.1), channel_id=1, source_target_pairs={{0,8},{4,12},{8,0},{12,4},{16,24},{20,28},{24,16},{28,20},{1,9},{5... | collective-permute-start | bytes 294920 | tf_op jit(solution)/shard_map/ppermute | solution.py:68
  659.2 87.4 %collective-permute-start.31 = (f32[32,768]{1,0:T(8,128)}, f32[32,768]{1,0:T(8,128)}, u32[]{:S(2)}, u32[]{:S(2)}) collective-permute-start(f32[32,768]{1,0:T(8,128)} %add_add_fusion.1), channel_id=1, source_target_pairs={{0,4},{4,0},{8,12},{12,8},{16,20},{20,16},{24,28},{28,24},{1,5},{5... | collective-permute-start | bytes 294920 | tf_op jit(solution)/shard_map/ppermute | solution.py:68
  752.2 5.3 collective-permute-start.38
  772.4 39.5 %collective-permute-start.40 = (bf16[1024,768]{1,0:T(8,128)(2,1)}, bf16[1024,768]{1,0:T(8,128)(2,1)}, u32[]{:S(2)}, u32[]{:S(2)}) collective-permute-start(bf16[1024,768]{1,0:T(8,128)(2,1)} %add_convert_fusion), channel_id=1, source_target_pairs={{0,2},{1,3},{2,0},{3,1},{4,6},{5,7},{6,4},{7,5},{8,10},{9,11},{10,... | collective-permute-start | bytes 4718600 | tf_op jit(solution)/shard_map/ppermute | solution.py:44
  780.3 31.6 %collective-permute-start.39 = (bf16[1024,768]{1,0:T(8,128)(2,1)}, bf16[1024,768]{1,0:T(8,128)(2,1)}, u32[]{:S(2)}, u32[]{:S(2)}) collective-permute-start(bf16[1024,768]{1,0:T(8,128)(2,1)} %get-tuple-element.255), channel_id=1, source_target_pairs={{0,1},{1,0},{2,3},{3,2},{4,5},{5,4},{6,7},{7,6},{8,9},{9,8},{10,11... | collective-permute-start | bytes 4718600 | tf_op jit(solution)/shard_map/ppermute | solution.py:44
  782.0 36.4 %all-to-all-start.1 = ((bf16[8,112,576]{2,1,0:T(8,128)(2,1)}), bf16[8,112,576]{2,1,0:T(8,128)(2,1)S(1)}, u32[]{:S(2)}, u32[]{:S(2)}) async-start(bf16[8,112,576]{2,1,0:T(8,128)(2,1)} %pad_maximum_fusion.1), calls=%async_computation.2 | async-start | bytes 2293760 | tf_op jit(solution)/shard_map/all_to_all | solution.py:741
  (53 other events, 1014.5 us)
Sparse Core Ops, SparseCore 0:
  10.8 51.6 all-gather.5
  65.5 100.6 all-gather.7
  169.2 103.9 all-gather.9
  423.0 162.8 reduce-scatter.2
  652.1 145.5 reduce-scatter.4

commit v6 on v4

--- a/solution.py
+++ b/solution.py
@@ -133,7 +133,7 @@
     )(*pieces, matrix, query_bias[None], value_bias[None], query_marks, key_marks)
 
 
-def attention_forward(low, high, place, queries, keys, values, base):
+def attention_forward(low, high, place, queries, keys, values):
     rows, wide = queries.shape
     heads = wide // LANES
     count = rows // TILE
@@ -141,11 +141,10 @@
     half = rows // 8
     half_blocks = half // TILE
     group = heads * HEAD_DIM
-    skip = base * per_chunk
 
     def body(low_ref, high_ref, place_ref, q_ref, k_ref, v_ref, ctx_ref, ql_ref, *scratch):
         peak, fade, total, score = scratch
-        block = pl.program_id(0) + skip
+        block = pl.program_id(0)
         own = place_ref[0]
         first = low_ref[block]
         last = high_ref[block]
@@ -214,12 +213,12 @@
         def _():
             ctx_ref[0, pl.ds(at, TILE), group : 2 * group] = ctx
 
-    row_spec = pl.BlockSpec((TILE, wide), lambda i, *_: (i + skip, 0))
+    row_spec = pl.BlockSpec((TILE, wide), lambda i, *_: (i, 0))
     return pl.pallas_call(
         body,
         grid_spec=pltpu.PrefetchScalarGridSpec(
             num_scalar_prefetch=3,
-            grid=(count // 2,),
+            grid=(count,),
             in_specs=[row_spec, WHOLE, WHOLE],
             out_specs=[
                 pl.BlockSpec((1, half, 2 * group), lambda i, *_: (i // per_chunk, 0, 0)),
@@ -233,12 +232,11 @@
             ],
         ),
         out_shape=[
-            jax.ShapeDtypeStruct((2, half, 2 * group), bf16),
+            jax.ShapeDtypeStruct((4, half, 2 * group), bf16),
             jax.ShapeDtypeStruct((rows, wide), bf16),
         ],
         compiler_params=kernel_params(),
-        input_output_aliases={3: 1},
-        cost_estimate=cost(4 * rows * rows * wide),
+        cost_estimate=cost(12 * rows * rows * wide),
         name="attention_forward",
     )(low, high, place, queries, keys, values)
 
@@ -252,7 +250,7 @@
     half_blocks = half // TILE
     group = heads * HEAD_DIM
 
-    def body(low_ref, high_ref, place_ref, q_ref, k_ref, v_ref, near, far, g0, g1, g2, g3, *rest):
+    def body(low_ref, high_ref, place_ref, q_ref, k_ref, v_ref, c_ref, g0, g1, g2, g3, *rest):
         dq_ref, dk_ref, dv_ref, do_all, dq_all, acc_k, acc_v, prob, slope = rest
         block = pl.program_id(0)
         own = place_ref[0]
@@ -264,14 +262,13 @@
             dq_all[...] = jnp.zeros_like(dq_all)
             lane = lax.broadcasted_iota(jnp.int32, (TILE, HEAD_DIM), 1)
             for chunk, g_ref in enumerate((g0, g1, g2, g3)):
-                c_ref = (near, far)[chunk // 2]
-
-                def prepare(b, carry, chunk=chunk, g_ref=g_ref, c_ref=c_ref):
+
+                def prepare(b, carry, chunk=chunk, g_ref=g_ref):
                     at = pl.multiple_of(b * TILE, TILE)
                     for side in range(2):
                         cols = slice(side * group, (side + 1) * group)
                         row = pl.multiple_of((2 * chunk + side) * half + at, TILE)
-                        c = c_ref[chunk % 2, pl.ds(at, TILE), cols].astype(f32)
+                        c = c_ref[chunk, pl.ds(at, TILE), cols].astype(f32)
                         g = g_ref[pl.ds(at, TILE), cols].astype(f32)
                         for h in range(heads):
                             lo = h * HEAD_DIM
@@ -344,7 +341,7 @@
         grid_spec=pltpu.PrefetchScalarGridSpec(
             num_scalar_prefetch=3,
             grid=(count,),
-            in_specs=[WHOLE, row_spec, row_spec] + [WHOLE] * 6,
+            in_specs=[WHOLE, row_spec, row_spec] + [WHOLE] * 5,
             out_specs=[WHOLE, out_spec, out_spec],
             scratch_shapes=[
                 pltpu.VMEM((rows, wide), bf16),
@@ -359,7 +356,7 @@
         compiler_params=kernel_params(),
         cost_estimate=cost(24 * rows * rows * wide),
         name="attention_backward",
-    )(low, high, place, queries, keys, values, *contexts, *grads)
+    )(low, high, place, queries, keys, values, contexts, *grads)
 
 
 SQRT_HALF = 0.7071067811865476
@@ -673,12 +670,9 @@
     queries, keys, values = project(
         chunks, matrix, params[3], params[4], query_marks, key_marks
     )
-    far, queries = attention_forward(low, high, place, queries, keys, values, 2)
-    sent = [flip(far[r], 2 + r) for r in range(2)]
-    near, queries = attention_forward(low, high, place, queries, keys, values, 0)
-    near, sent, ahead = tie(near, sent, ahead)
-    pieces = [near[0], flip(near[1], 1)] + sent
-    contexts = (near, far)
+    contexts, queries = attention_forward(low, high, place, queries, keys, values)
+    contexts, ahead = tie(contexts, ahead)
+    pieces = exchange_pieces([contexts[r] for r in range(4)])
     out, out_low, normed, act, slope, y1, y2, r1, r2 = tokens_forward(
         place, hidden, pieces, weights, up_bias, vectors
     )
@@ -713,7 +707,7 @@
     packed = weight_grads(place, normed, inner, branch, act, attn, pieces)
     grads, packed, around, narrow = tie(grads, packed, around, narrow)
     if earlier is not None:
-        sums = add_up(sums, around)
+        sums = sum_over(add_up(sums, around), "dp")
     wide = lax.psum_scatter(
         packed.reshape(4 * width, -1), ("tensor", "dp"), scatter_dimension=0, tiled=True
     ).astype(f32)
@@ -736,7 +730,7 @@
         grad_in, wide, both = tie(grad_in, wide, both)
         return grad_in, wide, (sums, both)
     both = lax.all_to_all(both, "dp", 0, 0, tiled=True)
-    both, grad_in, wide, sums = tie(both, grad_in, wide, sum_over(sums, "dp"))
+    both, grad_in, wide = tie(both, grad_in, wide)
     return grad_in, wide, (sums, both, narrow)
 
 

time: 841 us -> 826 us (0.982)
  Pallas kernels: 499 us -> 488 us
    ppermute x10, waiting for transfers between devices: 32.8 us -> 0.03 us  [send_around(): lax.ppermute(values, axis, [(i, i ^ step * r) for i in range(size)])]
    ppermute x31, waiting for transfers between devices: 69 us -> 98.8 us  [flip(): return lax.ppermute(values, 'tensor', [(i, i ^ bit) for i in range(size)])]
    all_gather x2, waiting for transfers between devices: 39.1 us -> 24.6 us  [gather_all(): parts = lax.all_gather(local, ('tensor', 'dp'), axis=0, tiled=False)]
    reduce_scatter x2, waiting for transfers between devices: 3.26 us -> 16.4 us  [layer_backward(): lax.psum_scatter(packed.reshape(4 * width, -1), ('tensor', 'dp'), scatter...]
    pallas_call x4 -> x2, Pallas kernels: 112 us -> 103 us  [attention_forward(): pl.pallas_call(body, grid_spec=pltpu.PrefetchScalarGridSpec(num_scalar_pr...]
  transfers between devices with their start and end apart: 48 -> 48, of which waited for: 14 -> 10; matrix products, arithmetic and copies ran while one was open for 8% -> 8% of each run, Pallas kernels for 50% -> 50%
where the time goes in v6:
time: 826 us; the launch traced here: 818 us
  Pallas kernels  488 us (59%)
  waiting for transfers between devices  141 us (17%)
  starting transfers between devices  47.1 us (6%)
  other arithmetic  45.9 us (6%)
  blocking collectives  38.4 us (5%)
  local copies, waits for them, and re-layouts  38 us (5%)
  between operations  19.9 us (2%)
    pallas_call x2, Pallas kernels, attention_backward(): pl.pallas_call(body, grid_spec=pltpu.PrefetchScalarGridSpec(num_scalar_pr...  171 us
    pallas_call x2, Pallas kernels, attention_forward(): pl.pallas_call(body, grid_spec=pltpu.PrefetchScalarGridSpec(num_scalar_pr...  103 us
    ppermute x31, waiting for transfers between devices, flip(): return lax.ppermute(values, 'tensor', [(i, i ^ bit) for i in range(size)])  98.8 us
    pallas_call x2, Pallas kernels, tokens_forward(): pl.pallas_call(body, grid_spec=pltpu.PrefetchScalarGridSpec(num_scalar_pr...  53.2 us
    pallas_call x2, Pallas kernels, tokens_backward(): pl.pallas_call(body, grid_spec=pltpu.PrefetchScalarGridSpec(num_scalar_pr...  48.5 us
    all_gather x1, blocking collectives, on_device(): lax.all_gather(jnp.concatenate(ask_params[0:3], axis=1), 'dp', axis=0, ti...  38.4 us
    pallas_call x2, Pallas kernels, weight_grads(): pl.pallas_call(body, grid_spec=pltpu.PrefetchScalarGridSpec(num_scalar_pr...  37.4 us
    pallas_call x6, Pallas kernels, input_grads(): pl.pallas_call(body, grid=(number,), in_specs=[spec] * 3 + [WHOLE], out_s...  31.6 us
  transfers between devices with their start and end apart: 48, of which 10 were waited for; matrix products, arithmetic and copies ran while one was open for 8% of the time, Pallas kernels for 50%

profile of v6, /device:TPU:0, one launch (start us, length us, event | category | flops | bytes accessed | tf_op | source)
XLA Modules:
  0.0 818.3 jit_solution(2144477927082485199)
XLA Ops:
  13.8 2.4 collective-permute-start.10
  22.4 1.8 fusion.2
  25.6 1.8 select_convert_fusion
  31.5 38.4 %all_gather.18.mat = bf16[768,576]{1,0:T(8,128)(2,1)} all-gather(bf16[96,576]{1,0:T(8,128)(2,1)S(1)} %pad_maximum_fusion.5), channel_id=1, replica_groups=mesh['dp'=8,'tensor'=4] {'dp'}, dimensions={0}, use_global_device_ids=true | all-gather | bytes 995328 | tf_op jit(solution)/shard_map/all_gather | solution.py:795
  78.4 10.7 %project.2 = (bf16[4096,384]{1,0:T(8,128)(2,1)}, bf16[4096,384]{1,0:T(8,128)(2,1)}, bf16[4096,384]{1,0:T(8,128)(2,1)}) custom-call(bf16[1024,768]{1,0:T(8,128)(2,1)} %p0.3, bf16[1024,768]{1,0:T(8,128)(2,1)} %collective-permute-done.p1, bf16[1024,768]{1,0:T(8,128)(2,1)} %copy-done.12, bf16[1024,768]{1,0:T(8,128)(2,1)} %copy-done.11, ...), custom_call_target="tpu_custom_call" | custom-call | flops 10871635968 | tf_op jit(solution)/shard_map/project/pallas_call | solution.py:124
  89.0 51.3 %attention_forward.2 = (bf16[4,512,384]{2,1,0:T(8,128)(2,1)}, bf16[4096,384]{1,0:T(8,128)(2,1)}) custom-call(s32[16]{0:T(128)} %squeeze.85.low_ref, s32[16]{0:T(128)} %squeeze.86.high_ref, s32[1]{0:T(128)} %bitcast.place_ref, bf16[4096,384]{1,0:T(8,128)(2,1)} %get-tuple-element.131.q_ref, bf16[4096,384]{1,0:T(8,128)(2,1)} %get-tuple-element.132.k_ref, ...), custom_call_target="tpu_custom_call" | custom-call | flops 77309411328 | tf_op jit(solution)/shard_map/attention_forward/pallas_call | solution.py:217
  140.4 2.5 slice.274.mat
  146.3 9.8 %collective-permute-done.6.c2 = bf16[512,384]{1,0:T(8,128)(2,1)S(1)} collective-permute-done((bf16[512,384]{1,0:T(8,128)(2,1)S(1)}, bf16[512,384]{1,0:T(8,128)(2,1)S(1)}, u32[]{:S(2)}, u32[]{:S(2)}) %collective-permute-start.6) | collective-permute-done | bytes 393248 | tf_op jit(solution)/shard_map/ppermute | solution.py:44
  156.1 6.7 collective-permute-done.7.c3
  163.7 26.4 %tokens_forward.2 = (f32[2,512,768]{2,1,0:T(8,128)}, bf16[2,512,768]{2,1,0:T(8,128)(2,1)}, bf16[2,512,768]{2,1,0:T(8,128)(2,1)}, bf16[2,512,3072]{2,1,0:T(8,128)...) custom-call(s32[1]{0:T(128)} %bitcast.place_ref, ...), custom_call_target="tpu_custom_call" | custom-call | flops 14495514624 | tf_op jit(solution)/shard_map/tokens_forward/pallas_call | solution.py:419
  193.9 18.3 %collective-permute-done.13 = bf16[512,768]{1,0:T(8,128)(2,1)S(1)} collective-permute-done((bf16[512,768]{1,0:T(8,128)(2,1)S(1)}, bf16[512,768]{1,0:T(8,128)(2,1)S(1)}, u32[]{:S(2)}, u32[]{:S(2)}) %collective-permute-start.13) | collective-permute-done | bytes 786464 | tf_op jit(solution)/shard_map/ppermute | solution.py:44
  212.2 16.6 %collective-permute-done.12 = bf16[512,768]{1,0:T(8,128)(2,1)S(1)} collective-permute-done((bf16[512,768]{1,0:T(8,128)(2,1)S(1)}, bf16[512,768]{1,0:T(8,128)(2,1)S(1)}, u32[]{:S(2)}, u32[]{:S(2)}) %collective-permute-start.12) | collective-permute-done | bytes 786464 | tf_op jit(solution)/shard_map/ppermute | solution.py:44
  234.9 2.6 pad_maximum_fusion.1.p3
  237.6 10.9 %project.3 = (bf16[4096,384]{1,0:T(8,128)(2,1)}, bf16[4096,384]{1,0:T(8,128)(2,1)}, bf16[4096,384]{1,0:T(8,128)(2,1)}) custom-call(bf16[1024,768]{1,0:T(8,128)(2,1)} %bitcast.100, bf16[1024,768]{1,0:T(8,128)(2,1)} %collective-permute-done.11.p1, bf16[1024,768]{1,0:T(8,128)(2,1)} %pad_maximum_fusion.p2, bf16[1024,768]{1,0:T(8,128)(2,1)} %pad_maximum_fusion.1.p3, ...), custom_call_target="tpu_custom_call" | custom-call | flops 10871635968 | tf_op jit(solution)/shard_map/project/pallas_call | solution.py:124
  248.6 51.3 %attention_forward.3 = (bf16[4,512,384]{2,1,0:T(8,128)(2,1)}, bf16[4096,384]{1,0:T(8,128)(2,1)}) custom-call(s32[16]{0:T(128)} %squeeze.85.low_ref, s32[16]{0:T(128)} %squeeze.86.high_ref, s32[1]{0:T(128)} %bitcast.place_ref, bf16[4096,384]{1,0:T(8,128)(2,1)} %get-tuple-element.143.q_ref, bf16[4096,384]{1,0:T(8,128)(2,1)} %get-tuple-element.144.k_ref, ...), custom_call_target="tpu_custom_call" | custom-call | flops 77309411328 | tf_op jit(solution)/shard_map/attention_forward/pallas_call | solution.py:217
  299.9 2.3 slice_bitcast_fusion.2
  304.9 24.6 %all-gather.10.cloned.1.call-done = bf16[3072,1792]{1,0:T(8,128)(2,1)} async-done(((bf16[96,1792]{1,0:T(8,128)(2,1)}), bf16[3072,1792]{1,0:T(8,128)(2,1)}) %all-gather.10.cloned.1.call-update) | async-done | bytes 11010064 | tf_op jit(solution)/shard_map/all_gather | solution.py:649
  333.4 26.9 %tokens_forward.3 = (f32[2,512,768]{2,1,0:T(8,128)}, bf16[2,512,768]{2,1,0:T(8,128)(2,1)}, bf16[2,512,768]{2,1,0:T(8,128)(2,1)}, bf16[2,512,3072]{2,1,0:T(8,128)...) custom-call(s32[1]{0:T(128)} %bitcast.place_ref, ...), custom_call_target="tpu_custom_call" | custom-call | flops 14495514624 | tf_op jit(solution)/shard_map/tokens_forward/pallas_call | solution.py:419
  360.3 4.0 fusion.1
  364.3 24.3 %tokens_backward.2 = (bf16[2,512,768]{2,1,0:T(8,128)(2,1)}, bf16[2,512,3072]{2,1,0:T(8,128)(2,1)}, f32[2,512,768]{2,1,0:T(8,128)}, bf16[2,512,768]{2,1,0:T(8,128...) custom-call(s32[1]{0:T(128)} %bitcast.place_ref, ...), custom_call_target="tpu_custom_call" | custom-call | flops 14495514624 | tf_op jit(solution)/shard_map/tokens_backward/pallas_call | solution.py:524
  390.5 18.7 %weight_grads.2 = bf16[4,768,1728]{2,1,0:T(8,128)(2,1)} custom-call(s32[1]{0:T(128)} %bitcast.place_ref, bf16[1024,768]{1,0:T(8,128)(2,1)} %bitcast.137, bf16[1024,3072]{1,0:T(8,128)(2,1)} %bitcast.132, bf16[1024,768]{1,0:T(8,128)(2,1)} %bitcast.138, bf16[1024,3072]{1,0:T(8,128)(2,1)} %bitcast.131, bf16[1024,768]{1,0:T(8,128)(2,1)} %bitcast.139, ...), custom_call_target="tpu_custom_call" | custom-call | flops 14495514624 | tf_op jit(solution)/shard_map/weight_grads/pallas_call | solution.py:573
  410.2 85.3 %attention_backward.2 = (bf16[4096,192]{1,0:T(8,128)(2,1)}, bf16[4096,192]{1,0:T(8,128)(2,1)}, bf16[4096,192]{1,0:T(8,128)(2,1)}) custom-call(s32[16]{0:T(128)} %squeeze.85.low_ref, s32[16]{0:T(128)} %squeeze.86.high_ref, s32[1]{0:T(128)} %bitcast.place_ref, bf16[4096,384]{1,0:T(8,128)(2,1)} %get-tuple-element.157.q_ref, ...), custom_call_target="tpu_custom_call" | custom-call | flops 154618822656 | tf_op jit(solution)/shard_map/attention_backward/pallas_call | solution.py:339
  495.5 4.3 input_grads.7
  500.5 4.4 input_grads.6
  504.9 3.0 add_convert_fusion.1
  508.3 7.2 input_grads.8
  515.6 11.2 %projection_grads.2 = (bf16[768,576]{1,0:T(8,128)(2,1)}, f32[8,192]{1,0:T(8,128)}) custom-call(bf16[1024,768]{1,0:T(8,128)(2,1)} %bitcast.101, bf16[1024,768]{1,0:T(8,128)(2,1)} %collective-permute-done.11.p1, bf16[1024,768]{1,0:T(8,128)(2,1)} %pad_maximum_fusion.p2, bf16[1024,768]{1,0:T(8,128)(2,1)} %pad_maximum_fusion.1.p3, ...), custom_call_target="tpu_custom_call" | custom-call | flops 10871635968 | tf_op jit(solution)/shard_map/projection_grads/pallas_call | solution.py:630
  527.6 2.4 pad_maximum_fusion.2
  530.0 24.3 %collective-permute-done.24 = bf16[1024,768]{1,0:T(8,128)(2,1)} collective-permute-done((bf16[1024,768]{1,0:T(8,128)(2,1)}, bf16[1024,768]{1,0:T(8,128)(2,1)}, u32[]{:S(2)}, u32[]{:S(2)}) %collective-permute-start.24) | collective-permute-done | bytes 1572896 | tf_op jit(solution)/shard_map/ppermute | solution.py:44
  554.3 4.5 bitcast_add_fusion.1
  558.8 16.4 %reduce-scatter.3.cloned.1.call-done = bf16[96,1728]{1,0:T(8,128)(2,1)} async-done(((bf16[3072,1728]{1,0:T(8,128)(2,1)}), bf16[96,1728]{1,0:T(8,128)(2,1)}) %reduce-scatter.3.cloned.1.call-update) | async-done | bytes 331792 | tf_op jit(solution)/shard_map/reduce_scatter | solution.py:711
  575.2 1.9 convert_element_type.159
  577.1 4.4 all-to-all-start
  581.6 24.3 %tokens_backward.3 = (bf16[2,512,768]{2,1,0:T(8,128)(2,1)}, bf16[2,512,3072]{2,1,0:T(8,128)(2,1)}, f32[2,512,768]{2,1,0:T(8,128)}, bf16[2,512,768]{2,1,0:T(8,128...) custom-call(s32[1]{0:T(128)} %bitcast.place_ref, ...), custom_call_target="tpu_custom_call" | custom-call | flops 14495514624 | tf_op jit(solution)/shard_map/tokens_backward/pallas_call | solution.py:524
  610.4 18.7 %weight_grads.3 = bf16[4,768,1728]{2,1,0:T(8,128)(2,1)} custom-call(s32[1]{0:T(128)} %bitcast.place_ref, bf16[1024,768]{1,0:T(8,128)(2,1)} %bitcast.134, bf16[1024,3072]{1,0:T(8,128)(2,1)} %bitcast.130, bf16[1024,768]{1,0:T(8,128)(2,1)} %bitcast.135, bf16[1024,3072]{1,0:T(8,128)(2,1)} %bitcast.129, bf16[1024,768]{1,0:T(8,128)(2,1)} %bitcast.136, ...), custom_call_target="tpu_custom_call" | custom-call | flops 14495514624 | tf_op jit(solution)/shard_map/weight_grads/pallas_call | solution.py:573
  631.1 4.7 collective-permute-start.37
  636.9 1.9 collective-permute-start.34
  638.8 2.3 collective-permute-start.33
  641.1 7.2 collective-permute-start.32
  649.8 85.6 %attention_backward.3 = (bf16[4096,192]{1,0:T(8,128)(2,1)}, bf16[4096,192]{1,0:T(8,128)(2,1)}, bf16[4096,192]{1,0:T(8,128)(2,1)}) custom-call(s32[16]{0:T(128)} %squeeze.85.low_ref, s32[16]{0:T(128)} %squeeze.86.high_ref, s32[1]{0:T(128)} %bitcast.place_ref, bf16[4096,384]{1,0:T(8,128)(2,1)} %get-tuple-element.149.q_ref, ...), custom_call_target="tpu_custom_call" | custom-call | flops 154618822656 | tf_op jit(solution)/shard_map/attention_backward/pallas_call | solution.py:339
  736.8 4.4 input_grads.10
  742.0 4.6 input_grads.9
  746.6 3.0 add_convert_fusion
  749.7 11.1 %projection_grads.3 = (bf16[768,576]{1,0:T(8,128)(2,1)}, f32[8,192]{1,0:T(8,128)}) custom-call(bf16[1024,768]{1,0:T(8,128)(2,1)} %p0.3, bf16[1024,768]{1,0:T(8,128)(2,1)} %collective-permute-done.p1, bf16[1024,768]{1,0:T(8,128)(2,1)} %copy-done.12, bf16[1024,768]{1,0:T(8,128)(2,1)} %copy-done.11, bf16[4096,192]{1,0:T(8,128)(2,1)} %get-tuple-element.214.q_ref, ...), custom_call_target="tpu_custom_call" | custom-call | flops 10871635968 | tf_op jit(solution)/shard_map/projection_grads/pallas_call | solution.py:630
  762.2 6.8 input_grads.11
  770.8 4.2 all-to-all-start.1
  779.2 21.8 %collective-permute-done.40 = bf16[1024,768]{1,0:T(8,128)(2,1)} collective-permute-done((bf16[1024,768]{1,0:T(8,128)(2,1)}, bf16[1024,768]{1,0:T(8,128)(2,1)}, u32[]{:S(2)}, u32[]{:S(2)}) %collective-permute-start.40) | collective-permute-done | bytes 1572896 | tf_op jit(solution)/shard_map/ppermute | solution.py:44
  801.0 5.2 bitcast_add_fusion
  (301 shorter events, 71.3 us)
Async XLA Ops:
  7.2 133.1 %all-gather.6.cloned.1.call-start = ((), (), s32[]{:S(2)}) async-start(), calls=%async_computation.4 | async-start | bytes 1327104 | tf_op jit(solution)/shard_map/all_gather | solution.py:802
  9.0 153.9 %all-gather.8.cloned.1.call-start = ((), (), s32[]{:S(2)}) async-start(), calls=%async_computation.7 | async-start | bytes 11354112 | tf_op jit(solution)/shard_map/all_gather | solution.py:649
  11.7 317.7 %all-gather.10.cloned.1.call-start = ((), (), s32[]{:S(2)}) async-start(), calls=%async_computation.8 | async-start | bytes 11354112 | tf_op jit(solution)/shard_map/all_gather | solution.py:649
  13.8 60.7 %collective-permute-start.10 = (f32[2,768]{1,0:T(2,128)}, f32[2,768]{1,0:T(2,128)}, u32[]{:S(2)}, u32[]{:S(2)}) collective-permute-start(f32[2,768]{1,0:T(2,128)} %get-tuple-element.347), channel_id=1, source_target_pairs={{0,3},{1,2},{2,1},{3,0},{4,7},{5,6},{6,5},{7,4},{8,11},{9,10},{10,... | collective-permute-start | bytes 18440 | tf_op jit(solution)/shard_map/ppermute | solution.py:44
  16.2 54.3 %collective-permute-start.9 = (f32[2,768]{1,0:T(2,128)}, f32[2,768]{1,0:T(2,128)}, u32[]{:S(2)}, u32[]{:S(2)}) collective-permute-start(f32[2,768]{1,0:T(2,128)} %get-tuple-element.347), channel_id=1, source_target_pairs={{0,2},{1,3},{2,0},{3,1},{4,6},{5,7},{6,4},{7,5},{8,10},{9,11},{10,... | collective-permute-start | bytes 18440 | tf_op jit(solution)/shard_map/ppermute | solution.py:44
  16.8 60.4 %collective-permute-start = (bf16[1024,768]{1,0:T(8,128)(2,1)}, bf16[1024,768]{1,0:T(8,128)(2,1)}, u32[]{:S(2)}, u32[]{:S(2)}) collective-permute-start(bf16[1024,768]{1,0:T(8,128)(2,1)} %p0.3), channel_id=1, source_target_pairs={{0,1},{1,0},{2,3},{3,2},{4,5},{5,4},{6,7},{7,6},{8,9},{9,8},{10,11... | collective-permute-start | bytes 4718600 | tf_op jit(solution)/shard_map/ppermute | solution.py:44
  17.9 52.0 %collective-permute-start.1 = (bf16[512,768]{1,0:T(8,128)(2,1)S(1)}, bf16[512,768]{1,0:T(8,128)(2,1)S(1)}, u32[]{:S(2)}, u32[]{:S(2)}) collective-permute-start(bf16[512,768]{1,0:T(8,128)(2,1)S(1)} %get-tuple-element.321), channel_id=1, source_target_pairs={{0,2},{1,3},{2,0},{3,1},{4,6},{5,7},{6,4},{7,5},{8,10},{9,11},{10,... | collective-permute-start | bytes 2359304 | tf_op jit(solution)/shard_map/ppermute | solution.py:44
  19.6 50.3 %collective-permute-start.2 = (bf16[512,768]{1,0:T(8,128)(2,1)}, bf16[512,768]{1,0:T(8,128)(2,1)S(1)}, u32[]{:S(2)}, u32[]{:S(2)}) collective-permute-start(bf16[512,768]{1,0:T(8,128)(2,1)} %get-tuple-element.320), channel_id=1, source_target_pairs={{0,2},{1,3},{2,0},{3,1},{4,6},{5,7},{6,4},{7,5},{8,10},{9,11},{10,... | collective-permute-start | bytes 2359304 | tf_op jit(solution)/shard_map/ppermute | solution.py:44
  69.9 5.5 collective-permute-start.3
  69.9 5.5 collective-permute-start.4
  70.5 4.0 collective-permute-start.8
  143.8 2.5 collective-permute-start.5
  144.2 12.0 %collective-permute-start.6 = (bf16[512,384]{1,0:T(8,128)(2,1)S(1)}, bf16[512,384]{1,0:T(8,128)(2,1)S(1)}, u32[]{:S(2)}, u32[]{:S(2)}) collective-permute-start(bf16[512,384]{1,0:T(8,128)(2,1)S(1)} %get-tuple-element.317), channel_id=1, source_target_pairs={{0,2},{1,3},{2,0},{3,1},{4,6},{5,7},{6,4},{7,5},{8,10},{9,11},{10,... | collective-permute-start | bytes 1179656 | tf_op jit(solution)/shard_map/ppermute | solution.py:44
  145.1 17.7 %collective-permute-start.7 = (bf16[512,384]{1,0:T(8,128)(2,1)S(1)}, bf16[512,384]{1,0:T(8,128)(2,1)S(1)}, u32[]{:S(2)}, u32[]{:S(2)}) collective-permute-start(bf16[512,384]{1,0:T(8,128)(2,1)S(1)} %get-tuple-element.316), channel_id=1, source_target_pairs={{0,3},{1,2},{2,1},{3,0},{4,7},{5,6},{6,5},{7,4},{8,11},{9,10},{10,... | collective-permute-start | bytes 1179656 | tf_op jit(solution)/shard_map/ppermute | solution.py:44
  191.7 20.5 %collective-permute-start.13 = (bf16[512,768]{1,0:T(8,128)(2,1)S(1)}, bf16[512,768]{1,0:T(8,128)(2,1)S(1)}, u32[]{:S(2)}, u32[]{:S(2)}) collective-permute-start(bf16[512,768]{1,0:T(8,128)(2,1)S(1)} %get-tuple-element.315), channel_id=1, source_target_pairs={{0,2},{1,3},{2,0},{3,1},{4,6},{5,7},{6,4},{7,5},{8,10},{9,11},{10,... | collective-permute-start | bytes 2359304 | tf_op jit(solution)/shard_map/ppermute | solution.py:44
  192.5 36.2 %collective-permute-start.12 = (bf16[512,768]{1,0:T(8,128)(2,1)S(1)}, bf16[512,768]{1,0:T(8,128)(2,1)S(1)}, u32[]{:S(2)}, u32[]{:S(2)}) collective-permute-start(bf16[512,768]{1,0:T(8,128)(2,1)S(1)} %get-tuple-element.314), channel_id=1, source_target_pairs={{0,2},{1,3},{2,0},{3,1},{4,6},{5,7},{6,4},{7,5},{8,10},{9,11},{10,... | collective-permute-start | bytes 2359304 | tf_op jit(solution)/shard_map/ppermute | solution.py:44
  193.8 43.8 %collective-permute-start.11 = (bf16[1024,768]{1,0:T(8,128)(2,1)S(1)}, bf16[1024,768]{1,0:T(8,128)(2,1)}, u32[]{:S(2)}, u32[]{:S(2)}) collective-permute-start(bf16[1024,768]{1,0:T(8,128)(2,1)S(1)} %bitcast.102), channel_id=1, source_target_pairs={{0,1},{1,0},{2,3},{3,2},{4,5},{5,4},{6,7},{7,6},{8,9},{9,8},{10,11... | collective-permute-start | bytes 4718600 | tf_op jit(solution)/shard_map/ppermute | solution.py:44
  212.2 22.8 %collective-permute-start.15 = (bf16[512,768]{1,0:T(8,128)(2,1)S(1)}, bf16[512,768]{1,0:T(8,128)(2,1)}, u32[]{:S(2)}, u32[]{:S(2)}) collective-permute-start(bf16[512,768]{1,0:T(8,128)(2,1)S(1)} %collective-permute-done.13), channel_id=1, source_target_pairs={{0,1},{1,0},{2,3},{3,2},{4,5},{5,4},{6,7},{7,6},{8,9},{9,8},{10,11... | collective-permute-start | bytes 2359304 | tf_op jit(solution)/shard_map/ppermute | solution.py:44
  228.7 6.2 collective-permute-start.14
  237.6 337.6 %reduce-scatter.3.cloned.1.call-start = ((), (), s32[]{:S(2)}) async-start(), calls=%async_computation.5 | async-start | bytes 11354112 | tf_op jit(solution)/shard_map/reduce_scatter | solution.py:711
  302.2 30.2 %collective-permute-start.16 = (bf16[512,384]{1,0:T(8,128)(2,1)S(1)}, bf16[512,384]{1,0:T(8,128)(2,1)S(1)}, u32[]{:S(2)}, u32[]{:S(2)}) collective-permute-start(bf16[512,384]{1,0:T(8,128)(2,1)S(1)} %get-tuple-element.312), channel_id=1, source_target_pairs={{0,1},{1,0},{2,3},{3,2},{4,5},{5,4},{6,7},{7,6},{8,9},{9,8},{10,11... | collective-permute-start | bytes 1179656 | tf_op jit(solution)/shard_map/ppermute | solution.py:44
  302.7 29.7 %collective-permute-start.17 = (bf16[512,384]{1,0:T(8,128)(2,1)S(1)}, bf16[512,384]{1,0:T(8,128)(2,1)S(1)}, u32[]{:S(2)}, u32[]{:S(2)}) collective-permute-start(bf16[512,384]{1,0:T(8,128)(2,1)S(1)} %get-tuple-element.311), channel_id=1, source_target_pairs={{0,2},{1,3},{2,0},{3,1},{4,6},{5,7},{6,4},{7,5},{8,10},{9,11},{10,... | collective-permute-start | bytes 1179656 | tf_op jit(solution)/shard_map/ppermute | solution.py:44
  303.6 28.9 %collective-permute-start.18 = (bf16[512,384]{1,0:T(8,128)(2,1)S(1)}, bf16[512,384]{1,0:T(8,128)(2,1)S(1)}, u32[]{:S(2)}, u32[]{:S(2)}) collective-permute-start(bf16[512,384]{1,0:T(8,128)(2,1)S(1)} %get-tuple-element.310), channel_id=1, source_target_pairs={{0,3},{1,2},{2,1},{3,0},{4,7},{5,6},{6,5},{7,4},{8,11},{9,10},{10,... | collective-permute-start | bytes 1179656 | tf_op jit(solution)/shard_map/ppermute | solution.py:44
  388.6 20.6 %collective-permute-start.19 = (bf16[512,384]{1,0:T(8,128)(2,1)}, bf16[512,384]{1,0:T(8,128)(2,1)S(1)}, u32[]{:S(2)}, u32[]{:S(2)}) collective-permute-start(bf16[512,384]{1,0:T(8,128)(2,1)} %get-tuple-element.159), channel_id=1, source_target_pairs={{0,1},{1,0},{2,3},{3,2},{4,5},{5,4},{6,7},{7,6},{8,9},{9,8},{10,11... | collective-permute-start | bytes 1179656 | tf_op jit(solution)/shard_map/ppermute | solution.py:44
  388.9 20.3 %collective-permute-start.20 = (bf16[512,384]{1,0:T(8,128)(2,1)}, bf16[512,384]{1,0:T(8,128)(2,1)S(1)}, u32[]{:S(2)}, u32[]{:S(2)}) collective-permute-start(bf16[512,384]{1,0:T(8,128)(2,1)} %get-tuple-element.160), channel_id=1, source_target_pairs={{0,2},{1,3},{2,0},{3,1},{4,6},{5,7},{6,4},{7,5},{8,10},{9,11},{10,... | collective-permute-start | bytes 1179656 | tf_op jit(solution)/shard_map/ppermute | solution.py:44
  388.9 20.3 %collective-permute-start.21 = (bf16[512,384]{1,0:T(8,128)(2,1)}, bf16[512,384]{1,0:T(8,128)(2,1)S(1)}, u32[]{:S(2)}, u32[]{:S(2)}) collective-permute-start(bf16[512,384]{1,0:T(8,128)(2,1)} %get-tuple-element.161), channel_id=1, source_target_pairs={{0,3},{1,2},{2,1},{3,0},{4,7},{5,6},{6,5},{7,4},{8,11},{9,10},{10,... | collective-permute-start | bytes 1179656 | tf_op jit(solution)/shard_map/ppermute | solution.py:44
  499.9 5.0 collective-permute-start.22
  507.8 46.5 %collective-permute-start.24 = (bf16[1024,768]{1,0:T(8,128)(2,1)}, bf16[1024,768]{1,0:T(8,128)(2,1)}, u32[]{:S(2)}, u32[]{:S(2)}) collective-permute-start(bf16[1024,768]{1,0:T(8,128)(2,1)} %add_convert_fusion.1), channel_id=1, source_target_pairs={{0,2},{1,3},{2,0},{3,1},{4,6},{5,7},{6,4},{7,5},{8,10},{9,11},{10,... | collective-permute-start | bytes 4718600 | tf_op jit(solution)/shard_map/ppermute | solution.py:44
  515.5 38.9 %collective-permute-start.23 = (bf16[1024,768]{1,0:T(8,128)(2,1)}, bf16[1024,768]{1,0:T(8,128)(2,1)}, u32[]{:S(2)}, u32[]{:S(2)}) collective-permute-start(bf16[1024,768]{1,0:T(8,128)(2,1)} %get-tuple-element.178), channel_id=1, source_target_pairs={{0,1},{1,0},{2,3},{3,2},{4,5},{5,4},{6,7},{7,6},{8,9},{9,8},{10,11... | collective-permute-start | bytes 4718600 | tf_op jit(solution)/shard_map/ppermute | solution.py:44
  577.1 53.2 %all-to-all-start = ((bf16[8,112,576]{2,1,0:T(8,128)(2,1)}), bf16[8,112,576]{2,1,0:T(8,128)(2,1)S(1)}, u32[]{:S(2)}, u32[]{:S(2)}) async-start(bf16[8,112,576]{2,1,0:T(8,128)(2,1)} %pad_maximum_fusion.2), calls=%async_computation.1 | async-start | bytes 2293760 | tf_op jit(solution)/shard_map/all_to_all | solution.py:705
  581.5 224.7 %reduce-scatter.5.cloned.1.call-start = ((), (), s32[]{:S(2)}) async-start(), calls=%async_computation.6 | async-start | bytes 11354112 | tf_op jit(solution)/shard_map/reduce_scatter | solution.py:711
  606.7 2.8 collective-permute-start.28
  606.7 22.4 %collective-permute-start.29 = (f32[32,768]{1,0:T(8,128)S(1)}, f32[32,768]{1,0:T(8,128)S(1)}, u32[]{:S(2)}, u32[]{:S(2)}) collective-permute-start(f32[32,768]{1,0:T(8,128)S(1)} %constant_dynamic-update-slice_fusion.4), channel_id=1, source_target_pairs={{0,2},{1,3},{2,0},{3,1},{4,6},{5,7},{6,4},{7,5},{8,10},{9,11},{10,... | collective-permute-start | bytes 294920 | tf_op jit(solution)/shard_map/ppermute | solution.py:66
  607.4 21.7 %collective-permute-start.30 = (f32[32,768]{1,0:T(8,128)S(1)}, f32[32,768]{1,0:T(8,128)S(1)}, u32[]{:S(2)}, u32[]{:S(2)}) collective-permute-start(f32[32,768]{1,0:T(8,128)S(1)} %constant_dynamic-update-slice_fusion.4), channel_id=1, source_target_pairs={{0,3},{1,2},{2,1},{3,0},{4,7},{5,6},{6,5},{7,4},{8,11},{9,10},{10,... | collective-permute-start | bytes 294920 | tf_op jit(solution)/shard_map/ppermute | solution.py:66
  608.5 20.5 %collective-permute-start.25 = (bf16[512,384]{1,0:T(8,128)(2,1)}, bf16[512,384]{1,0:T(8,128)(2,1)S(1)}, u32[]{:S(2)}, u32[]{:S(2)}) collective-permute-start(bf16[512,384]{1,0:T(8,128)(2,1)} %get-tuple-element.190), channel_id=1, source_target_pairs={{0,1},{1,0},{2,3},{3,2},{4,5},{5,4},{6,7},{7,6},{8,9},{9,8},{10,11... | collective-permute-start | bytes 1179656 | tf_op jit(solution)/shard_map/ppermute | solution.py:44
  608.8 20.3 %collective-permute-start.26 = (bf16[512,384]{1,0:T(8,128)(2,1)}, bf16[512,384]{1,0:T(8,128)(2,1)S(1)}, u32[]{:S(2)}, u32[]{:S(2)}) collective-permute-start(bf16[512,384]{1,0:T(8,128)(2,1)} %get-tuple-element.191), channel_id=1, source_target_pairs={{0,2},{1,3},{2,0},{3,1},{4,6},{5,7},{6,4},{7,5},{8,10},{9,11},{10,... | collective-permute-start | bytes 1179656 | tf_op jit(solution)/shard_map/ppermute | solution.py:44
  609.5 20.9 %collective-permute-start.27 = (bf16[512,384]{1,0:T(8,128)(2,1)}, bf16[512,384]{1,0:T(8,128)(2,1)S(1)}, u32[]{:S(2)}, u32[]{:S(2)}) collective-permute-start(bf16[512,384]{1,0:T(8,128)(2,1)} %get-tuple-element.192), channel_id=1, source_target_pairs={{0,3},{1,2},{2,1},{3,0},{4,7},{5,6},{6,5},{7,4},{8,11},{9,10},{10,... | collective-permute-start | bytes 1179656 | tf_op jit(solution)/shard_map/ppermute | solution.py:44
  631.1 10.0 %collective-permute-start.37 = (f32[32,768]{1,0:T(8,128)}, f32[32,768]{1,0:T(8,128)S(1)}, u32[]{:S(2)}, u32[]{:S(2)}) collective-permute-start(f32[32,768]{1,0:T(8,128)} %add_add_fusion.1), channel_id=1, source_target_pairs={{0,28},{4,24},{8,20},{12,16},{16,12},{20,8},{24,4},{28,0},{1,29},{... | collective-permute-start | bytes 294920 | tf_op jit(solution)/shard_map/ppermute | solution.py:66
  635.8 12.5 %collective-permute-start.36 = (f32[32,768]{1,0:T(8,128)}, f32[32,768]{1,0:T(8,128)S(1)}, u32[]{:S(2)}, u32[]{:S(2)}) collective-permute-start(f32[32,768]{1,0:T(8,128)} %add_add_fusion.1), channel_id=1, source_target_pairs={{0,24},{4,28},{8,16},{12,20},{16,8},{20,12},{24,0},{28,4},{1,25},{... | collective-permute-start | bytes 294920 | tf_op jit(solution)/shard_map/ppermute | solution.py:66
  636.3 99.1 %collective-permute-start.35 = (f32[32,768]{1,0:T(8,128)}, f32[32,768]{1,0:T(8,128)}, u32[]{:S(2)}, u32[]{:S(2)}) collective-permute-start(f32[32,768]{1,0:T(8,128)} %add_add_fusion.1), channel_id=1, source_target_pairs={{0,20},{4,16},{8,28},{12,24},{16,4},{20,0},{24,12},{28,8},{1,21},{... | collective-permute-start | bytes 294920 | tf_op jit(solution)/shard_map/ppermute | solution.py:66
  636.9 98.6 %collective-permute-start.34 = (f32[32,768]{1,0:T(8,128)}, f32[32,768]{1,0:T(8,128)}, u32[]{:S(2)}, u32[]{:S(2)}) collective-permute-start(f32[32,768]{1,0:T(8,128)} %add_add_fusion.1), channel_id=1, source_target_pairs={{0,16},{4,20},{8,24},{12,28},{16,0},{20,4},{24,8},{28,12},{1,17},{... | collective-permute-start | bytes 294920 | tf_op jit(solution)/shard_map/ppermute | solution.py:66
  638.8 96.7 %collective-permute-start.33 = (f32[32,768]{1,0:T(8,128)}, f32[32,768]{1,0:T(8,128)}, u32[]{:S(2)}, u32[]{:S(2)}) collective-permute-start(f32[32,768]{1,0:T(8,128)} %add_add_fusion.1), channel_id=1, source_target_pairs={{0,12},{4,8},{8,4},{12,0},{16,28},{20,24},{24,20},{28,16},{1,13},{... | collective-permute-start | bytes 294920 | tf_op jit(solution)/shard_map/ppermute | solution.py:66
  641.1 94.4 %collective-permute-start.32 = (f32[32,768]{1,0:T(8,128)}, f32[32,768]{1,0:T(8,128)}, u32[]{:S(2)}, u32[]{:S(2)}) collective-permute-start(f32[32,768]{1,0:T(8,128)} %add_add_fusion.1), channel_id=1, source_target_pairs={{0,8},{4,12},{8,0},{12,4},{16,24},{20,28},{24,16},{28,20},{1,9},{5... | collective-permute-start | bytes 294920 | tf_op jit(solution)/shard_map/ppermute | solution.py:66
  648.3 87.2 %collective-permute-start.31 = (f32[32,768]{1,0:T(8,128)}, f32[32,768]{1,0:T(8,128)}, u32[]{:S(2)}, u32[]{:S(2)}) collective-permute-start(f32[32,768]{1,0:T(8,128)} %add_add_fusion.1), channel_id=1, source_target_pairs={{0,4},{4,0},{8,12},{12,8},{16,20},{20,16},{24,28},{28,24},{1,5},{5... | collective-permute-start | bytes 294920 | tf_op jit(solution)/shard_map/ppermute | solution.py:66
  741.2 5.4 collective-permute-start.38
  761.5 39.5 %collective-permute-start.40 = (bf16[1024,768]{1,0:T(8,128)(2,1)}, bf16[1024,768]{1,0:T(8,128)(2,1)}, u32[]{:S(2)}, u32[]{:S(2)}) collective-permute-start(bf16[1024,768]{1,0:T(8,128)(2,1)} %add_convert_fusion), channel_id=1, source_target_pairs={{0,2},{1,3},{2,0},{3,1},{4,6},{5,7},{6,4},{7,5},{8,10},{9,11},{10,... | collective-permute-start | bytes 4718600 | tf_op jit(solution)/shard_map/ppermute | solution.py:44
  769.0 32.1 %collective-permute-start.39 = (bf16[1024,768]{1,0:T(8,128)(2,1)}, bf16[1024,768]{1,0:T(8,128)(2,1)}, u32[]{:S(2)}, u32[]{:S(2)}) collective-permute-start(bf16[1024,768]{1,0:T(8,128)(2,1)} %get-tuple-element.221), channel_id=1, source_target_pairs={{0,1},{1,0},{2,3},{3,2},{4,5},{5,4},{6,7},{7,6},{8,9},{9,8},{10,11... | collective-permute-start | bytes 4718600 | tf_op jit(solution)/shard_map/ppermute | solution.py:44
  770.8 37.5 %all-to-all-start.1 = ((bf16[8,112,576]{2,1,0:T(8,128)(2,1)}), bf16[8,112,576]{2,1,0:T(8,128)(2,1)S(1)}, u32[]{:S(2)}, u32[]{:S(2)}) async-start(bf16[8,112,576]{2,1,0:T(8,128)(2,1)} %pad_maximum_fusion.3), calls=%async_computation.2 | async-start | bytes 2293760 | tf_op jit(solution)/shard_map/all_to_all | solution.py:732
  (53 other events, 977.4 us)
Sparse Core Ops, SparseCore 0:
  10.8 52.6 all-gather.5
  66.5 88.3 all-gather.7
  237.7 91.6 all-gather.9
  409.4 165.7 reduce-scatter.2
  641.2 150.2 reduce-scatter.4
